TPU v7x, 128 devices: a whole 4x4x4 slice. The times are simulated.
128 devices in a mesh: dir: 32 (over y, z, core), near: 4 (over x).
Axes of the slice: x: 4, y: 4, z: 4, core: 2. Of those that a mesh axis runs over, the one named last changes fastest.
Arguments:
- currents: bfloat16 [4096, 128, 128], P(('dir', 'near')), may hold values from -6 to 6
- counts: int32 [128], replicated, may hold values from 0 to 4, as said below
- near_source: int32 [4096, 6], P(('dir', 'near')), may hold values from 0 to 4095, as said below
- near_blocks: bfloat16 [4096, 6, 128, 256], P(('dir', 'near')), may hold values from -0.15625 to 0.15625
- aggregate: bfloat16 [8, 1152, 256], replicated, may hold values from -0.125 to 0.125
- receive: bfloat16 [8, 128, 2304], replicated, may hold values from -0.125 to 0.125
- translations: bfloat16 [4, 3, 1152, 64, 128], P(None, None, ('dir', 'near')), may hold values from -0.3125 to 0.3125
- source_blocks: int32 [4, 3], replicated, may hold values from 0 to 3, as said below
Outputs:
- fields: bfloat16 [4096, 128, 128], P(('dir', 'near'))
Inputs may be any that keep to these rules, and one draw needn't show every extreme that they name: `counts`: devices 2 m and 2 m + 1 of dir and near together (neighbours along near) own exactly 4 parents between them; some device owns 4 and its neighbour none. `near_source`: every entry names a live leaf slot on the device of its row or on a device next to it along near with the same dir index. `source_blocks`: each row names 3 different blocks.
All inputs are finite; a program needn't handle non-finite values.
Results may differ from a plain program's by a relative error of at most 0.005.
Values may be sent and summed in bfloat16 or wider, within the bound.
No kernel may reach another device: no remote copies, remote signals or barrier semaphores. Data moves between devices by JAX's collectives and lax.ppermute only.
A program may use at most 128 MiB of HBM per device.

v0:
```python
import jax
import jax.numpy as jnp
from jax import lax
from jax.sharding import PartitionSpec as P


def padded(cells, sides, width):
    for axis, dim in sides:
        count = lax.axis_size(axis)
        ends = count - 1
        head = lax.slice_in_dim(cells, 0, width, axis=dim)
        tail = lax.slice_in_dim(cells, cells.shape[dim] - width, cells.shape[dim], axis=dim)
        cells = jnp.concatenate(
            [
                lax.ppermute(tail, axis, [(i, (i + 1) % count) for i in range(ends)]),
                cells,
                lax.ppermute(head, axis, [((i + 1) % count, i) for i in range(ends)]),
            ],
            axis=dim,
        )
    return cells


def turned(values):
    middle = values.shape[-1] // 2
    return jnp.concatenate([-values[..., middle:], values[..., :middle]], axis=-1)


def regroup(patterns, slot_count):
    groups = lax.axis_size(("dir", "near"))
    channels = patterns.shape[-1]
    per_group = patterns.shape[1] // groups
    shaped = patterns.reshape(1, slot_count, groups, per_group, channels)
    exchanged = lax.all_to_all(shaped, ("dir", "near"), split_axis=2, concat_axis=0, tiled=True)
    return exchanged.reshape(groups * slot_count, per_group, channels)


def collect(fields, slot_count):
    groups = lax.axis_size(("dir", "near"))
    channels = fields.shape[-1]
    per_group = fields.shape[1]
    shaped = fields.reshape(groups, slot_count, 1, per_group, channels)
    exchanged = lax.all_to_all(shaped, ("dir", "near"), split_axis=0, concat_axis=2, tiled=True)
    return exchanged.reshape(slot_count, groups * per_group, channels)


def translate(ordered, translations, source_blocks):
    block_count, list_length, per_group, block_size, doubled_size = translations.shape
    channels = ordered.shape[-1]
    blocks = ordered.reshape(block_count, block_size, per_group, channels)
    with_turned = jnp.concatenate([blocks, turned(blocks)], axis=1)
    sources = with_turned[source_blocks]
    summed = jnp.einsum(
        "tlkij,tljkr->tikr", translations, sources, preferred_element_type=jnp.float32
    )
    return summed.astype(jnp.bfloat16).reshape(block_count * block_size, per_group, channels)


def body(
    currents, counts, near_source, near_blocks, aggregate, receive, translations, source_blocks
):
    device_index = lax.axis_index(("dir", "near"))
    leaf_slots, unknowns, channels = currents.shape
    parent_slots = leaf_slots // 8
    parents = translations.shape[0] * translations.shape[3]
    starts = jnp.cumsum(counts) - counts
    own_count = counts[device_index]
    children = currents.reshape(parent_slots, 8, unknowns, channels)
    work_slots = children.shape[0]
    stacked = jnp.concatenate([children, turned(children)], axis=2)
    patterns = jnp.einsum(
        "ckq,scqr->skr", aggregate, stacked, preferred_element_type=jnp.float32
    ).astype(jnp.bfloat16)
    gathered = regroup(patterns, work_slots)
    parent_ids = jnp.arange(parents, dtype=jnp.int32)
    range_ends = jnp.cumsum(counts)
    before = (range_ends[None, :] <= parent_ids[:, None]).astype(jnp.int32)
    owners = jnp.sum(before, axis=1)
    local_slot = parent_ids - jnp.sum(before * counts[None, :], axis=1)
    slot_ids = jnp.arange(work_slots, dtype=jnp.int32)[None, :]
    position = owners * parent_slots + local_slot
    anchor = starts[:, None] + slot_ids
    incoming = translate(gathered[position], translations, source_blocks)
    anchor = jnp.clip(anchor, 0, parents - 1).reshape(-1)
    returned = collect(incoming[anchor], work_slots)
    doubled = jnp.concatenate([returned, turned(returned)], axis=1)
    far_field = jnp.einsum("cpk,skr->scpr", receive, doubled, preferred_element_type=jnp.float32)
    window = padded(currents, (("near", 0),), leaf_slots)
    window_start = (device_index - 1) * leaf_slots
    sources = window[near_source - window_start]
    with_turned = jnp.concatenate([sources, turned(sources)], axis=2)
    near_field = jnp.einsum(
        "ienq,ieqr->inr", near_blocks, with_turned, preferred_element_type=jnp.float32
    )
    summed = far_field.reshape(leaf_slots, unknowns, channels) + near_field
    is_live = jnp.arange(leaf_slots) // 8 < own_count
    return jnp.where(is_live[:, None, None], summed, 0.0).astype(jnp.bfloat16)


def solution(mesh):
    return jax.shard_map(
        body,
        mesh=mesh,
        in_specs=(
            P(("dir", "near"), None, None),
            P(),
            P(("dir", "near"), None),
            P(("dir", "near"), None, None, None),
            P(),
            P(),
            P(None, None, ("dir", "near"), None, None),
            P(),
        ),
        out_specs=P(("dir", "near"), None, None),
        check_vma=False,
    )
```

profile of v0, /device:TPU:1, one launch (start us, length us, event | category | flops | bytes accessed | tf_op | source)
XLA Modules:
  0.0 114.9 jit_solution(8596844211028731293)
XLA Ops:
  0.0 4.9 %collective-permute-start = (bf16[32,128,128]{2,1,0:T(8,128)(2,1)}, bf16[32,128,128]{2,1,0:T(8,128)(2,1)}, u32[]{:S(2)}, u32[]{:S(2)}) collective-permute-start(bf16[32,128,128]{2,1,0:T(8,128)(2,1)} %param.8), channel_id=1, source_target_pairs={{0,1},{1,2},{2,3},{4,5},{5,6},{6,7},{8,9},{9,10},{10,11},{12,13},{... | collective-permute-start | bytes 3145736 | tf_op jit(solution)/shard_map/ppermute | solution.py:15
  4.9 1.3 %collective-permute-start.1 = (bf16[32,128,128]{2,1,0:T(8,128)(2,1)}, bf16[32,128,128]{2,1,0:T(8,128)(2,1)}, u32[]{:S(2)}, u32[]{:S(2)}) collective-permute-start(bf16[32,128,128]{2,1,0:T(8,128)(2,1)} %param.8), channel_id=1, source_target_pairs={{1,0},{2,1},{3,2},{5,4},{6,5},{7,6},{9,8},{10,9},{11,10},{13,12},{... | collective-permute-start | bytes 3145736 | tf_op jit(solution)/shard_map/ppermute | solution.py:17
  6.2 1.6 %copy.86 = bf16[32,128,128]{1,2,0:T(8,128)(2,1)S(1)} copy(bf16[32,128,128]{2,1,0:T(8,128)(2,1)} %param.8) | data formatting | bytes 2097152 | tf_op args[0]
  7.9 0.1 slice_negate_fusion.3
  8.0 5.2 %fusion.18 = bf16[4,1152,128]{1,2,0:T(8,128)(2,1)S(1)} fusion(bf16[8,1152,256]{2,1,0:T(8,128)(2,1)} %param.12, bf16[4,8,128,64]{2,3,1,0:T(8,128)(2,1)S(1)} %get-tuple-element.12, bf16[4,8,128,64]{2,3,1,0:T(8,128)(2,1)S(1)} %get-tuple-element.11, bf16[4,8,128,128]{2,3,1,0:T(8,128)(2,1)S(1)} %bitcast.80), kind=kOutput, calls=%fused_computation.20 | convolution fusion | flops 2422800384 | bytes 7995392 | tf_op jit(solution)/shard_map/ckq,scqr->skr/dot_general | solution.py:71
  13.2 0.0 copy-start.1
  13.2 0.0 copy-start.2
  13.2 2.0 %copy.87 = bf16[4,1152,128]{2,0,1:T(4,128)(2,1)} copy(bf16[4,1152,128]{1,2,0:T(8,128)(2,1)S(1)} %fusion.18) | data formatting | bytes 2359296 | tf_op jit(solution)/shard_map/convert_element_type | solution.py:73
  15.3 11.8 %all-to-all-start = ((bf16[1,4,128,9,128]{4,1,3,0,2:T(4,128)(2,1)}), bf16[1,4,128,9,128]{4,1,3,0,2:T(4,128)(2,1)S(1)}, u32[]{:S(2)}, u32[]{:S(2)}) async-start(bf16[1,4,128,9,128]{4,1,3,0,2:T(4,128)(2,1)} %bitcast.7), calls=%async_computation | async-start | bytes 2359296 | tf_op jit(solution)/shard_map/all_to_all | solution.py:34
  27.1 0.0 copy-done.1
  27.1 0.1 copy.90
  27.2 0.2 reduce-window.8
  27.4 0.1 reduce
  27.5 0.1 add_clamp_fusion
  27.6 0.0 copy-done.2
  27.6 0.1 reshape.153
  27.7 0.1 min.12
  27.8 0.1 select_reduce_fusion
  28.0 20.7 %all-to-all-done = bf16[1,4,128,9,128]{4,1,3,0,2:T(4,128)(2,1)S(1)} async-done(((bf16[1,4,128,9,128]{4,1,3,0,2:T(4,128)(2,1)}), bf16[1,4,128,9,128]{4,1,3,0,2:T(4,128)(2,1)S(1)}, u32[]{:S(2)}, u32[]{:S(2)}) %all-to-all-start) | async-done | bytes 1179680 | tf_op jit(solution)/shard_map/all_to_all | solution.py:34
  48.8 0.5 copy.89
  49.2 0.9 copy.91
  50.1 0.8 gather_fusion
  50.9 0.2 copy.94
  51.1 0.3 slice_negate_fusion.2
  51.4 0.4 maximum_maximum_fusion
  51.7 0.0 copy-start.3
  51.8 2.9 %gather_fusion.1 = bf16[12,128,9,128]{3,1,2,0:T(8,128)(2,1)} fusion(bf16[4,128,9,128]{3,1,2,0:T(8,128)(2,1)S(1)} %maximum_maximum_fusion, s32[1024]{0:T(1024)S(1)} %pad_clamp_fusion.2), kind=kCustom, calls=%fused_computation.1 | custom fusion | bytes 7077936 | tf_op jit(solution)/shard_map/gather | solution.py:52
  54.6 0.0 copy-done.3
  54.6 2.8 %fusion.45 = bf16[4,64,9,128]{3,1,2,0:T(8,128)(2,1)S(1)} fusion(bf16[4,3,128,9,128]{4,2,3,1,0:T(8,128)(2,1)} %bitcast.75, bf16[4,3,9,64,128]{4,3,2,1,0:T(8,128)(2,1)S(1)} %copy-done.3), kind=kOutput, calls=%fused_computation.37 | convolution fusion | flops 226787328 | bytes 5898240 | tf_op jit(solution)/shard_map/tlkij,tljkr->tikr/dot_general | solution.py:53
  57.5 0.4 copy.98
  57.9 2.0 %gather_fusion.2 = bf16[512,9,128]{2,1,0:T(8,128)(2,1)S(1)} fusion(bf16[256,9,128]{2,1,0:T(8,128)(2,1)S(1)} %copy.98, s32[1024]{0:T(1024)S(1)} %pad_clamp_fusion.1), kind=kCustom, calls=%fused_computation.2 | custom fusion | bytes 2361344 | tf_op jit(solution)/shard_map/gather | solution.py:85
  59.9 0.0 copy-start
  60.0 1.5 %copy.100 = bf16[128,4,1,9,128]{4,1,3,2,0:T(4,128)(2,1)} copy(bf16[128,4,1,9,128]{4,3,1,0,2:T(8,128)(2,1)S(1)} %bitcast.76) | data formatting | bytes 2359296 | tf_op jit(solution)/shard_map/reshape | solution.py:42
  61.4 7.1 %all-to-all-start.1 = ((bf16[128,4,1,9,128]{4,1,3,2,0:T(4,128)(2,1)}), bf16[128,4,1,9,128]{4,1,3,2,0:T(4,128)(2,1)}, u32[]{:S(2)}, u32[]{:S(2)}) async-start(bf16[128,4,1,9,128]{4,1,3,2,0:T(4,128)(2,1)} %copy.100), calls=%async_computation.1 | async-start | bytes 2359296 | tf_op jit(solution)/shard_map/all_to_all | solution.py:43
  68.5 0.6 dynamic_slice.3
  69.1 0.0 copy-done
  69.1 0.1 copy.104
  69.2 0.1 reshape.169
  69.3 0.7 fusion.50
  70.0 0.0 collective-permute-done
  70.0 0.0 collective-permute-done.1
  70.0 2.1 %pad_maximum_fusion = bf16[96,128,128]{2,1,0:T(8,128)(2,1)S(1)} fusion(bf16[32,128,128]{2,1,0:T(8,128)(2,1)} %collective-permute-done.1, bf16[32,128,128]{2,1,0:T(8,128)(2,1)} %param.8, bf16[32,128,128]{2,1,0:T(8,128)(2,1)} %collective-permute-done), kind=kLoop, calls=%fused_computation.18 | loop fusion | flops 3145728 | bytes 6291456 | tf_op jit(solution)/shard_map/concatenate | solution.py:13
  72.0 8.0 %gather_fusion.3 = bf16[192,128,128]{2,1,0:T(8,128)(2,1)} fusion(bf16[96,128,128]{2,1,0:T(8,128)(2,1)S(1)} %pad_maximum_fusion, s32[1024]{0:T(1024)S(1)} %pad_clamp_fusion), kind=kCustom, calls=%fused_computation.3 | custom fusion | bytes 12583680 | tf_op jit(solution)/shard_map/gather | solution.py:90
  80.1 8.6 %copy.105 = bf16[192,128,128]{1,2,0:T(8,128)(2,1)} copy(bf16[192,128,128]{2,1,0:T(8,128)(2,1)} %gather_fusion.3) | data formatting | bytes 12582912 | tf_op jit(solution)/shard_map/gather | solution.py:90
  88.7 6.2 %slice_negate_fusion = (bf16[32,6,128,64]{2,3,1,0:T(8,128)(2,1)}, bf16[32,6,128,64]{2,3,1,0:T(8,128)(2,1)}) fusion(bf16[32,6,128,128]{2,3,1,0:T(8,128)(2,1)} %bitcast.73), kind=kLoop, calls=%fused_computation.17 | loop fusion | flops 1572864 | bytes 12582912 | tf_op jit(solution)/shard_map/neg | solution.py:26
  94.9 0.0 all-to-all-done.1
  94.9 2.5 %copy.103 = bf16[4,1152,128]{1,2,0:T(8,128)(2,1)S(1)} copy(bf16[4,1152,128]{2,0,1:T(4,128)(2,1)} %bitcast.25) | data formatting | bytes 2359296 | tf_op jit(solution)/shard_map/reshape | solution.py:44
  97.4 0.1 slice_negate_fusion.1
  97.5 5.5 %fusion.6 = f32[4,128,8,128]{3,1,2,0:T(8,128)} fusion(bf16[8,128,2304]{2,1,0:T(8,128)(2,1)} %param.13, bf16[4,1152,64]{1,2,0:T(8,128)(2,1)S(1)} %get-tuple-element.10, bf16[4,1152,64]{1,2,0:T(8,128)(2,1)S(1)} %get-tuple-element.9, bf16[4,1152,128]{1,2,0:T(8,128)(2,1)S(1)} %copy.103), kind=kOutput, calls=%fused_computation.10 | convolution fusion | flops 2422996992 | bytes 9175040 | tf_op jit(solution)/shard_map/cpk,skr->scpr/dot_general | solution.py:87
  103.0 10.6 %fusion.31 = bf16[32,128,128]{1,2,0:T(8,128)(2,1)S(1)} fusion(f32[4,128,8,128]{3,1,2,0:T(8,128)} %fusion.6, bf16[32,6,128,256]{3,2,1,0:T(8,128)(2,1)} %param.11, bf16[32,6,128,64]{2,3,1,0:T(8,128)(2,1)} %get-tuple-element.8, bf16[32,6,128,64]{2,3,1,0:T(8,128)(2,1)} %get-tuple-element.7, bf16[32,6,128,128]{2,3,1,0:T(8,128)(2,1)} %bitcast.74, ...), kind=kOutput, calls=%fused_computation.33 | convolution fusion | flops 1649934336 | bytes 28311584 | tf_op jit(solution)/shard_map/ienq,ieqr->inr/dot_general | solution.py:92
  113.6 1.3 %copy.106 = bf16[32,128,128]{2,1,0:T(8,128)(2,1)} copy(bf16[32,128,128]{1,2,0:T(8,128)(2,1)S(1)} %fusion.31) | data formatting | bytes 2097152 | tf_op jit(solution)/shard_map/convert_element_type | solution.py:97
  (11 shorter events, 0.1 us)
Async XLA Ops:
  0.0 70.0 %collective-permute-start = (bf16[32,128,128]{2,1,0:T(8,128)(2,1)}, bf16[32,128,128]{2,1,0:T(8,128)(2,1)}, u32[]{:S(2)}, u32[]{:S(2)}) collective-permute-start(bf16[32,128,128]{2,1,0:T(8,128)(2,1)} %param.8), channel_id=1, source_target_pairs={{0,1},{1,2},{2,3},{4,5},{5,6},{6,7},{8,9},{9,10},{10,11},{12,13},{... | collective-permute-start | bytes 3145736 | tf_op jit(solution)/shard_map/ppermute | solution.py:15
  4.9 65.0 %collective-permute-start.1 = (bf16[32,128,128]{2,1,0:T(8,128)(2,1)}, bf16[32,128,128]{2,1,0:T(8,128)(2,1)}, u32[]{:S(2)}, u32[]{:S(2)}) collective-permute-start(bf16[32,128,128]{2,1,0:T(8,128)(2,1)} %param.8), channel_id=1, source_target_pairs={{1,0},{2,1},{3,2},{5,4},{6,5},{7,6},{9,8},{10,9},{11,10},{13,12},{... | collective-permute-start | bytes 3145736 | tf_op jit(solution)/shard_map/ppermute | solution.py:17
  13.2 13.9 %copy-start.1 = (s32[128]{0:T(128)S(1)}, s32[128]{0:T(128)}, u32[]{:S(2)}) copy-start(s32[128]{0:T(128)} %param.9) | copy-start | bytes 1540
  13.2 14.4 %copy-start.2 = (s32[4,3]{1,0:T(4,128)S(1)}, s32[4,3]{1,0:T(4,128)}, u32[]{:S(2)}) copy-start(s32[4,3]{1,0:T(4,128)} %param.15) | copy-start | bytes 148
  15.3 33.5 %all-to-all-start = ((bf16[1,4,128,9,128]{4,1,3,0,2:T(4,128)(2,1)}), bf16[1,4,128,9,128]{4,1,3,0,2:T(4,128)(2,1)S(1)}, u32[]{:S(2)}, u32[]{:S(2)}) async-start(bf16[1,4,128,9,128]{4,1,3,0,2:T(4,128)(2,1)} %bitcast.7), calls=%async_computation | async-start | bytes 2359296 | tf_op jit(solution)/shard_map/all_to_all | solution.py:34
  51.7 2.9 %copy-start.3 = (bf16[4,3,9,64,128]{4,3,2,1,0:T(8,128)(2,1)S(1)}, bf16[4,3,9,64,128]{4,3,2,1,0:T(8,128)(2,1)}, u32[]{:S(2)}) copy-start(bf16[4,3,9,64,128]{4,3,2,1,0:T(8,128)(2,1)} %param.14) | copy-start | bytes 5308420
  59.9 9.1 %copy-start = (s32[32,6]{0,1:T(8,128)S(1)}, s32[32,6]{0,1:T(8,128)}, u32[]{:S(2)}) copy-start(s32[32,6]{0,1:T(8,128)} %param.10) | copy-start | bytes 2308
  61.4 33.4 %all-to-all-start.1 = ((bf16[128,4,1,9,128]{4,1,3,2,0:T(4,128)(2,1)}), bf16[128,4,1,9,128]{4,1,3,2,0:T(4,128)(2,1)}, u32[]{:S(2)}, u32[]{:S(2)}) async-start(bf16[128,4,1,9,128]{4,1,3,2,0:T(4,128)(2,1)} %copy.100), calls=%async_computation.1 | async-start | bytes 2359296 | tf_op jit(solution)/shard_map/all_to_all | solution.py:43
where the time goes:
time: 116 us; the launch traced here: 115 us
  local copies, waits for them, and re-layouts  34.4 us (30%)
  starting transfers between devices  25.1 us (22%)
  matrix products  24.1 us (21%)
  waiting for transfers between devices  20.7 us (18%)
  other arithmetic  10.2 us (9%)
    all_to_all x1, waiting for transfers between devices, regroup(): lax.all_to_all(shaped, ('dir', 'near'), split_axis=2, concat_axis=0, tile...  20.7 us
    gather x2, local copies, waits for them, and re-layouts, body(): sources = window[near_source - window_start]  16.7 us
    all_to_all x1, starting transfers between devices, regroup(): lax.all_to_all(shaped, ('dir', 'near'), split_axis=2, concat_axis=0, tile...  11.8 us
    dot_general x1, matrix products, body(): jnp.einsum('ienq,ieqr->inr', near_blocks, with_turned, preferred_element_...  10.6 us
    all_to_all x1, starting transfers between devices, collect(): lax.all_to_all(shaped, ('dir', 'near'), split_axis=0, concat_axis=2, tile...  7.05 us
    neg x4, other arithmetic, turned(): -values[..., middle:]  6.6 us
    dot_general x1, matrix products, body(): jnp.einsum('cpk,skr->scpr', receive, doubled, preferred_element_type=jnp....  5.47 us
    dot_general x1, matrix products, body(): jnp.einsum('ckq,scqr->skr', aggregate, stacked, preferred_element_type=jn...  5.24 us
  transfers between devices with their start and end apart: 4, of which 1 were waited for; matrix products, arithmetic and copies ran while one was open for 42% of the time, Pallas kernels for 0%

commit v1 on v0

v1 whole, which is shorter than its diff:
```python
import numpy as np
import jax
import jax.numpy as jnp
from jax import lax
from jax.experimental import pallas as pl
from jax.experimental.pallas import tpu as pltpu
from jax.sharding import PartitionSpec as P

AXES = ("dir", "near")
MIB = 1 << 20


def turned(values):
    middle = values.shape[-1] // 2
    return jnp.concatenate([-values[..., middle:], values[..., :middle]], axis=-1)


def radiate_kernel(place_ref, currents_ref, aggregate_ref, out_ref, stacked_ref, rows_ref):
    children = aggregate_ref.shape[0]
    tile = aggregate_ref.shape[1]
    positions = stacked_ref.shape[2] // 128

    @pl.when(pl.program_id(0) == 0)
    def _():
        offset = place_ref[0]
        count = place_ref[1]
        for p in range(positions):
            slot = p - offset
            live = jnp.logical_and(slot >= 0, slot < count)
            row = jnp.clip(slot, 0, positions - 1) * children

            @pl.when(live)
            def _():
                for c in range(children):
                    v = currents_ref[row + c]
                    stacked_ref[c, 0:128, p * 128 : (p + 1) * 128] = v
                    stacked_ref[c, 128:256, p * 128 : (p + 1) * 128] = turned(v)

            @pl.when(jnp.logical_not(live))
            def _():
                stacked_ref[:, :, p * 128 : (p + 1) * 128] = jnp.zeros(
                    (children, 256, 128), jnp.bfloat16
                )

    total = jnp.dot(aggregate_ref[0], stacked_ref[0], preferred_element_type=jnp.float32)
    for c in range(1, children):
        total += jnp.dot(aggregate_ref[c], stacked_ref[c], preferred_element_type=jnp.float32)
    for p in range(positions):
        rows_ref[pl.ds(p, tile, stride=positions), :] = total[:, p * 128 : (p + 1) * 128]
    out_ref[...] = rows_ref[...].astype(jnp.bfloat16)


def radiate(place, currents, aggregate):
    children, directions, width = aggregate.shape
    positions = currents.shape[0] // children
    tile = 144
    return pl.pallas_call(
        radiate_kernel,
        grid_spec=pltpu.PrefetchScalarGridSpec(
            num_scalar_prefetch=1,
            grid=(directions // tile,),
            in_specs=[
                pl.BlockSpec(currents.shape, lambda i, _: (0, 0, 0)),
                pl.BlockSpec((children, tile, width), lambda i, _: (0, i, 0)),
            ],
            out_specs=pl.BlockSpec((tile * positions, 128), lambda i, _: (i, 0)),
            scratch_shapes=[
                pltpu.VMEM((children, width, positions * 128), jnp.bfloat16),
                pltpu.VMEM((tile * positions, 128), jnp.float32),
            ],
        ),
        out_shape=jax.ShapeDtypeStruct((directions * positions, 128), jnp.bfloat16),
        compiler_params=pltpu.CompilerParams(vmem_limit_bytes=32 * MIB),
        name="radiate",
    )(place, currents, aggregate)


def pair_rows(per_group, positions):
    pairs = 4
    select = np.zeros((per_group * pairs * positions, 2 * pairs * per_group * positions))
    for r in range(per_group):
        for pair in range(pairs):
            for p in range(positions):
                row = (r * pairs + pair) * positions + p
                for side in range(2):
                    select[row, ((2 * pair + side) * per_group + r) * positions + p] = 1.0
    return select


def translate_kernel(
    blocks_ref, rows_ref, translations_ref, select_ref, spread_ref, out_ref, values_ref, sums_ref
):
    block_count, list_length, per_group = translations_ref.shape[:3]
    block = translations_ref.shape[3]
    chunk = select_ref.shape[1]
    groups = rows_ref.shape[0] // chunk
    per_block = groups // block_count
    step = block // per_block
    for g in range(groups):
        picked = jnp.dot(
            select_ref[...],
            rows_ref[g * chunk : (g + 1) * chunk, :],
            preferred_element_type=jnp.float32,
        ).astype(jnp.bfloat16)
        other = turned(picked)
        b = g // per_block
        start = (g % per_block) * step
        for r in range(per_group):
            part = slice(r * step, (r + 1) * step)
            values_ref[b, r, start : start + step, :] = picked[part]
            values_ref[b, r, block + start : block + start + step, :] = other[part]
    for t in range(block_count):
        for r in range(per_group):
            total = jnp.dot(
                translations_ref[t, 0, r],
                values_ref[blocks_ref[t, 0], r],
                preferred_element_type=jnp.float32,
            )
            for e in range(1, list_length):
                total += jnp.dot(
                    translations_ref[t, e, r],
                    values_ref[blocks_ref[t, e], r],
                    preferred_element_type=jnp.float32,
                )
            total = total.astype(jnp.bfloat16)
            for q in range(per_block):
                sums_ref[t * per_block + q, r * step : (r + 1) * step, :] = total[
                    q * step : (q + 1) * step
                ]
    for g in range(groups):
        out_ref[g * chunk : (g + 1) * chunk, :] = jnp.dot(
            spread_ref[...], sums_ref[g], preferred_element_type=jnp.float32
        ).astype(jnp.bfloat16)


def translate(source_blocks, rows, translations, positions):
    block_count, _, per_group, block, doubled = translations.shape
    select = pair_rows(per_group, positions)
    groups = rows.shape[0] // select.shape[1]
    vmem = pl.BlockSpec(memory_space=pltpu.VMEM)
    return pl.pallas_call(
        translate_kernel,
        in_specs=[pl.BlockSpec(memory_space=pltpu.SMEM), vmem, vmem, vmem, vmem],
        out_specs=vmem,
        scratch_shapes=[
            pltpu.VMEM((block_count, per_group, doubled, 128), jnp.bfloat16),
            pltpu.VMEM((groups, select.shape[0], 128), jnp.bfloat16),
        ],
        out_shape=jax.ShapeDtypeStruct(rows.shape, jnp.bfloat16),
        compiler_params=pltpu.CompilerParams(vmem_limit_bytes=32 * MIB),
        name="translate",
    )(
        source_blocks,
        rows,
        translations,
        jnp.asarray(select, jnp.bfloat16),
        jnp.asarray(select.T, jnp.bfloat16),
    )


def near_kernel(source_ref, left_ref, own_ref, right_ref, blocks_ref, out_ref, window_ref):
    slots = own_ref.shape[0]
    unknowns = own_ref.shape[1]
    terms = blocks_ref.shape[1]
    leaf = pl.program_id(0)

    @pl.when(leaf == 0)
    def _():
        for part, ref in enumerate((left_ref, own_ref, right_ref)):

            def fill(i, carry, part=part, ref=ref):
                v = ref[i]
                window_ref[part * slots + i, 0:unknowns, :] = v
                window_ref[part * slots + i, unknowns : 2 * unknowns, :] = turned(v)
                return carry

            lax.fori_loop(0, slots, fill, 0)

    total = jnp.dot(
        blocks_ref[0, 0], window_ref[source_ref[leaf * terms]], preferred_element_type=jnp.float32
    )
    for e in range(1, terms):
        total += jnp.dot(
            blocks_ref[0, e],
            window_ref[source_ref[leaf * terms + e]],
            preferred_element_type=jnp.float32,
        )
    out_ref[0] = total


def near(source, left, own, right, blocks):
    slots, unknowns, channels = own.shape
    _, terms, _, doubled = blocks.shape
    whole = pl.BlockSpec(own.shape, lambda i, _: (0, 0, 0))
    return pl.pallas_call(
        near_kernel,
        grid_spec=pltpu.PrefetchScalarGridSpec(
            num_scalar_prefetch=1,
            grid=(slots,),
            in_specs=[
                whole,
                whole,
                whole,
                pl.BlockSpec((1, terms, unknowns, doubled), lambda i, _: (i, 0, 0, 0)),
            ],
            out_specs=pl.BlockSpec((1, unknowns, channels), lambda i, _: (i, 0, 0)),
            scratch_shapes=[pltpu.VMEM((3 * slots, doubled, channels), jnp.bfloat16)],
        ),
        out_shape=jax.ShapeDtypeStruct((slots, unknowns, channels), jnp.float32),
        compiler_params=pltpu.CompilerParams(vmem_limit_bytes=40 * MIB),
        name="near",
    )(source.reshape(-1), left, own, right, blocks)


def receive_kernel(place_ref, rows_ref, receive_ref, near_ref, out_ref, wide_ref, doubled_ref):
    octants = receive_ref.shape[0]
    unknowns = receive_ref.shape[1]
    directions = receive_ref.shape[2] // 2
    positions = doubled_ref.shape[1] // 128
    children = 8
    step = pl.program_id(0)
    offset = place_ref[0]
    count = place_ref[1]

    @pl.when(step == 0)
    def _():
        wide_ref[...] = rows_ref[...].astype(jnp.float32)
        for p in range(positions):
            v = wide_ref[pl.ds(p, directions, stride=positions), :].astype(jnp.bfloat16)
            doubled_ref[0:directions, p * 128 : (p + 1) * 128] = v
            doubled_ref[directions : 2 * directions, p * 128 : (p + 1) * 128] = turned(v)
        out_ref[...] = jnp.zeros(out_ref.shape, out_ref.dtype)

    lines = receive_ref[...].reshape(octants * unknowns, 2 * directions)
    far = jnp.dot(lines, doubled_ref[...], preferred_element_type=jnp.float32)
    for p in range(positions):
        slot = p - offset

        @pl.when(jnp.logical_and(slot >= 0, slot < count))
        def _():
            for c in range(octants):
                leaf = slot * children + step * octants + c
                part = far[c * unknowns : (c + 1) * unknowns, p * 128 : (p + 1) * 128]
                out_ref[leaf] = (part + near_ref[leaf]).astype(jnp.bfloat16)


def absorb(place, rows, receive, near_field):
    children, unknowns, doubled = receive.shape
    slots = near_field.shape[0]
    positions = slots // children
    octants = 2
    return pl.pallas_call(
        receive_kernel,
        grid_spec=pltpu.PrefetchScalarGridSpec(
            num_scalar_prefetch=1,
            grid=(children // octants,),
            in_specs=[
                pl.BlockSpec(rows.shape, lambda i, _: (0, 0)),
                pl.BlockSpec((octants, unknowns, doubled), lambda i, _: (i, 0, 0)),
                pl.BlockSpec(near_field.shape, lambda i, _: (0, 0, 0)),
            ],
            out_specs=pl.BlockSpec(near_field.shape, lambda i, _: (0, 0, 0)),
            scratch_shapes=[
                pltpu.VMEM(rows.shape, jnp.float32),
                pltpu.VMEM((doubled, positions * 128), jnp.bfloat16),
            ],
        ),
        out_shape=jax.ShapeDtypeStruct(near_field.shape, jnp.bfloat16),
        compiler_params=pltpu.CompilerParams(vmem_limit_bytes=40 * MIB),
        name="absorb",
    )(place, rows, receive, near_field)


def in_hbm(array):
    return pltpu.with_memory_space_constraint(array, pltpu.HBM)


def swap(rows, positions):
    channels = rows.shape[-1]
    shaped = rows.reshape(-1, positions, channels)
    return lax.all_to_all(shaped, AXES, 0, 0, tiled=True).reshape(-1, channels)


def body(
    currents, counts, near_source, near_blocks, aggregate, receive, translations, source_blocks
):
    device = lax.axis_index(AXES)
    slots, unknowns, channels = currents.shape
    positions = slots // aggregate.shape[0]
    own_count = counts[device]
    offset = jnp.where(device % 2 == 1, counts[device - device % 2], 0)
    place = jnp.stack([offset, own_count]).astype(jnp.int32)

    patterns = radiate(place, in_hbm(currents), in_hbm(aggregate))
    gathered = swap(patterns, positions)

    later, _ = lax.optimization_barrier((currents, patterns))
    count = lax.axis_size("near")
    left = lax.ppermute(later, "near", [(i, i + 1) for i in range(count - 1)])
    right = lax.ppermute(later, "near", [(i + 1, i) for i in range(count - 1)])
    gathered, left, right = lax.optimization_barrier((gathered, left, right))

    incoming = translate(source_blocks, gathered, translations, positions)
    returned = swap(incoming, positions)

    local = near_source - (device - 1) * slots
    local, _ = lax.optimization_barrier((local, incoming))
    near_field = near(local, left, in_hbm(currents), right, in_hbm(near_blocks))
    return absorb(place, returned, in_hbm(receive), near_field)


def solution(mesh):
    spread = P(AXES, None, None)
    return jax.shard_map(
        body,
        mesh=mesh,
        in_specs=(
            spread,
            P(),
            P(AXES, None),
            P(AXES, None, None, None),
            P(),
            P(),
            P(None, None, AXES, None, None),
            P(),
        ),
        out_specs=spread,
        check_vma=False,
    )
```

time: 116 us -> 118 us (1.017)
  Pallas kernels: 0 us -> 51 us
  local copies, waits for them, and re-layouts: 34.4 us -> 5.97 us
  matrix products: 24.1 us -> 0 us
  waiting for transfers between devices: 20.7 us -> 31.2 us
  other arithmetic: 10.2 us -> 0.7 us
  starting transfers between devices: 25.1 us -> 27.3 us
    pallas_call x0 -> x4, Pallas kernels: none -> 51 us  [the longest x1 30.3 us: near(): pl.pallas_call(near_kernel, grid_spec=pltpu.PrefetchScalarGridSpec(num_sc...]
    ppermute x2, waiting for transfers between devices: 0.01 us -> 31.2 us  [the longest x1 31.2 us: body(): right = lax.ppermute(later, 'near', [(i + 1, i) for i in range(count - 1)])]
    dot_general x4 -> x0, matrix products: 24.1 us -> none  [the longest x1 10.6 us: body(): jnp.einsum('ienq,ieqr->inr', near_blocks, with_turned, preferred_element_...]
    gather x5 -> x0, local copies, waits for them, and re-layouts: 22.4 us -> none  [the longest x2 16.7 us: body(): sources = window[near_source - window_start]]
    all_to_all x2, waiting for transfers between devices: 20.7 us -> 0.01 us  [swap(): return lax.all_to_all(shaped, AXES, 0, 0, tiled=True).reshape(-1, channels)]
    neg x4 -> x0, other arithmetic: 6.6 us -> none  [turned(): -values[..., middle:]]
    reshape x5 -> x1, local copies, waits for them, and re-layouts: 5.48 us -> 0.1 us  [near(): source.reshape(-1)]
    convert_element_type x3 -> x0, local copies, waits for them, and re-layouts: 3.37 us -> none  [the longest x1 2.02 us: body(): patterns = jnp.einsum('ckq,scqr->skr', aggregate, stacked, preferred_elem...]
  transfers between devices with their start and end apart: 4 -> 4, of which waited for: 1 -> 1; matrix products, arithmetic and copies ran while one was open for 42% -> 0% of each run, Pallas kernels for 0% -> 26%
where the time goes in v1:
time: 118 us; the launch traced here: 117 us
  Pallas kernels  51 us (43%)
  waiting for transfers between devices  31.2 us (26%)
  starting transfers between devices  27.3 us (23%)
  local copies, waits for them, and re-layouts  5.97 us (5%)
    ppermute x1, waiting for transfers between devices, body(): right = lax.ppermute(later, 'near', [(i + 1, i) for i in range(count - 1)])  31.2 us
    pallas_call x1, Pallas kernels, near(): pl.pallas_call(near_kernel, grid_spec=pltpu.PrefetchScalarGridSpec(num_sc...  30.3 us
    all_to_all x2, starting transfers between devices, swap(): return lax.all_to_all(shaped, AXES, 0, 0, tiled=True).reshape(-1, channels)  21.9 us
    pallas_call x1, Pallas kernels, radiate(): pl.pallas_call(radiate_kernel, grid_spec=pltpu.PrefetchScalarGridSpec(num...  9.04 us
    pallas_call x1, Pallas kernels, absorb(): pl.pallas_call(receive_kernel, grid_spec=pltpu.PrefetchScalarGridSpec(num...  7.56 us
    unnamed x18, local copies, waits for them, and re-layouts  4.4 us
    pallas_call x1, Pallas kernels, translate(): pl.pallas_call(translate_kernel, in_specs=[pl.BlockSpec(memory_space=pltp...  4.14 us
    ppermute x1, starting transfers between devices, body(): left = lax.ppermute(later, 'near', [(i, i + 1) for i in range(count - 1)])  4.06 us
  transfers between devices with their start and end apart: 4, of which 1 were waited for; matrix products, arithmetic and copies ran while one was open for 0% of the time, Pallas kernels for 26%

profile of v1, /device:TPU:1, one launch (start us, length us, event | category | flops | bytes accessed | tf_op | source)
XLA Modules:
  0.0 116.9 jit_solution(14910380315052109901)
XLA Ops:
  0.0 1.4 %fusion = (s32[1]{0:T(128)}, s32[1]{0:T(128)}) fusion(s32[128]{0:T(128)} %param.11, s32[]{:T(128)S(6)} %select_n.20, s32[]{:T(128)S(6)} %select_n.22), kind=kLoop, calls=%fused_computation.2 | loop fusion | bytes 24 | tf_op jit(solution)/shard_map/dynamic_slice | solution.py:291
  2.0 0.7 pad_add_fusion.place_ref
  2.7 9.0 %radiate.1 = bf16[4608,128]{1,0:T(8,128)(2,1)} custom-call(s32[2]{0:T(128)S(1)} %pad_add_fusion.place_ref, bf16[32,128,128]{2,1,0:T(8,128)(2,1)} %own_ref.1, bf16[8,1152,256]{2,1,0:T(8,128)(2,1)} %aggregate_ref.1), custom_call_target="tpu_custom_call" | custom-call | tf_op jit(solution)/shard_map/radiate/pallas_call | solution.py:57
  11.8 0.0 copy-start
  11.8 0.0 copy-start.5
  11.8 0.0 copy-start.6
  11.8 0.0 copy-start.7
  11.8 12.1 %all-to-all-start = ((bf16[1152,4,128]{2,1,0:T(4,128)(2,1)}), bf16[1152,4,128]{2,1,0:T(4,128)(2,1)S(1)}, u32[]{:S(2)}, u32[]{:S(2)}) async-start(bf16[1152,4,128]{2,1,0:T(4,128)(2,1)} %bitcast.2), calls=%async_computation | async-start | bytes 2359296 | tf_op jit(solution)/shard_map/all_to_all | solution.py:281
  23.9 1.3 %collective-permute-start.1 = (bf16[32,128,128]{2,1,0:T(8,128)(2,1)}, bf16[32,128,128]{2,1,0:T(8,128)(2,1)S(1)}, u32[]{:S(2)}, u32[]{:S(2)}) collective-permute-start(bf16[32,128,128]{2,1,0:T(8,128)(2,1)} %own_ref.1), channel_id=1, source_target_pairs={{1,0},{2,1},{3,2},{5,4},{6,5},{7,6},{9,8},{10,9},{11,10},{13,12},{... | collective-permute-start | bytes 3145736 | tf_op jit(solution)/shard_map/ppermute | solution.py:300
  25.2 4.1 %collective-permute-start = (bf16[32,128,128]{2,1,0:T(8,128)(2,1)}, bf16[32,128,128]{2,1,0:T(8,128)(2,1)S(1)}, u32[]{:S(2)}, u32[]{:S(2)}) collective-permute-start(bf16[32,128,128]{2,1,0:T(8,128)(2,1)} %own_ref.1), channel_id=1, source_target_pairs={{0,1},{1,2},{2,3},{4,5},{5,6},{6,7},{8,9},{9,10},{10,11},{12,13},{... | collective-permute-start | bytes 3145736 | tf_op jit(solution)/shard_map/ppermute | solution.py:299
  29.3 31.2 %collective-permute-done.1.right_ref = bf16[32,128,128]{2,1,0:T(8,128)(2,1)S(1)} collective-permute-done((bf16[32,128,128]{2,1,0:T(8,128)(2,1)}, bf16[32,128,128]{2,1,0:T(8,128)(2,1)S(1)}, u32[]{:S(2)}, u32[]{:S(2)}) %collective-permute-start.1) | collective-permute-done | bytes 1048608 | tf_op jit(solution)/shard_map/ppermute | solution.py:300
  60.5 0.0 copy-start.1
  60.5 1.0 copy-done.1
  61.5 0.0 collective-permute-done.left_ref
  61.5 0.0 copy-start.3
  61.5 1.0 copy-done.3
  62.4 0.0 all-to-all-done
  62.4 0.0 copy-done
  62.4 0.0 copy-done.5
  62.5 0.0 copy-done.6
  62.5 0.0 copy-done.7
  62.5 4.1 %translate.1 = bf16[4608,128]{1,0:T(8,128)(2,1)} custom-call(s32[4,3]{1,0:T(4,128)S(1)} %copy-done.7, bf16[4608,128]{1,0:T(8,128)(2,1)S(1)} %bitcast.7, bf16[4,3,9,64,128]{4,3,2,1,0:T(8,128)(2,1)S(1)} %copy-done, bf16[144,288]{1,0:T(8,128)(2,1)S(1)} %copy-done.6, bf16[288,144]{1,0:T(8,128)(2,1)S(1)} %copy-done.5), custom_call_target="tpu_custom_call" | custom-call | tf_op jit(solution)/shard_map/translate/pallas_call | solution.py:141
  66.6 0.0 copy-start.8
  66.6 9.8 %all-to-all-start.1 = ((bf16[1152,4,128]{2,1,0:T(4,128)(2,1)}), bf16[1152,4,128]{2,1,0:T(4,128)(2,1)S(1)}, u32[]{:S(2)}, u32[]{:S(2)}) async-start(bf16[1152,4,128]{2,1,0:T(4,128)(2,1)} %bitcast.4), calls=%async_computation.1 | async-start | bytes 2359296 | tf_op jit(solution)/shard_map/all_to_all | solution.py:281
  76.4 0.0 copy-done.8
  76.4 0.1 copy.11
  76.5 0.1 reshape.19.source_ref
  76.6 0.0 copy-start.2
  76.6 1.2 %copy-done.2 = bf16[32,128,128]{2,1,0:T(8,128)(2,1)S(1)} copy-done((bf16[32,128,128]{2,1,0:T(8,128)(2,1)S(1)}, bf16[32,128,128]{2,1,0:T(8,128)(2,1)}, u32[]{:S(2)}) %copy-start.2) | copy-done | bytes 1048600
  77.9 0.0 copy-start.4
  77.9 1.2 %copy-done.4 = bf16[32,128,128]{2,1,0:T(8,128)(2,1)S(1)} copy-done((bf16[32,128,128]{2,1,0:T(8,128)(2,1)S(1)}, bf16[32,128,128]{2,1,0:T(8,128)(2,1)}, u32[]{:S(2)}) %copy-start.4) | copy-done | bytes 1048600
  79.1 30.3 %near.1.near_ref = f32[32,128,128]{2,1,0:T(8,128)S(1)} custom-call(s32[192]{0:T(256)S(1)} %reshape.19.source_ref, bf16[32,128,128]{2,1,0:T(8,128)(2,1)S(1)} %copy-done.4, bf16[32,128,128]{2,1,0:T(8,128)(2,1)} %own_ref.1, bf16[32,128,128]{2,1,0:T(8,128)(2,1)S(1)} %copy-done.2, bf16[32,6,128,256]{3,2,1,0:T(8,128)(2,1)} %blocks_ref.3), custom_call_target="tpu_custom_call" | custom-call | tf_op jit(solution)/shard_map/near/pallas_call | solution.py:195
  109.4 0.0 all-to-all-done.1
  109.4 7.6 %absorb.1 = bf16[32,128,128]{2,1,0:T(8,128)(2,1)} custom-call(s32[2]{0:T(128)S(1)} %pad_add_fusion.place_ref, bf16[4608,128]{1,0:T(8,128)(2,1)S(1)} %bitcast.6, bf16[8,128,2304]{2,1,0:T(8,128)(2,1)} %receive_ref.1, f32[32,128,128]{2,1,0:T(8,128)S(1)} %near.1.near_ref), custom_call_target="tpu_custom_call" | custom-call | tf_op jit(solution)/shard_map/absorb/pallas_call | solution.py:252
  (1 shorter events, 0.0 us)
Async XLA Ops:
  11.8 50.7 %copy-start = (bf16[4,3,9,64,128]{4,3,2,1,0:T(8,128)(2,1)S(1)}, bf16[4,3,9,64,128]{4,3,2,1,0:T(8,128)(2,1)}, u32[]{:S(2)}) copy-start(bf16[4,3,9,64,128]{4,3,2,1,0:T(8,128)(2,1)} %translations_ref.1) | copy-start | bytes 5308420
  11.8 50.7 %copy-start.5 = (bf16[288,144]{1,0:T(8,128)(2,1)S(1)}, bf16[288,144]{1,0:T(8,128)(2,1)}, u32[]{:S(2)}) copy-start(bf16[288,144]{1,0:T(8,128)(2,1)} %constant.39.clone.spread_ref) | copy-start | bytes 248836
  11.8 50.7 %copy-start.6 = (bf16[144,288]{1,0:T(8,128)(2,1)S(1)}, bf16[144,288]{1,0:T(8,128)(2,1)}, u32[]{:S(2)}) copy-start(bf16[144,288]{1,0:T(8,128)(2,1)} %constant.38.clone.select_ref) | copy-start | bytes 248836
  11.8 50.7 %copy-start.7 = (s32[4,3]{1,0:T(4,128)S(1)}, s32[4,3]{1,0:T(4,128)}, u32[]{:S(2)}) copy-start(s32[4,3]{1,0:T(4,128)} %blocks_ref.2) | copy-start | bytes 148
  11.8 50.7 %all-to-all-start = ((bf16[1152,4,128]{2,1,0:T(4,128)(2,1)}), bf16[1152,4,128]{2,1,0:T(4,128)(2,1)S(1)}, u32[]{:S(2)}, u32[]{:S(2)}) async-start(bf16[1152,4,128]{2,1,0:T(4,128)(2,1)} %bitcast.2), calls=%async_computation | async-start | bytes 2359296 | tf_op jit(solution)/shard_map/all_to_all | solution.py:281
  23.9 36.6 %collective-permute-start.1 = (bf16[32,128,128]{2,1,0:T(8,128)(2,1)}, bf16[32,128,128]{2,1,0:T(8,128)(2,1)S(1)}, u32[]{:S(2)}, u32[]{:S(2)}) collective-permute-start(bf16[32,128,128]{2,1,0:T(8,128)(2,1)} %own_ref.1), channel_id=1, source_target_pairs={{1,0},{2,1},{3,2},{5,4},{6,5},{7,6},{9,8},{10,9},{11,10},{13,12},{... | collective-permute-start | bytes 3145736 | tf_op jit(solution)/shard_map/ppermute | solution.py:300
  25.2 36.3 %collective-permute-start = (bf16[32,128,128]{2,1,0:T(8,128)(2,1)}, bf16[32,128,128]{2,1,0:T(8,128)(2,1)S(1)}, u32[]{:S(2)}, u32[]{:S(2)}) collective-permute-start(bf16[32,128,128]{2,1,0:T(8,128)(2,1)} %own_ref.1), channel_id=1, source_target_pairs={{0,1},{1,2},{2,3},{4,5},{5,6},{6,7},{8,9},{9,10},{10,11},{12,13},{... | collective-permute-start | bytes 3145736 | tf_op jit(solution)/shard_map/ppermute | solution.py:299
  60.5 1.0 copy-start.1
  61.5 1.0 copy-start.3
  66.6 9.8 %copy-start.8 = (s32[32,6]{0,1:T(8,128)S(1)}, s32[32,6]{0,1:T(8,128)}, u32[]{:S(2)}) copy-start(s32[32,6]{0,1:T(8,128)} %param.12) | copy-start | bytes 2308
  66.6 42.8 %all-to-all-start.1 = ((bf16[1152,4,128]{2,1,0:T(4,128)(2,1)}), bf16[1152,4,128]{2,1,0:T(4,128)(2,1)S(1)}, u32[]{:S(2)}, u32[]{:S(2)}) async-start(bf16[1152,4,128]{2,1,0:T(4,128)(2,1)} %bitcast.4), calls=%async_computation.1 | async-start | bytes 2359296 | tf_op jit(solution)/shard_map/all_to_all | solution.py:281
  76.6 1.2 %copy-start.2 = (bf16[32,128,128]{2,1,0:T(8,128)(2,1)S(1)}, bf16[32,128,128]{2,1,0:T(8,128)(2,1)}, u32[]{:S(2)}) copy-start(bf16[32,128,128]{2,1,0:T(8,128)(2,1)} %copy-done.1) | copy-start | bytes 3145732
  77.9 1.2 %copy-start.4 = (bf16[32,128,128]{2,1,0:T(8,128)(2,1)S(1)}, bf16[32,128,128]{2,1,0:T(8,128)(2,1)}, u32[]{:S(2)}) copy-start(bf16[32,128,128]{2,1,0:T(8,128)(2,1)} %copy-done.3) | copy-start | bytes 3145732

commit v2 on v1

--- a/solution.py
+++ b/solution.py
@@ -15,15 +15,26 @@
     return jnp.concatenate([-values[..., middle:], values[..., :middle]], axis=-1)
 
 
-def radiate_kernel(place_ref, currents_ref, aggregate_ref, out_ref, stacked_ref, rows_ref):
+def quarter(v):
+    lane = lax.broadcasted_iota(jnp.int32, (1, v.shape[-1]), 1)
+    sign = jnp.where(lane < v.shape[-1] // 2, -1.0, 1.0).astype(v.dtype)
+    return pltpu.roll(v, v.shape[-1] // 2, 1) * sign
+
+
+def own_range(counts_ref):
+    device = lax.axis_index("dir") * lax.axis_size("near") + lax.axis_index("near")
+    odd = device % 2
+    return odd * counts_ref[device - odd], counts_ref[device]
+
+
+def radiate_kernel(counts_ref, currents_ref, aggregate_ref, out_ref, stacked_ref, rows_ref):
     children = aggregate_ref.shape[0]
     tile = aggregate_ref.shape[1]
     positions = stacked_ref.shape[2] // 128
 
     @pl.when(pl.program_id(0) == 0)
     def _():
-        offset = place_ref[0]
-        count = place_ref[1]
+        offset, count = own_range(counts_ref)
         for p in range(positions):
             slot = p - offset
             live = jnp.logical_and(slot >= 0, slot < count)
@@ -34,7 +45,7 @@
                 for c in range(children):
                     v = currents_ref[row + c]
                     stacked_ref[c, 0:128, p * 128 : (p + 1) * 128] = v
-                    stacked_ref[c, 128:256, p * 128 : (p + 1) * 128] = turned(v)
+                    stacked_ref[c, 128:256, p * 128 : (p + 1) * 128] = quarter(v)
 
             @pl.when(jnp.logical_not(live))
             def _():
@@ -50,10 +61,10 @@
     out_ref[...] = rows_ref[...].astype(jnp.bfloat16)
 
 
-def radiate(place, currents, aggregate):
+def radiate(counts, currents, aggregate):
     children, directions, width = aggregate.shape
     positions = currents.shape[0] // children
-    tile = 144
+    tile = 576
     return pl.pallas_call(
         radiate_kernel,
         grid_spec=pltpu.PrefetchScalarGridSpec(
@@ -72,7 +83,7 @@
         out_shape=jax.ShapeDtypeStruct((directions * positions, 128), jnp.bfloat16),
         compiler_params=pltpu.CompilerParams(vmem_limit_bytes=32 * MIB),
         name="radiate",
-    )(place, currents, aggregate)
+    )(counts, currents, aggregate)
 
 
 def pair_rows(per_group, positions):
@@ -102,7 +113,7 @@
             rows_ref[g * chunk : (g + 1) * chunk, :],
             preferred_element_type=jnp.float32,
         ).astype(jnp.bfloat16)
-        other = turned(picked)
+        other = quarter(picked)
         b = g // per_block
         start = (g % per_block) * step
         for r in range(per_group):
@@ -158,69 +169,69 @@
     )
 
 
-def near_kernel(source_ref, left_ref, own_ref, right_ref, blocks_ref, out_ref, window_ref):
+def near_kernel(source_ref, across_ref, own_ref, partner_ref, blocks_ref, out_ref, window_ref):
     slots = own_ref.shape[0]
     unknowns = own_ref.shape[1]
-    terms = blocks_ref.shape[1]
-    leaf = pl.program_id(0)
-
-    @pl.when(leaf == 0)
+    leaves, terms = blocks_ref.shape[:2]
+    first = pl.program_id(0) * leaves
+
+    @pl.when(first == 0)
     def _():
-        for part, ref in enumerate((left_ref, own_ref, right_ref)):
+        for part, ref in enumerate((across_ref, own_ref, partner_ref)):
 
             def fill(i, carry, part=part, ref=ref):
-                v = ref[i]
-                window_ref[part * slots + i, 0:unknowns, :] = v
-                window_ref[part * slots + i, unknowns : 2 * unknowns, :] = turned(v)
+                for j in range(4):
+                    v = ref[i * 4 + j]
+                    row = part * slots + i * 4 + j
+                    window_ref[row, 0:unknowns, :] = v
+                    window_ref[row, unknowns : 2 * unknowns, :] = quarter(v)
                 return carry
 
-            lax.fori_loop(0, slots, fill, 0)
-
-    total = jnp.dot(
-        blocks_ref[0, 0], window_ref[source_ref[leaf * terms]], preferred_element_type=jnp.float32
-    )
-    for e in range(1, terms):
-        total += jnp.dot(
-            blocks_ref[0, e],
-            window_ref[source_ref[leaf * terms + e]],
+            lax.fori_loop(0, slots // 4, fill, 0)
+
+    for i in range(leaves):
+        sources = [source_ref[(first + i) * terms + e] for e in range(terms)]
+        out_ref[i] = jnp.dot(
+            jnp.concatenate([blocks_ref[i, e] for e in range(terms)], axis=1),
+            jnp.concatenate([window_ref[source] for source in sources], axis=0),
             preferred_element_type=jnp.float32,
         )
-    out_ref[0] = total
-
-
-def near(source, left, own, right, blocks):
+
+
+def near(source, across, own, partner, blocks):
     slots, unknowns, channels = own.shape
     _, terms, _, doubled = blocks.shape
+    leaves = 4
     whole = pl.BlockSpec(own.shape, lambda i, _: (0, 0, 0))
     return pl.pallas_call(
         near_kernel,
         grid_spec=pltpu.PrefetchScalarGridSpec(
             num_scalar_prefetch=1,
-            grid=(slots,),
+            grid=(slots // leaves,),
             in_specs=[
                 whole,
                 whole,
                 whole,
-                pl.BlockSpec((1, terms, unknowns, doubled), lambda i, _: (i, 0, 0, 0)),
-            ],
-            out_specs=pl.BlockSpec((1, unknowns, channels), lambda i, _: (i, 0, 0)),
+                pl.BlockSpec((leaves, terms, unknowns, doubled), lambda i, _: (i, 0, 0, 0)),
+            ],
+            out_specs=pl.BlockSpec((leaves, unknowns, channels), lambda i, _: (i, 0, 0)),
             scratch_shapes=[pltpu.VMEM((3 * slots, doubled, channels), jnp.bfloat16)],
         ),
         out_shape=jax.ShapeDtypeStruct((slots, unknowns, channels), jnp.float32),
         compiler_params=pltpu.CompilerParams(vmem_limit_bytes=40 * MIB),
+        cost_estimate=pl.CostEstimate(flops=10**10, transcendentals=0, bytes_accessed=2 * 10**7),
         name="near",
-    )(source.reshape(-1), left, own, right, blocks)
-
-
-def receive_kernel(place_ref, rows_ref, receive_ref, near_ref, out_ref, wide_ref, doubled_ref):
+    )(source.reshape(-1), across, own, partner, blocks)
+
+
+def receive_kernel(counts_ref, rows_ref, receive_ref, near_ref, out_ref, wide_ref, doubled_ref):
     octants = receive_ref.shape[0]
     unknowns = receive_ref.shape[1]
     directions = receive_ref.shape[2] // 2
     positions = doubled_ref.shape[1] // 128
     children = 8
     step = pl.program_id(0)
-    offset = place_ref[0]
-    count = place_ref[1]
+    offset, count = own_range(counts_ref)
 
     @pl.when(step == 0)
     def _():
@@ -228,7 +239,7 @@
         for p in range(positions):
             v = wide_ref[pl.ds(p, directions, stride=positions), :].astype(jnp.bfloat16)
             doubled_ref[0:directions, p * 128 : (p + 1) * 128] = v
-            doubled_ref[directions : 2 * directions, p * 128 : (p + 1) * 128] = turned(v)
+            doubled_ref[directions : 2 * directions, p * 128 : (p + 1) * 128] = quarter(v)
         out_ref[...] = jnp.zeros(out_ref.shape, out_ref.dtype)
 
     lines = receive_ref[...].reshape(octants * unknowns, 2 * directions)
@@ -244,11 +255,11 @@
                 out_ref[leaf] = (part + near_ref[leaf]).astype(jnp.bfloat16)
 
 
-def absorb(place, rows, receive, near_field):
+def absorb(counts, rows, receive, near_field):
     children, unknowns, doubled = receive.shape
     slots = near_field.shape[0]
     positions = slots // children
-    octants = 2
+    octants = 4
     return pl.pallas_call(
         receive_kernel,
         grid_spec=pltpu.PrefetchScalarGridSpec(
@@ -268,7 +279,7 @@
         out_shape=jax.ShapeDtypeStruct(near_field.shape, jnp.bfloat16),
         compiler_params=pltpu.CompilerParams(vmem_limit_bytes=40 * MIB),
         name="absorb",
-    )(place, rows, receive, near_field)
+    )(counts, rows, receive, near_field)
 
 
 def in_hbm(array):
@@ -284,29 +295,26 @@
 def body(
     currents, counts, near_source, near_blocks, aggregate, receive, translations, source_blocks
 ):
+    slots = currents.shape[0]
+    positions = slots // aggregate.shape[0]
     device = lax.axis_index(AXES)
-    slots, unknowns, channels = currents.shape
-    positions = slots // aggregate.shape[0]
-    own_count = counts[device]
-    offset = jnp.where(device % 2 == 1, counts[device - device % 2], 0)
-    place = jnp.stack([offset, own_count]).astype(jnp.int32)
-
-    patterns = radiate(place, in_hbm(currents), in_hbm(aggregate))
+    local = near_source - (device - 1) * slots
+    mirrored = local + 2 * slots - 2 * slots * (local // slots)
+    local = jnp.where(device % 2 == 1, mirrored, local)
+    count = lax.axis_size("near")
+    inner = [(i, i + 1) for i in range(1, count - 1, 2)]
+    outer = [(i, i + 1) for i in range(0, count, 2)]
+    across = lax.ppermute(currents, "near", inner + [(j, i) for i, j in inner])
+    partner = lax.ppermute(currents, "near", outer + [(j, i) for i, j in outer])
+
+    patterns = radiate(counts, in_hbm(currents), in_hbm(aggregate))
     gathered = swap(patterns, positions)
-
-    later, _ = lax.optimization_barrier((currents, patterns))
-    count = lax.axis_size("near")
-    left = lax.ppermute(later, "near", [(i, i + 1) for i in range(count - 1)])
-    right = lax.ppermute(later, "near", [(i + 1, i) for i in range(count - 1)])
-    gathered, left, right = lax.optimization_barrier((gathered, left, right))
-
     incoming = translate(source_blocks, gathered, translations, positions)
     returned = swap(incoming, positions)
 
-    local = near_source - (device - 1) * slots
     local, _ = lax.optimization_barrier((local, incoming))
-    near_field = near(local, left, in_hbm(currents), right, in_hbm(near_blocks))
-    return absorb(place, returned, in_hbm(receive), near_field)
+    near_field = near(local, across, in_hbm(currents), partner, in_hbm(near_blocks))
+    return absorb(counts, returned, in_hbm(receive), near_field)
 
 
 def solution(mesh):

time: 118 us -> 82.3 us (0.70)
  Pallas kernels: 51 us -> 30.7 us
  starting transfers between devices: 27.3 us -> 19.8 us
  local copies, waits for them, and re-layouts: 5.97 us -> 0.87 us
    ppermute x2, waiting for transfers between devices: 31.2 us -> 6.98 us  [the longest x1 6.98 us: body(): partner = lax.ppermute(currents, 'near', outer + [(j, i) for i, j in outer])]
    all_to_all x2, waiting for transfers between devices: 0.01 us -> 23.7 us  [swap(): return lax.all_to_all(shaped, AXES, 0, 0, tiled=True).reshape(-1, channels)]
    pallas_call x1, Pallas kernels: 30.3 us -> 12.9 us  [near(): pl.pallas_call(near_kernel, grid_spec=pltpu.PrefetchScalarGridSpec(num_sc...]
    all_to_all x2, starting transfers between devices: 21.9 us -> 15.2 us  [swap(): return lax.all_to_all(shaped, AXES, 0, 0, tiled=True).reshape(-1, channels)]
    unnamed x18 -> x14, local copies, waits for them, and re-layouts: 4.4 us -> 0.68 us
    pallas_call x1, Pallas kernels: 9.04 us -> 6.78 us  [radiate(): pl.pallas_call(radiate_kernel, grid_spec=pltpu.PrefetchScalarGridSpec(num...]
    dynamic_slice x1 -> x0, local copies, waits for them, and re-layouts: 1.38 us -> none  [body(): offset = jnp.where(device % 2 == 1, counts[device - device % 2], 0)]
  transfers between devices with their start and end apart: 4 -> 4, of which waited for: 1 -> 3; matrix products, arithmetic and copies ran while one was open for 0% -> 0% of each run, Pallas kernels for 26% -> 21%
where the time goes in v2:
time: 82.3 us; the launch traced here: 82.1 us
  Pallas kernels  30.7 us (37%)
  waiting for transfers between devices  30.7 us (37%)
  starting transfers between devices  19.8 us (24%)
  local copies, waits for them, and re-layouts  0.87 us (1%)
    all_to_all x2, waiting for transfers between devices, swap(): return lax.all_to_all(shaped, AXES, 0, 0, tiled=True).reshape(-1, channels)  23.7 us
    all_to_all x2, starting transfers between devices, swap(): return lax.all_to_all(shaped, AXES, 0, 0, tiled=True).reshape(-1, channels)  15.2 us
    pallas_call x1, Pallas kernels, near(): pl.pallas_call(near_kernel, grid_spec=pltpu.PrefetchScalarGridSpec(num_sc...  12.9 us
    ppermute x1, waiting for transfers between devices, body(): partner = lax.ppermute(currents, 'near', outer + [(j, i) for i, j in outer])  6.98 us
    pallas_call x1, Pallas kernels, absorb(): pl.pallas_call(receive_kernel, grid_spec=pltpu.PrefetchScalarGridSpec(num...  6.91 us
    pallas_call x1, Pallas kernels, radiate(): pl.pallas_call(radiate_kernel, grid_spec=pltpu.PrefetchScalarGridSpec(num...  6.78 us
    pallas_call x1, Pallas kernels, translate(): pl.pallas_call(translate_kernel, in_specs=[pl.BlockSpec(memory_space=pltp...  4.11 us
    ppermute x1, starting transfers between devices, body(): partner = lax.ppermute(currents, 'near', outer + [(j, i) for i, j in outer])  2.92 us
  transfers between devices with their start and end apart: 4, of which 3 were waited for; matrix products, arithmetic and copies ran while one was open for 0% of the time, Pallas kernels for 21%

profile of v2, /device:TPU:1, one launch (start us, length us, event | category | flops | bytes accessed | tf_op | source)
XLA Modules:
  0.0 82.1 jit_solution(3396907431045190648)
XLA Ops:
  0.0 0.0 copy-start.4
  0.0 0.7 copy-done.4
  0.7 6.8 %radiate.1 = bf16[4608,128]{1,0:T(8,128)(2,1)} custom-call(s32[128]{0:T(128)S(1)} %copy-done.4, bf16[32,128,128]{2,1,0:T(8,128)(2,1)} %own_ref.1, bf16[8,1152,256]{2,1,0:T(8,128)(2,1)} %aggregate_ref.1), custom_call_target="tpu_custom_call" | custom-call | tf_op jit(solution)/shard_map/radiate/pallas_call | solution.py:68
  7.4 0.0 copy-start
  7.4 0.0 copy-start.1
  7.4 0.0 copy-start.2
  7.4 0.0 copy-start.3
  7.5 11.5 %all-to-all-start = ((bf16[1152,4,128]{2,1,0:T(4,128)(2,1)}), bf16[1152,4,128]{2,1,0:T(4,128)(2,1)S(1)}, u32[]{:S(2)}, u32[]{:S(2)}) async-start(bf16[1152,4,128]{2,1,0:T(4,128)(2,1)} %bitcast), calls=%async_computation | async-start | bytes 2359296 | tf_op jit(solution)/shard_map/all_to_all | solution.py:292
  19.0 1.6 %collective-permute-start = (bf16[32,128,128]{2,1,0:T(8,128)(2,1)}, bf16[32,128,128]{2,1,0:T(8,128)(2,1)}, u32[]{:S(2)}, u32[]{:S(2)}) collective-permute-start(bf16[32,128,128]{2,1,0:T(8,128)(2,1)} %own_ref.1), channel_id=1, source_target_pairs={{1,2},{2,1},{5,6},{6,5},{9,10},{10,9},{13,14},{14,13},{17,18},{18,... | collective-permute-start | bytes 3145736 | tf_op jit(solution)/shard_map/ppermute | solution.py:307
  20.6 2.9 %collective-permute-start.1 = (bf16[32,128,128]{2,1,0:T(8,128)(2,1)}, bf16[32,128,128]{2,1,0:T(8,128)(2,1)}, u32[]{:S(2)}, u32[]{:S(2)}) collective-permute-start(bf16[32,128,128]{2,1,0:T(8,128)(2,1)} %own_ref.1), channel_id=1, source_target_pairs={{0,1},{2,3},{1,0},{3,2},{4,5},{6,7},{5,4},{7,6},{8,9},{10,11},{9,8... | collective-permute-start | bytes 3145736 | tf_op jit(solution)/shard_map/ppermute | solution.py:308
  23.5 17.1 %all-to-all-done = bf16[1152,4,128]{2,1,0:T(4,128)(2,1)S(1)} async-done(((bf16[1152,4,128]{2,1,0:T(4,128)(2,1)}), bf16[1152,4,128]{2,1,0:T(4,128)(2,1)S(1)}, u32[]{:S(2)}, u32[]{:S(2)}) %all-to-all-start) | async-done | bytes 1179680 | tf_op jit(solution)/shard_map/all_to_all | solution.py:292
  40.6 0.0 copy-done
  40.6 0.0 copy-done.1
  40.6 0.0 copy-done.2
  40.6 0.0 copy-done.3
  40.6 4.1 %translate.1 = bf16[4608,128]{1,0:T(8,128)(2,1)} custom-call(s32[4,3]{1,0:T(4,128)S(1)} %copy-done.3, bf16[4608,128]{1,0:T(8,128)(2,1)S(1)} %bitcast.5, bf16[4,3,9,64,128]{4,3,2,1,0:T(8,128)(2,1)S(1)} %copy-done, bf16[144,288]{1,0:T(8,128)(2,1)S(1)} %copy-done.2, bf16[288,144]{1,0:T(8,128)(2,1)S(1)} %copy-done.1), custom_call_target="tpu_custom_call" | custom-call | tf_op jit(solution)/shard_map/translate/pallas_call | solution.py:152
  44.7 0.0 copy-start.6
  44.7 3.7 %all-to-all-start.1 = ((bf16[1152,4,128]{2,1,0:T(4,128)(2,1)}), bf16[1152,4,128]{2,1,0:T(4,128)(2,1)S(1)}, u32[]{:S(2)}, u32[]{:S(2)}) async-start(bf16[1152,4,128]{2,1,0:T(4,128)(2,1)} %bitcast.2), calls=%async_computation.1 | async-start | bytes 2359296 | tf_op jit(solution)/shard_map/all_to_all | solution.py:292
  48.4 0.0 copy-done.6
  48.5 0.1 copy.11
  48.6 0.1 reshape.19.source_ref
  48.7 0.0 copy-start.5
  48.7 0.0 collective-permute-done.across_ref
  48.7 7.0 %collective-permute-done.1.partner_ref = bf16[32,128,128]{2,1,0:T(8,128)(2,1)} collective-permute-done((bf16[32,128,128]{2,1,0:T(8,128)(2,1)}, bf16[32,128,128]{2,1,0:T(8,128)(2,1)}, u32[]{:S(2)}, u32[]{:S(2)}) %collective-permute-start.1) | collective-permute-done | bytes 1048608 | tf_op jit(solution)/shard_map/ppermute | solution.py:308
  55.7 12.9 %near.1.near_ref = f32[32,128,128]{2,1,0:T(8,128)S(1)} custom-call(s32[192]{0:T(256)S(1)} %reshape.19.source_ref, bf16[32,128,128]{2,1,0:T(8,128)(2,1)} %collective-permute-done.across_ref, bf16[32,128,128]{2,1,0:T(8,128)(2,1)} %own_ref.1, bf16[32,128,128]{2,1,0:T(8,128)(2,1)} %collective-permute-done.1.partner_ref, bf16[32,6,128,256]{3,2,1,0:T(8,128)(2,1)} %blocks_ref.3), custom_call_target="tpu_custom_call" | custom-call | flops 10000000000 | bytes 20000000 | tf_op jit(solution)/shard_map/near/pallas_call | solution.py:206
  68.5 6.7 %all-to-all-done.1 = bf16[1152,4,128]{2,1,0:T(4,128)(2,1)S(1)} async-done(((bf16[1152,4,128]{2,1,0:T(4,128)(2,1)}), bf16[1152,4,128]{2,1,0:T(4,128)(2,1)S(1)}, u32[]{:S(2)}, u32[]{:S(2)}) %all-to-all-start.1) | async-done | bytes 1179680 | tf_op jit(solution)/shard_map/all_to_all | solution.py:292
  75.2 0.0 copy-done.5
  75.2 6.9 %absorb.1 = bf16[32,128,128]{2,1,0:T(8,128)(2,1)} custom-call(s32[128]{0:T(128)S(1)} %copy-done.5, bf16[4608,128]{1,0:T(8,128)(2,1)S(1)} %bitcast.4, bf16[8,128,2304]{2,1,0:T(8,128)(2,1)} %receive_ref.1, f32[32,128,128]{2,1,0:T(8,128)S(1)} %near.1.near_ref), custom_call_target="tpu_custom_call" | custom-call | tf_op jit(solution)/shard_map/absorb/pallas_call | solution.py:263
  (1 shorter events, 0.0 us)
Async XLA Ops:
  0.0 0.7 copy-start.4
  7.4 33.2 %copy-start = (bf16[4,3,9,64,128]{4,3,2,1,0:T(8,128)(2,1)S(1)}, bf16[4,3,9,64,128]{4,3,2,1,0:T(8,128)(2,1)}, u32[]{:S(2)}) copy-start(bf16[4,3,9,64,128]{4,3,2,1,0:T(8,128)(2,1)} %translations_ref.1) | copy-start | bytes 5308420
  7.4 33.2 %copy-start.1 = (bf16[288,144]{1,0:T(8,128)(2,1)S(1)}, bf16[288,144]{1,0:T(8,128)(2,1)}, u32[]{:S(2)}) copy-start(bf16[288,144]{1,0:T(8,128)(2,1)} %constant.48.clone.spread_ref) | copy-start | bytes 248836
  7.4 33.2 %copy-start.2 = (bf16[144,288]{1,0:T(8,128)(2,1)S(1)}, bf16[144,288]{1,0:T(8,128)(2,1)}, u32[]{:S(2)}) copy-start(bf16[144,288]{1,0:T(8,128)(2,1)} %constant.47.clone.select_ref) | copy-start | bytes 248836
  7.4 33.2 %copy-start.3 = (s32[4,3]{1,0:T(4,128)S(1)}, s32[4,3]{1,0:T(4,128)}, u32[]{:S(2)}) copy-start(s32[4,3]{1,0:T(4,128)} %blocks_ref.2) | copy-start | bytes 148
  7.5 33.1 %all-to-all-start = ((bf16[1152,4,128]{2,1,0:T(4,128)(2,1)}), bf16[1152,4,128]{2,1,0:T(4,128)(2,1)S(1)}, u32[]{:S(2)}, u32[]{:S(2)}) async-start(bf16[1152,4,128]{2,1,0:T(4,128)(2,1)} %bitcast), calls=%async_computation | async-start | bytes 2359296 | tf_op jit(solution)/shard_map/all_to_all | solution.py:292
  19.0 29.7 %collective-permute-start = (bf16[32,128,128]{2,1,0:T(8,128)(2,1)}, bf16[32,128,128]{2,1,0:T(8,128)(2,1)}, u32[]{:S(2)}, u32[]{:S(2)}) collective-permute-start(bf16[32,128,128]{2,1,0:T(8,128)(2,1)} %own_ref.1), channel_id=1, source_target_pairs={{1,2},{2,1},{5,6},{6,5},{9,10},{10,9},{13,14},{14,13},{17,18},{18,... | collective-permute-start | bytes 3145736 | tf_op jit(solution)/shard_map/ppermute | solution.py:307
  20.6 35.1 %collective-permute-start.1 = (bf16[32,128,128]{2,1,0:T(8,128)(2,1)}, bf16[32,128,128]{2,1,0:T(8,128)(2,1)}, u32[]{:S(2)}, u32[]{:S(2)}) collective-permute-start(bf16[32,128,128]{2,1,0:T(8,128)(2,1)} %own_ref.1), channel_id=1, source_target_pairs={{0,1},{2,3},{1,0},{3,2},{4,5},{6,7},{5,4},{7,6},{8,9},{10,11},{9,8... | collective-permute-start | bytes 3145736 | tf_op jit(solution)/shard_map/ppermute | solution.py:308
  44.7 3.7 %copy-start.6 = (s32[32,6]{0,1:T(8,128)S(1)}, s32[32,6]{0,1:T(8,128)}, u32[]{:S(2)}) copy-start(s32[32,6]{0,1:T(8,128)} %param.12) | copy-start | bytes 2308
  44.7 30.5 %all-to-all-start.1 = ((bf16[1152,4,128]{2,1,0:T(4,128)(2,1)}), bf16[1152,4,128]{2,1,0:T(4,128)(2,1)S(1)}, u32[]{:S(2)}, u32[]{:S(2)}) async-start(bf16[1152,4,128]{2,1,0:T(4,128)(2,1)} %bitcast.2), calls=%async_computation.1 | async-start | bytes 2359296 | tf_op jit(solution)/shard_map/all_to_all | solution.py:292
  48.7 26.6 %copy-start.5 = (s32[128]{0:T(128)S(1)}, s32[128]{0:T(128)}, u32[]{:S(2)}) copy-start(s32[128]{0:T(128)} %counts_ref.3) | copy-start | bytes 1540

commit v3 on v2

--- a/solution.py
+++ b/solution.py
@@ -169,113 +169,133 @@
     )
 
 
-def near_kernel(source_ref, across_ref, own_ref, partner_ref, blocks_ref, out_ref, window_ref):
-    slots = own_ref.shape[0]
-    unknowns = own_ref.shape[1]
+def widen_kernel(across_ref, own_ref, partner_ref, out_ref):
+    slots, unknowns, _ = own_ref.shape
+    for part, ref in enumerate((across_ref, own_ref, partner_ref)):
+
+        def fill(i, carry, part=part, ref=ref):
+            for j in range(4):
+                v = ref[i * 4 + j]
+                row = part * slots + i * 4 + j
+                out_ref[row, 0:unknowns, :] = v
+                out_ref[row, unknowns : 2 * unknowns, :] = quarter(v)
+            return carry
+
+        lax.fori_loop(0, slots // 4, fill, 0)
+
+
+def widen(across, own, partner):
+    slots, unknowns, channels = own.shape
+    vmem = pl.BlockSpec(memory_space=pltpu.VMEM)
+    return pl.pallas_call(
+        widen_kernel,
+        in_specs=[vmem, vmem, vmem],
+        out_specs=vmem,
+        out_shape=pltpu.VMEM((3 * slots, 2 * unknowns, channels), own.dtype),
+        compiler_params=pltpu.CompilerParams(vmem_limit_bytes=40 * MIB),
+        cost_estimate=pl.CostEstimate(flops=5 * 10**10, transcendentals=0, bytes_accessed=10**7),
+        name="widen",
+    )(across, own, partner)
+
+
+def near_kernel(source_ref, window_ref, blocks_ref, receive_hbm, out_ref, receive_ref, sem):
     leaves, terms = blocks_ref.shape[:2]
-    first = pl.program_id(0) * leaves
-
-    @pl.when(first == 0)
+    step = pl.program_id(0)
+    fetch = pltpu.make_async_copy(receive_hbm, receive_ref, sem)
+
+    @pl.when(step == 0)
     def _():
-        for part, ref in enumerate((across_ref, own_ref, partner_ref)):
-
-            def fill(i, carry, part=part, ref=ref):
-                for j in range(4):
-                    v = ref[i * 4 + j]
-                    row = part * slots + i * 4 + j
-                    window_ref[row, 0:unknowns, :] = v
-                    window_ref[row, unknowns : 2 * unknowns, :] = quarter(v)
-                return carry
-
-            lax.fori_loop(0, slots // 4, fill, 0)
+        fetch.start()
 
     for i in range(leaves):
-        sources = [source_ref[(first + i) * terms + e] for e in range(terms)]
+        first = (step * leaves + i) * terms
+        sources = [source_ref[first + e] for e in range(terms)]
         out_ref[i] = jnp.dot(
             jnp.concatenate([blocks_ref[i, e] for e in range(terms)], axis=1),
             jnp.concatenate([window_ref[source] for source in sources], axis=0),
             preferred_element_type=jnp.float32,
         )
 
-
-def near(source, across, own, partner, blocks):
-    slots, unknowns, channels = own.shape
-    _, terms, _, doubled = blocks.shape
+    @pl.when(step == pl.num_programs(0) - 1)
+    def _():
+        fetch.wait()
+
+
+def near(source, window, blocks, receive):
+    slots, terms, unknowns, doubled = blocks.shape
+    channels = window.shape[-1]
     leaves = 4
-    whole = pl.BlockSpec(own.shape, lambda i, _: (0, 0, 0))
     return pl.pallas_call(
         near_kernel,
         grid_spec=pltpu.PrefetchScalarGridSpec(
             num_scalar_prefetch=1,
             grid=(slots // leaves,),
             in_specs=[
-                whole,
-                whole,
-                whole,
+                pl.BlockSpec(memory_space=pltpu.VMEM),
                 pl.BlockSpec((leaves, terms, unknowns, doubled), lambda i, _: (i, 0, 0, 0)),
+                pl.BlockSpec(memory_space=pltpu.HBM),
             ],
-            out_specs=pl.BlockSpec((leaves, unknowns, channels), lambda i, _: (i, 0, 0)),
-            scratch_shapes=[pltpu.VMEM((3 * slots, doubled, channels), jnp.bfloat16)],
+            out_specs=[
+                pl.BlockSpec((leaves, unknowns, channels), lambda i, _: (i, 0, 0)),
+                pl.BlockSpec(memory_space=pltpu.VMEM),
+            ],
+            scratch_shapes=[pltpu.SemaphoreType.DMA],
         ),
-        out_shape=jax.ShapeDtypeStruct((slots, unknowns, channels), jnp.float32),
+        out_shape=[
+            jax.ShapeDtypeStruct((slots, unknowns, channels), jnp.float32),
+            pltpu.VMEM(receive.shape, receive.dtype),
+        ],
         compiler_params=pltpu.CompilerParams(vmem_limit_bytes=40 * MIB),
         cost_estimate=pl.CostEstimate(flops=10**10, transcendentals=0, bytes_accessed=2 * 10**7),
         name="near",
-    )(source.reshape(-1), across, own, partner, blocks)
-
-
-def receive_kernel(counts_ref, rows_ref, receive_ref, near_ref, out_ref, wide_ref, doubled_ref):
-    octants = receive_ref.shape[0]
-    unknowns = receive_ref.shape[1]
-    directions = receive_ref.shape[2] // 2
+    )(source.reshape(-1), window, blocks, receive)
+
+
+def absorb_kernel(counts_ref, rows_ref, receive_ref, near_ref, out_ref, wide_ref, doubled_ref):
+    children, unknowns, doubled = receive_ref.shape
+    directions = doubled // 2
     positions = doubled_ref.shape[1] // 128
-    children = 8
-    step = pl.program_id(0)
+    octants = 2
     offset, count = own_range(counts_ref)
-
-    @pl.when(step == 0)
-    def _():
-        wide_ref[...] = rows_ref[...].astype(jnp.float32)
+    wide_ref[...] = rows_ref[...].astype(jnp.float32)
+    for p in range(positions):
+        v = wide_ref[pl.ds(p, directions, stride=positions), :].astype(jnp.bfloat16)
+        doubled_ref[0:directions, p * 128 : (p + 1) * 128] = v
+        doubled_ref[directions:doubled, p * 128 : (p + 1) * 128] = quarter(v)
+    for q in range(0, children, octants):
+        lines = receive_ref[q : q + octants].reshape(octants * unknowns, doubled)
+        far = jnp.dot(lines, doubled_ref[...], preferred_element_type=jnp.float32)
         for p in range(positions):
-            v = wide_ref[pl.ds(p, directions, stride=positions), :].astype(jnp.bfloat16)
-            doubled_ref[0:directions, p * 128 : (p + 1) * 128] = v
-            doubled_ref[directions : 2 * directions, p * 128 : (p + 1) * 128] = quarter(v)
-        out_ref[...] = jnp.zeros(out_ref.shape, out_ref.dtype)
-
-    lines = receive_ref[...].reshape(octants * unknowns, 2 * directions)
-    far = jnp.dot(lines, doubled_ref[...], preferred_element_type=jnp.float32)
-    for p in range(positions):
-        slot = p - offset
-
-        @pl.when(jnp.logical_and(slot >= 0, slot < count))
+            slot = p - offset
+
+            @pl.when(jnp.logical_and(slot >= 0, slot < count))
+            def _():
+                for c in range(octants):
+                    leaf = slot * children + q + c
+                    part = far[c * unknowns : (c + 1) * unknowns, p * 128 : (p + 1) * 128]
+                    out_ref[leaf] = (part + near_ref[leaf]).astype(jnp.bfloat16)
+
+    for slot in range(positions):
+
+        @pl.when(slot >= count)
         def _():
-            for c in range(octants):
-                leaf = slot * children + step * octants + c
-                part = far[c * unknowns : (c + 1) * unknowns, p * 128 : (p + 1) * 128]
-                out_ref[leaf] = (part + near_ref[leaf]).astype(jnp.bfloat16)
+            out_ref[slot * children : (slot + 1) * children] = jnp.zeros(
+                (children, unknowns, 128), jnp.bfloat16
+            )
 
 
 def absorb(counts, rows, receive, near_field):
-    children, unknowns, doubled = receive.shape
-    slots = near_field.shape[0]
-    positions = slots // children
-    octants = 4
-    return pl.pallas_call(
-        receive_kernel,
-        grid_spec=pltpu.PrefetchScalarGridSpec(
-            num_scalar_prefetch=1,
-            grid=(children // octants,),
-            in_specs=[
-                pl.BlockSpec(rows.shape, lambda i, _: (0, 0)),
-                pl.BlockSpec((octants, unknowns, doubled), lambda i, _: (i, 0, 0)),
-                pl.BlockSpec(near_field.shape, lambda i, _: (0, 0, 0)),
-            ],
-            out_specs=pl.BlockSpec(near_field.shape, lambda i, _: (0, 0, 0)),
-            scratch_shapes=[
-                pltpu.VMEM(rows.shape, jnp.float32),
-                pltpu.VMEM((doubled, positions * 128), jnp.bfloat16),
-            ],
-        ),
+    _, _, doubled = receive.shape
+    positions = near_field.shape[0] // receive.shape[0]
+    vmem = pl.BlockSpec(memory_space=pltpu.VMEM)
+    return pl.pallas_call(
+        absorb_kernel,
+        in_specs=[pl.BlockSpec(memory_space=pltpu.SMEM), vmem, vmem, vmem],
+        out_specs=vmem,
+        scratch_shapes=[
+            pltpu.VMEM(rows.shape, jnp.float32),
+            pltpu.VMEM((doubled, positions * 128), jnp.bfloat16),
+        ],
         out_shape=jax.ShapeDtypeStruct(near_field.shape, jnp.bfloat16),
         compiler_params=pltpu.CompilerParams(vmem_limit_bytes=40 * MIB),
         name="absorb",
@@ -307,14 +327,16 @@
     across = lax.ppermute(currents, "near", inner + [(j, i) for i, j in inner])
     partner = lax.ppermute(currents, "near", outer + [(j, i) for i, j in outer])
 
-    patterns = radiate(counts, in_hbm(currents), in_hbm(aggregate))
+    patterns = radiate(in_hbm(counts), in_hbm(currents), in_hbm(aggregate))
     gathered = swap(patterns, positions)
+    window = widen(across, currents, partner)
+    gathered, window = lax.optimization_barrier((gathered, window))
     incoming = translate(source_blocks, gathered, translations, positions)
     returned = swap(incoming, positions)
 
     local, _ = lax.optimization_barrier((local, incoming))
-    near_field = near(local, across, in_hbm(currents), partner, in_hbm(near_blocks))
-    return absorb(counts, returned, in_hbm(receive), near_field)
+    near_field, held = near(local, window, in_hbm(near_blocks), in_hbm(receive))
+    return absorb(counts, returned, held, near_field)
 
 
 def solution(mesh):

time: 82.3 us -> 86.1 us (1.046)
  local copies, waits for them, and re-layouts: 0.87 us -> 11.3 us
  waiting for transfers between devices: 30.7 us -> 24.5 us
    unnamed x14 -> x22, local copies, waits for them, and re-layouts: 0.68 us -> 11.1 us
    all_to_all x2, waiting for transfers between devices: 23.7 us -> 18 us  [swap(): return lax.all_to_all(shaped, AXES, 0, 0, tiled=True).reshape(-1, channels)]
    pallas_call x1, Pallas kernels: 12.9 us -> 10.5 us  [near(): pl.pallas_call(near_kernel, grid_spec=pltpu.PrefetchScalarGridSpec(num_sc...]
    pallas_call x1 -> x2, Pallas kernels: 6.91 us -> 9.17 us  [the longest x1 5.12 us: absorb(): pl.pallas_call(absorb_kernel, in_specs=[pl.BlockSpec(memory_space=pltpu.S...]
    all_to_all x2, starting transfers between devices: 15.2 us -> 14.1 us  [swap(): return lax.all_to_all(shaped, AXES, 0, 0, tiled=True).reshape(-1, channels)]
  transfers between devices with their start and end apart: 4 -> 4, of which waited for: 3 -> 3; matrix products, arithmetic and copies ran while one was open for 0% -> 0% of each run, Pallas kernels for 21% -> 25%
where the time goes in v3:
time: 86.1 us; the launch traced here: 85.7 us
  Pallas kernels  30.4 us (35%)
  waiting for transfers between devices  24.5 us (28%)
  starting transfers between devices  19.3 us (22%)
  local copies, waits for them, and re-layouts  11.3 us (13%)
    all_to_all x2, waiting for transfers between devices, swap(): return lax.all_to_all(shaped, AXES, 0, 0, tiled=True).reshape(-1, channels)  18 us
    all_to_all x2, starting transfers between devices, swap(): return lax.all_to_all(shaped, AXES, 0, 0, tiled=True).reshape(-1, channels)  14.1 us
    unnamed x22, local copies, waits for them, and re-layouts  11.1 us
    pallas_call x1, Pallas kernels, near(): pl.pallas_call(near_kernel, grid_spec=pltpu.PrefetchScalarGridSpec(num_sc...  10.5 us
    pallas_call x1, Pallas kernels, radiate(): pl.pallas_call(radiate_kernel, grid_spec=pltpu.PrefetchScalarGridSpec(num...  6.63 us
    ppermute x1, waiting for transfers between devices, body(): partner = lax.ppermute(currents, 'near', outer + [(j, i) for i, j in outer])  6.51 us
    pallas_call x1, Pallas kernels, absorb(): pl.pallas_call(absorb_kernel, in_specs=[pl.BlockSpec(memory_space=pltpu.S...  5.12 us
    pallas_call x1, Pallas kernels, translate(): pl.pallas_call(translate_kernel, in_specs=[pl.BlockSpec(memory_space=pltp...  4.11 us
  transfers between devices with their start and end apart: 4, of which 3 were waited for; matrix products, arithmetic and copies ran while one was open for 0% of the time, Pallas kernels for 25%

profile of v3, /device:TPU:1, one launch (start us, length us, event | category | flops | bytes accessed | tf_op | source)
XLA Modules:
  0.0 85.7 jit_solution(6285760400391616659)
XLA Ops:
  0.0 1.6 %collective-permute-start = (bf16[32,128,128]{2,1,0:T(8,128)(2,1)}, bf16[32,128,128]{2,1,0:T(8,128)(2,1)}, u32[]{:S(2)}, u32[]{:S(2)}) collective-permute-start(bf16[32,128,128]{2,1,0:T(8,128)(2,1)} %own_ref.1), channel_id=1, source_target_pairs={{1,2},{2,1},{5,6},{6,5},{9,10},{10,9},{13,14},{14,13},{17,18},{18,... | collective-permute-start | bytes 3145736 | tf_op jit(solution)/shard_map/ppermute | solution.py:327
  1.6 3.6 %collective-permute-start.1 = (bf16[32,128,128]{2,1,0:T(8,128)(2,1)}, bf16[32,128,128]{2,1,0:T(8,128)(2,1)}, u32[]{:S(2)}, u32[]{:S(2)}) collective-permute-start(bf16[32,128,128]{2,1,0:T(8,128)(2,1)} %own_ref.1), channel_id=1, source_target_pairs={{0,1},{2,3},{1,0},{3,2},{4,5},{6,7},{5,4},{7,6},{8,9},{10,11},{9,8... | collective-permute-start | bytes 3145736 | tf_op jit(solution)/shard_map/ppermute | solution.py:328
  5.2 6.6 %radiate.1 = bf16[4608,128]{1,0:T(8,128)(2,1)} custom-call(s32[128]{0:T(128)} %counts_ref.3, bf16[32,128,128]{2,1,0:T(8,128)(2,1)} %own_ref.1, bf16[8,1152,256]{2,1,0:T(8,128)(2,1)} %aggregate_ref.1), custom_call_target="tpu_custom_call" | custom-call | tf_op jit(solution)/shard_map/radiate/pallas_call | solution.py:68
  11.9 0.0 copy-start.4
  11.9 0.0 copy-start.5
  11.9 0.0 copy-start.6
  11.9 9.7 %all-to-all-start = ((bf16[1152,4,128]{2,1,0:T(4,128)(2,1)}), bf16[1152,4,128]{2,1,0:T(4,128)(2,1)S(1)}, u32[]{:S(2)}, u32[]{:S(2)}) async-start(bf16[1152,4,128]{2,1,0:T(4,128)(2,1)} %bitcast), calls=%async_computation | async-start | bytes 2359296 | tf_op jit(solution)/shard_map/all_to_all | solution.py:312
  21.6 0.0 copy-start.2
  21.6 0.0 collective-permute-done.across_ref
  21.6 6.5 %collective-permute-done.1.partner_ref = bf16[32,128,128]{2,1,0:T(8,128)(2,1)} collective-permute-done((bf16[32,128,128]{2,1,0:T(8,128)(2,1)}, bf16[32,128,128]{2,1,0:T(8,128)(2,1)}, u32[]{:S(2)}, u32[]{:S(2)}) %collective-permute-start.1) | collective-permute-done | bytes 1048608 | tf_op jit(solution)/shard_map/ppermute | solution.py:328
  28.1 0.0 copy-start.3
  28.1 1.2 %copy-done.3 = bf16[32,128,128]{2,1,0:T(8,128)(2,1)S(1)} copy-done((bf16[32,128,128]{2,1,0:T(8,128)(2,1)S(1)}, bf16[32,128,128]{2,1,0:T(8,128)(2,1)}, u32[]{:S(2)}) %copy-start.3) | copy-done | bytes 1048600
  29.4 4.0 %widen.1.window_ref = bf16[96,256,128]{2,1,0:T(8,128)(2,1)S(1)} custom-call(bf16[32,128,128]{2,1,0:T(8,128)(2,1)} %collective-permute-done.across_ref, bf16[32,128,128]{2,1,0:T(8,128)(2,1)S(1)} %copy-done.3, bf16[32,128,128]{2,1,0:T(8,128)(2,1)} %collective-permute-done.1.partner_ref), custom_call_target="tpu_custom_call" | custom-call | flops 49999998976 | bytes 10000000 | tf_op jit(solution)/shard_map/widen/pallas_call | solution.py:190
  33.4 0.0 copy-start.8
  33.4 2.7 %copy-done.8 = bf16[96,256,128]{2,1,0:T(8,128)(2,1)} copy-done((bf16[96,256,128]{2,1,0:T(8,128)(2,1)}, bf16[96,256,128]{2,1,0:T(8,128)(2,1)S(1)}, u32[]{:S(2)}) %copy-start.8) | copy-done | bytes 6291480
  36.1 12.4 %all-to-all-done = bf16[1152,4,128]{2,1,0:T(4,128)(2,1)S(1)} async-done(((bf16[1152,4,128]{2,1,0:T(4,128)(2,1)}), bf16[1152,4,128]{2,1,0:T(4,128)(2,1)S(1)}, u32[]{:S(2)}, u32[]{:S(2)}) %all-to-all-start) | async-done | bytes 1179680 | tf_op jit(solution)/shard_map/all_to_all | solution.py:312
  48.5 0.0 copy-done.4
  48.5 0.0 copy-done.5
  48.5 0.0 copy-done.6
  48.5 0.0 copy-done.2
  48.5 4.1 %translate.1 = bf16[4608,128]{1,0:T(8,128)(2,1)} custom-call(s32[4,3]{1,0:T(4,128)S(1)} %copy-done.6, bf16[4608,128]{1,0:T(8,128)(2,1)S(1)} %bitcast.5, bf16[4,3,9,64,128]{4,3,2,1,0:T(8,128)(2,1)S(1)} %copy-done.2, bf16[144,288]{1,0:T(8,128)(2,1)S(1)} %copy-done.5, bf16[288,144]{1,0:T(8,128)(2,1)S(1)} %copy-done.4), custom_call_target="tpu_custom_call" | custom-call | tf_op jit(solution)/shard_map/translate/pallas_call | solution.py:152
  52.6 0.0 copy-start.10
  52.6 4.4 %all-to-all-start.1 = ((bf16[1152,4,128]{2,1,0:T(4,128)(2,1)}), bf16[1152,4,128]{2,1,0:T(4,128)(2,1)S(1)}, u32[]{:S(2)}, u32[]{:S(2)}) async-start(bf16[1152,4,128]{2,1,0:T(4,128)(2,1)} %bitcast.2), calls=%async_computation.1 | async-start | bytes 2359296 | tf_op jit(solution)/shard_map/all_to_all | solution.py:312
  57.1 0.0 copy-done.10
  57.1 0.1 copy.11
  57.2 0.1 reshape.19.source_ref
  57.3 0.0 copy-start.9
  57.3 2.8 %copy-done.9 = bf16[96,256,128]{2,1,0:T(8,128)(2,1)S(1)} copy-done((bf16[96,256,128]{2,1,0:T(8,128)(2,1)S(1)}, bf16[96,256,128]{2,1,0:T(8,128)(2,1)}, u32[]{:S(2)}) %copy-start.9) | copy-done | bytes 6291480
  60.1 0.0 copy-start.7
  60.1 10.5 %near.1 = (f32[32,128,128]{2,1,0:T(8,128)S(1)}, bf16[8,128,2304]{2,1,0:T(8,128)(2,1)S(1)}) custom-call(s32[192]{0:T(256)S(1)} %reshape.19.source_ref, bf16[96,256,128]{2,1,0:T(8,128)(2,1)S(1)} %copy-done.9, bf16[32,6,128,256]{3,2,1,0:T(8,128)(2,1)} %blocks_ref.3, bf16[8,128,2304]{2,1,0:T(8,128)(2,1)} %receive_hbm.1), custom_call_target="tpu_custom_call" | custom-call | flops 10000000000 | bytes 20000000 | tf_op jit(solution)/shard_map/near/pallas_call | solution.py:228
  70.6 0.0 copy-start
  70.6 2.1 %copy-done = bf16[8,128,2304]{2,1,0:T(8,128)(2,1)} copy-done((bf16[8,128,2304]{2,1,0:T(8,128)(2,1)}, bf16[8,128,2304]{2,1,0:T(8,128)(2,1)S(1)}, u32[]{:S(2)}) %copy-start) | copy-done | bytes 4718616
  72.7 5.5 %all-to-all-done.1 = bf16[1152,4,128]{2,1,0:T(4,128)(2,1)S(1)} async-done(((bf16[1152,4,128]{2,1,0:T(4,128)(2,1)}), bf16[1152,4,128]{2,1,0:T(4,128)(2,1)S(1)}, u32[]{:S(2)}, u32[]{:S(2)}) %all-to-all-start.1) | async-done | bytes 1179680 | tf_op jit(solution)/shard_map/all_to_all | solution.py:312
  78.2 0.0 copy-done.7
  78.2 0.0 copy-start.1
  78.2 2.3 %copy-done.1 = bf16[8,128,2304]{2,1,0:T(8,128)(2,1)S(1)} copy-done((bf16[8,128,2304]{2,1,0:T(8,128)(2,1)S(1)}, bf16[8,128,2304]{2,1,0:T(8,128)(2,1)}, u32[]{:S(2)}) %copy-start.1) | copy-done | bytes 4718616
  80.6 5.1 %absorb.1 = bf16[32,128,128]{2,1,0:T(8,128)(2,1)} custom-call(s32[128]{0:T(128)S(1)} %copy-done.7, bf16[4608,128]{1,0:T(8,128)(2,1)S(1)} %bitcast.4, bf16[8,128,2304]{2,1,0:T(8,128)(2,1)S(1)} %copy-done.1, f32[32,128,128]{2,1,0:T(8,128)S(1)} %get-tuple-element.14.near_ref), custom_call_target="tpu_custom_call" | custom-call | tf_op jit(solution)/shard_map/absorb/pallas_call | solution.py:291
  (1 shorter events, 0.0 us)
Async XLA Ops:
  0.0 21.6 %collective-permute-start = (bf16[32,128,128]{2,1,0:T(8,128)(2,1)}, bf16[32,128,128]{2,1,0:T(8,128)(2,1)}, u32[]{:S(2)}, u32[]{:S(2)}) collective-permute-start(bf16[32,128,128]{2,1,0:T(8,128)(2,1)} %own_ref.1), channel_id=1, source_target_pairs={{1,2},{2,1},{5,6},{6,5},{9,10},{10,9},{13,14},{14,13},{17,18},{18,... | collective-permute-start | bytes 3145736 | tf_op jit(solution)/shard_map/ppermute | solution.py:327
  1.6 26.5 %collective-permute-start.1 = (bf16[32,128,128]{2,1,0:T(8,128)(2,1)}, bf16[32,128,128]{2,1,0:T(8,128)(2,1)}, u32[]{:S(2)}, u32[]{:S(2)}) collective-permute-start(bf16[32,128,128]{2,1,0:T(8,128)(2,1)} %own_ref.1), channel_id=1, source_target_pairs={{0,1},{2,3},{1,0},{3,2},{4,5},{6,7},{5,4},{7,6},{8,9},{10,11},{9,8... | collective-permute-start | bytes 3145736 | tf_op jit(solution)/shard_map/ppermute | solution.py:328
  11.9 36.6 %copy-start.4 = (bf16[288,144]{1,0:T(8,128)(2,1)S(1)}, bf16[288,144]{1,0:T(8,128)(2,1)}, u32[]{:S(2)}) copy-start(bf16[288,144]{1,0:T(8,128)(2,1)} %constant.48.clone.spread_ref) | copy-start | bytes 248836
  11.9 36.6 %copy-start.5 = (bf16[144,288]{1,0:T(8,128)(2,1)S(1)}, bf16[144,288]{1,0:T(8,128)(2,1)}, u32[]{:S(2)}) copy-start(bf16[144,288]{1,0:T(8,128)(2,1)} %constant.47.clone.select_ref) | copy-start | bytes 248836
  11.9 36.6 %copy-start.6 = (s32[4,3]{1,0:T(4,128)S(1)}, s32[4,3]{1,0:T(4,128)}, u32[]{:S(2)}) copy-start(s32[4,3]{1,0:T(4,128)} %blocks_ref.2) | copy-start | bytes 148
  11.9 36.6 %all-to-all-start = ((bf16[1152,4,128]{2,1,0:T(4,128)(2,1)}), bf16[1152,4,128]{2,1,0:T(4,128)(2,1)S(1)}, u32[]{:S(2)}, u32[]{:S(2)}) async-start(bf16[1152,4,128]{2,1,0:T(4,128)(2,1)} %bitcast), calls=%async_computation | async-start | bytes 2359296 | tf_op jit(solution)/shard_map/all_to_all | solution.py:312
  21.6 26.9 %copy-start.2 = (bf16[4,3,9,64,128]{4,3,2,1,0:T(8,128)(2,1)S(1)}, bf16[4,3,9,64,128]{4,3,2,1,0:T(8,128)(2,1)}, u32[]{:S(2)}) copy-start(bf16[4,3,9,64,128]{4,3,2,1,0:T(8,128)(2,1)} %translations_ref.1) | copy-start | bytes 5308420
  28.1 1.2 %copy-start.3 = (bf16[32,128,128]{2,1,0:T(8,128)(2,1)S(1)}, bf16[32,128,128]{2,1,0:T(8,128)(2,1)}, u32[]{:S(2)}) copy-start(bf16[32,128,128]{2,1,0:T(8,128)(2,1)} %own_ref.1) | copy-start | bytes 3145732
  33.4 2.7 %copy-start.8 = (bf16[96,256,128]{2,1,0:T(8,128)(2,1)}, bf16[96,256,128]{2,1,0:T(8,128)(2,1)S(1)}, u32[]{:S(2)}) copy-start(bf16[96,256,128]{2,1,0:T(8,128)(2,1)S(1)} %widen.1.window_ref) | copy-start | bytes 18874372
  52.6 4.4 %copy-start.10 = (s32[32,6]{0,1:T(8,128)S(1)}, s32[32,6]{0,1:T(8,128)}, u32[]{:S(2)}) copy-start(s32[32,6]{0,1:T(8,128)} %param.12) | copy-start | bytes 2308
  52.6 25.6 %all-to-all-start.1 = ((bf16[1152,4,128]{2,1,0:T(4,128)(2,1)}), bf16[1152,4,128]{2,1,0:T(4,128)(2,1)S(1)}, u32[]{:S(2)}, u32[]{:S(2)}) async-start(bf16[1152,4,128]{2,1,0:T(4,128)(2,1)} %bitcast.2), calls=%async_computation.1 | async-start | bytes 2359296 | tf_op jit(solution)/shard_map/all_to_all | solution.py:312
  57.3 2.8 %copy-start.9 = (bf16[96,256,128]{2,1,0:T(8,128)(2,1)S(1)}, bf16[96,256,128]{2,1,0:T(8,128)(2,1)}, u32[]{:S(2)}) copy-start(bf16[96,256,128]{2,1,0:T(8,128)(2,1)} %copy-done.8) | copy-start | bytes 18874372
  60.1 18.1 %copy-start.7 = (s32[128]{0:T(128)S(1)}, s32[128]{0:T(128)}, u32[]{:S(2)}) copy-start(s32[128]{0:T(128)} %counts_ref.3) | copy-start | bytes 1540
  70.6 2.1 %copy-start = (bf16[8,128,2304]{2,1,0:T(8,128)(2,1)}, bf16[8,128,2304]{2,1,0:T(8,128)(2,1)S(1)}, u32[]{:S(2)}) copy-start(bf16[8,128,2304]{2,1,0:T(8,128)(2,1)S(1)} %get-tuple-element.13.receive_ref) | copy-start | bytes 14155780
  78.2 2.3 %copy-start.1 = (bf16[8,128,2304]{2,1,0:T(8,128)(2,1)S(1)}, bf16[8,128,2304]{2,1,0:T(8,128)(2,1)}, u32[]{:S(2)}) copy-start(bf16[8,128,2304]{2,1,0:T(8,128)(2,1)} %copy-done) | copy-start | bytes 14155780

commit v4 on v3

v4 whole, which is shorter than its diff:
```python
import numpy as np
import jax
import jax.numpy as jnp
from jax import lax
from jax.experimental import pallas as pl
from jax.experimental.pallas import tpu as pltpu
from jax.sharding import PartitionSpec as P

AXES = ("dir", "near")
MIB = 1 << 20


def quarter(v):
    lane = lax.broadcasted_iota(jnp.int32, (1, v.shape[-1]), 1)
    sign = jnp.where(lane < v.shape[-1] // 2, -1.0, 1.0).astype(v.dtype)
    return pltpu.roll(v, v.shape[-1] // 2, 1) * sign


def device_index():
    return lax.axis_index("dir") * lax.axis_size("near") + lax.axis_index("near")


def own_range(counts_ref):
    device = device_index()
    odd = device % 2
    return odd * counts_ref[device - odd], counts_ref[device]


def radiate_kernel(
    counts_ref, own_ref, moved_ref, aggregate_ref, out_hbm, stacked_ref, rows_ref, out_ref, sems
):
    children, directions, width = aggregate_ref.shape
    unknowns = width // 2
    share = stacked_ref.shape[1] // 128
    tiles = sems.shape[0]
    tile = directions // tiles
    device = device_index()
    odd = device % 2
    first = counts_ref[device - odd]
    for q in range(share):
        parent = share * odd + q
        lanes = slice(q * 128, (q + 1) * 128)
        mine = jnp.where(odd == 1, parent >= first, parent < first)
        slot = jnp.where(odd == 1, jnp.maximum(parent - first, 0), parent)
        arrived = jnp.where(odd == 1, q, jnp.clip(q - first, 0, share - 1))

        def place(ref, row, lanes=lanes):
            for c in range(children):
                v = ref[row * children + c]
                stacked_ref[c * width : c * width + unknowns, lanes] = v
                stacked_ref[c * width + unknowns : (c + 1) * width, lanes] = quarter(v)

        @pl.when(mine)
        def _():
            place(own_ref, slot)

        @pl.when(jnp.logical_not(mine))
        def _():
            place(moved_ref, arrived)

    stores = []
    for i in range(tiles):
        rows = slice(i * tile, (i + 1) * tile)
        total = jnp.dot(
            jnp.concatenate([aggregate_ref[c, rows, :] for c in range(children)], axis=1),
            stacked_ref[...],
            preferred_element_type=jnp.float32,
        )
        for q in range(share):
            rows_ref[pl.ds(q, tile, stride=share), :] = total[:, q * 128 : (q + 1) * 128]
        span = slice(i * tile * share, (i + 1) * tile * share)
        out_ref[span, :] = rows_ref[...].astype(jnp.bfloat16)
        store = pltpu.make_async_copy(out_ref.at[span], out_hbm.at[span], sems.at[i])
        store.start()
        stores.append(store)
    for store in stores:
        store.wait()


def radiate(counts, own, moved, aggregate):
    children, directions, width = aggregate.shape
    share = moved.shape[0] // children
    tiles = 4
    vmem = pl.BlockSpec(memory_space=pltpu.VMEM)
    return pl.pallas_call(
        radiate_kernel,
        in_specs=[pl.BlockSpec(memory_space=pltpu.SMEM), vmem, vmem, vmem],
        out_specs=pl.BlockSpec(memory_space=pltpu.HBM),
        scratch_shapes=[
            pltpu.VMEM((children * width, share * 128), jnp.bfloat16),
            pltpu.VMEM((directions // tiles * share, 128), jnp.float32),
            pltpu.VMEM((directions * share, 128), jnp.bfloat16),
            pltpu.SemaphoreType.DMA((tiles,)),
        ],
        out_shape=jax.ShapeDtypeStruct((directions * share, 128), jnp.bfloat16),
        compiler_params=pltpu.CompilerParams(vmem_limit_bytes=40 * MIB),
        name="radiate",
    )(counts, own, moved, aggregate)


def pair_rows(per_group, positions, copies):
    pairs = 4
    share = positions // (2 // copies)
    select = np.zeros((per_group * pairs * positions, 2 * pairs * per_group * share))
    for r in range(per_group):
        for pair in range(pairs):
            for p in range(positions):
                row = (r * pairs + pair) * positions + p
                for side in range(2) if copies == 2 else (p // share,):
                    column = ((2 * pair + side) * per_group + r) * share + p % share
                    select[row, column] = 1.0
    return select


def translate_kernel(
    blocks_ref, rows_ref, translations_ref, select_ref, spread_ref, out_hbm, values_ref, sums_ref,
    out_ref, sems,
):
    block_count, list_length, per_group = translations_ref.shape[:3]
    block = translations_ref.shape[3]
    chunk = select_ref.shape[1]
    wide = spread_ref.shape[0]
    groups = rows_ref.shape[0] // chunk
    per_block = groups // block_count
    step = block // per_block
    for g in range(groups):
        picked = jnp.dot(
            select_ref[...],
            rows_ref[g * chunk : (g + 1) * chunk, :],
            preferred_element_type=jnp.float32,
        ).astype(jnp.bfloat16)
        other = quarter(picked)
        b = g // per_block
        start = (g % per_block) * step
        for r in range(per_group):
            part = slice(r * step, (r + 1) * step)
            values_ref[b, r, start : start + step, :] = picked[part]
            values_ref[b, r, block + start : block + start + step, :] = other[part]
    stores = []
    for t in range(block_count):
        sources = [blocks_ref[t, e] for e in range(list_length)]
        for r in range(per_group):
            total = jnp.dot(
                jnp.concatenate([translations_ref[t, e, r] for e in range(list_length)], axis=1),
                jnp.concatenate([values_ref[source, r] for source in sources], axis=0),
                preferred_element_type=jnp.float32,
            )
            total = total.astype(jnp.bfloat16)
            for q in range(per_block):
                sums_ref[t * per_block + q, r * step : (r + 1) * step, :] = total[
                    q * step : (q + 1) * step
                ]
        for g in range(t * per_block, (t + 1) * per_block):
            out_ref[g * wide : (g + 1) * wide, :] = jnp.dot(
                spread_ref[...], sums_ref[g], preferred_element_type=jnp.float32
            ).astype(jnp.bfloat16)
        span = slice(t * per_block * wide, (t + 1) * per_block * wide)
        store = pltpu.make_async_copy(out_ref.at[span], out_hbm.at[span], sems.at[t])
        store.start()
        stores.append(store)
    for store in stores:
        store.wait()


def translate(source_blocks, rows, translations, positions):
    block_count, _, per_group, block, doubled = translations.shape
    select = pair_rows(per_group, positions, 1)
    spread = pair_rows(per_group, positions, 2).T
    groups = rows.shape[0] // select.shape[1]
    vmem = pl.BlockSpec(memory_space=pltpu.VMEM)
    return pl.pallas_call(
        translate_kernel,
        in_specs=[pl.BlockSpec(memory_space=pltpu.SMEM), vmem, vmem, vmem, vmem],
        out_specs=pl.BlockSpec(memory_space=pltpu.HBM),
        scratch_shapes=[
            pltpu.VMEM((block_count, per_group, doubled, 128), jnp.bfloat16),
            pltpu.VMEM((groups, select.shape[0], 128), jnp.bfloat16),
            pltpu.VMEM((groups * spread.shape[0], 128), jnp.bfloat16),
            pltpu.SemaphoreType.DMA((block_count,)),
        ],
        out_shape=jax.ShapeDtypeStruct((groups * spread.shape[0], 128), jnp.bfloat16),
        compiler_params=pltpu.CompilerParams(vmem_limit_bytes=32 * MIB),
        name="translate",
    )(
        source_blocks,
        rows,
        translations,
        jnp.asarray(select, jnp.bfloat16),
        jnp.asarray(spread, jnp.bfloat16),
    )


def widen_kernel(across_ref, own_ref, moved_ref, rest_ref, out_ref):
    unknowns = own_ref.shape[1]
    start = 0
    for ref in (across_ref, own_ref, moved_ref, rest_ref):

        def fill(i, carry, start=start, ref=ref):
            for j in range(4):
                v = ref[i * 4 + j]
                row = start + i * 4 + j
                out_ref[row, 0:unknowns, :] = v
                out_ref[row, unknowns : 2 * unknowns, :] = quarter(v)
            return carry

        lax.fori_loop(0, ref.shape[0] // 4, fill, 0)
        start += ref.shape[0]


def widen(across, own, moved, rest):
    slots, unknowns, channels = own.shape
    vmem = pl.BlockSpec(memory_space=pltpu.VMEM)
    return pl.pallas_call(
        widen_kernel,
        in_specs=[vmem] * 4,
        out_specs=vmem,
        out_shape=jax.ShapeDtypeStruct((3 * slots, 2 * unknowns, channels), own.dtype),
        compiler_params=pltpu.CompilerParams(vmem_limit_bytes=40 * MIB),
        cost_estimate=pl.CostEstimate(flops=5 * 10**10, transcendentals=0, bytes_accessed=10**7),
        name="widen",
    )(across, own, moved, rest)


def near_kernel(source_ref, window_ref, blocks_ref, out_ref):
    leaves, terms = blocks_ref.shape[:2]
    step = pl.program_id(0)
    for i in range(leaves):
        first = (step * leaves + i) * terms
        sources = [source_ref[first + e] for e in range(terms)]
        out_ref[i] = jnp.dot(
            jnp.concatenate([blocks_ref[i, e] for e in range(terms)], axis=1),
            jnp.concatenate([window_ref[source] for source in sources], axis=0),
            preferred_element_type=jnp.float32,
        )


def near(source, window, blocks):
    slots, terms, unknowns, doubled = blocks.shape
    channels = window.shape[-1]
    leaves = 4
    return pl.pallas_call(
        near_kernel,
        grid_spec=pltpu.PrefetchScalarGridSpec(
            num_scalar_prefetch=1,
            grid=(slots // leaves,),
            in_specs=[
                pl.BlockSpec(memory_space=pltpu.VMEM),
                pl.BlockSpec((leaves, terms, unknowns, doubled), lambda i, _: (i, 0, 0, 0)),
            ],
            out_specs=pl.BlockSpec((leaves, unknowns, channels), lambda i, _: (i, 0, 0)),
        ),
        out_shape=jax.ShapeDtypeStruct((slots, unknowns, channels), jnp.float32),
        compiler_params=pltpu.CompilerParams(vmem_limit_bytes=40 * MIB),
        cost_estimate=pl.CostEstimate(flops=10**10, transcendentals=0, bytes_accessed=2 * 10**7),
        name="near",
    )(source.reshape(-1), window, blocks)


def absorb_kernel(
    counts_ref, rows_ref, near_ref, receive_hbm, out_hbm, wide_ref, doubled_ref, receive_ref,
    fields_ref, fetch_sems, store_sems,
):
    children, unknowns, doubled = receive_ref.shape
    directions = doubled // 2
    positions = doubled_ref.shape[1] // 128
    steps = fetch_sems.shape[0]
    octants = children // steps
    parts = []
    for q in range(steps):
        span = slice(q * octants, (q + 1) * octants)
        part = pltpu.make_async_copy(receive_hbm.at[span], receive_ref.at[span], fetch_sems.at[q])
        part.start()
        parts.append(part)
    offset, count = own_range(counts_ref)
    for slot in range(positions):

        @pl.when(slot >= count)
        def _():
            fields_ref[slot * children : (slot + 1) * children] = jnp.zeros(
                (children, unknowns, 128), jnp.bfloat16
            )

    wide_ref[...] = rows_ref[...].astype(jnp.float32)
    for p in range(positions):
        v = wide_ref[pl.ds(p, directions, stride=positions), :].astype(jnp.bfloat16)
        doubled_ref[0:directions, p * 128 : (p + 1) * 128] = v
        doubled_ref[directions:doubled, p * 128 : (p + 1) * 128] = quarter(v)
    stores = []
    for q in range(steps):
        parts[q].wait()
        lines = receive_ref[q * octants : (q + 1) * octants].reshape(octants * unknowns, doubled)
        far = jnp.dot(lines, doubled_ref[...], preferred_element_type=jnp.float32)
        for p in range(positions):
            slot = p - offset

            @pl.when(jnp.logical_and(slot >= 0, slot < count))
            def _():
                for c in range(octants):
                    leaf = slot * children + q * octants + c
                    part = far[c * unknowns : (c + 1) * unknowns, p * 128 : (p + 1) * 128]
                    fields_ref[leaf] = (part + near_ref[leaf]).astype(jnp.bfloat16)

        for slot in range(positions):
            span = pl.ds(slot * children + q * octants, octants)
            store = pltpu.make_async_copy(
                fields_ref.at[span], out_hbm.at[span], store_sems.at[q, slot]
            )
            store.start()
            stores.append(store)
    for store in stores:
        store.wait()


def absorb(counts, rows, receive, near_field):
    children, _, doubled = receive.shape
    positions = near_field.shape[0] // children
    steps = 4
    vmem = pl.BlockSpec(memory_space=pltpu.VMEM)
    hbm = pl.BlockSpec(memory_space=pltpu.HBM)
    return pl.pallas_call(
        absorb_kernel,
        in_specs=[pl.BlockSpec(memory_space=pltpu.SMEM), vmem, vmem, hbm],
        out_specs=hbm,
        scratch_shapes=[
            pltpu.VMEM(rows.shape, jnp.float32),
            pltpu.VMEM((doubled, positions * 128), jnp.bfloat16),
            pltpu.VMEM(receive.shape, receive.dtype),
            pltpu.VMEM(near_field.shape, jnp.bfloat16),
            pltpu.SemaphoreType.DMA((steps,)),
            pltpu.SemaphoreType.DMA((steps, positions)),
        ],
        out_shape=jax.ShapeDtypeStruct(near_field.shape, jnp.bfloat16),
        compiler_params=pltpu.CompilerParams(vmem_limit_bytes=48 * MIB),
        name="absorb",
    )(counts, rows, near_field, receive)


def in_hbm(array):
    return pltpu.with_memory_space_constraint(array, pltpu.HBM)


def swap(rows, share):
    channels = rows.shape[-1]
    shaped = rows.reshape(-1, share, channels)
    return lax.all_to_all(shaped, AXES, 0, 0, tiled=True).reshape(-1, channels)


def body(
    currents, counts, near_source, near_blocks, aggregate, receive, translations, source_blocks
):
    slots = currents.shape[0]
    half = slots // 2
    positions = slots // aggregate.shape[0]
    device = lax.axis_index(AXES)
    odd = device % 2
    count = lax.axis_size("near")
    inner = [(i, i + 1) for i in range(1, count - 1, 2)]
    outer = [(i, i + 1) for i in range(0, count, 2)]
    inner += [(j, i) for i, j in inner]
    outer += [(j, i) for i, j in outer]
    excess = lax.dynamic_slice_in_dim(currents, (1 - odd) * half, half, 0)
    kept = lax.dynamic_slice_in_dim(currents, odd * half, half, 0)
    moved = lax.ppermute(excess, "near", outer)
    across = lax.ppermute(currents, "near", inner)
    rest = lax.ppermute(kept, "near", outer)

    patterns = radiate(in_hbm(counts), currents, moved, aggregate)
    gathered = swap(patterns, positions // 2)
    window = widen(across, currents, moved, rest)
    gathered, window = lax.optimization_barrier((gathered, window))
    incoming = translate(source_blocks, gathered, translations, positions)
    returned = swap(incoming, positions)

    local = near_source - (device - 1) * slots
    side, slot = local // slots, local % slots
    flipped = jnp.where(side == 0, 2 * slots + (slot + half) % slots, (2 - side) * slots + slot)
    local = jnp.where(odd == 1, flipped, local)
    local, _ = lax.optimization_barrier((local, incoming))
    near_field = near(local, window, in_hbm(near_blocks))
    return absorb(in_hbm(counts), returned, in_hbm(receive), near_field)


def solution(mesh):
    spread = P(AXES, None, None)
    return jax.shard_map(
        body,
        mesh=mesh,
        in_specs=(
            spread,
            P(),
            P(AXES, None),
            P(AXES, None, None, None),
            P(),
            P(),
            P(None, None, AXES, None, None),
            P(),
        ),
        out_specs=spread,
        check_vma=False,
    )
```

time: 86.1 us -> 89.7 us (1.042)
  Pallas kernels: 30.4 us -> 26.3 us
  local copies, waits for them, and re-layouts: 11.3 us -> 14.1 us
  waiting for transfers between devices: 24.5 us -> 26.6 us
  starting transfers between devices: 19.3 us -> 21.2 us
    ppermute x2 -> x3, waiting for transfers between devices: 6.51 us -> 11.3 us  [the longest x1 11.3 us: body(): moved = lax.ppermute(excess, 'near', outer)]
    pallas_call x2, Pallas kernels: 10.7 us -> 7.09 us  [the longest x1 3.87 us: widen(): pl.pallas_call(widen_kernel, in_specs=[vmem] * 4, out_specs=vmem, out_sha...]
    all_to_all x2, waiting for transfers between devices: 18 us -> 15.3 us  [swap(): return lax.all_to_all(shaped, AXES, 0, 0, tiled=True).reshape(-1, channels)]
    dynamic_slice x0 -> x1, local copies, waits for them, and re-layouts: none -> 2.22 us  [body(): kept = lax.dynamic_slice_in_dim(currents, odd * half, half, 0)]
    all_to_all x2, starting transfers between devices: 14.1 us -> 16 us  [swap(): return lax.all_to_all(shaped, AXES, 0, 0, tiled=True).reshape(-1, channels)]
    pallas_call x1, Pallas kernels: 10.5 us -> 9.4 us  [near(): pl.pallas_call(near_kernel, grid_spec=pltpu.PrefetchScalarGridSpec(num_sc...]
    ppermute x2 -> x3, starting transfers between devices: 5.24 us -> 5.23 us  [the longest x1 3.56 us: body(): moved = lax.ppermute(excess, 'near', outer)]
  transfers between devices with their start and end apart: 4 -> 5, of which waited for: 3 -> 3; matrix products, arithmetic and copies ran while one was open for 0% -> 3% of each run, Pallas kernels for 25% -> 18%
where the time goes in v4:
time: 89.7 us; the launch traced here: 89.1 us
  waiting for transfers between devices  26.6 us (30%)
  Pallas kernels  26.3 us (29%)
  starting transfers between devices  21.2 us (24%)
  local copies, waits for them, and re-layouts  14.1 us (16%)
    all_to_all x2, starting transfers between devices, swap(): return lax.all_to_all(shaped, AXES, 0, 0, tiled=True).reshape(-1, channels)  16 us
    all_to_all x2, waiting for transfers between devices, swap(): return lax.all_to_all(shaped, AXES, 0, 0, tiled=True).reshape(-1, channels)  15.3 us
    unnamed x22, local copies, waits for them, and re-layouts  11.7 us
    ppermute x1, waiting for transfers between devices, body(): moved = lax.ppermute(excess, 'near', outer)  11.3 us
    pallas_call x1, Pallas kernels, near(): pl.pallas_call(near_kernel, grid_spec=pltpu.PrefetchScalarGridSpec(num_sc...  9.4 us
    pallas_call x1, Pallas kernels, absorb(): pl.pallas_call(absorb_kernel, in_specs=[pl.BlockSpec(memory_space=pltpu.S...  6.01 us
    pallas_call x1, Pallas kernels, widen(): pl.pallas_call(widen_kernel, in_specs=[vmem] * 4, out_specs=vmem, out_sha...  3.87 us
    pallas_call x1, Pallas kernels, translate(): pl.pallas_call(translate_kernel, in_specs=[pl.BlockSpec(memory_space=pltp...  3.78 us
  transfers between devices with their start and end apart: 5, of which 3 were waited for; matrix products, arithmetic and copies ran while one was open for 3% of the time, Pallas kernels for 18%

profile of v4, /device:TPU:1, one launch (start us, length us, event | category | flops | bytes accessed | tf_op | source)
XLA Modules:
  0.0 89.1 jit_solution(1434783098167644981)
XLA Ops:
  0.0 1.6 %collective-permute-start.1 = (bf16[32,128,128]{2,1,0:T(8,128)(2,1)}, bf16[32,128,128]{2,1,0:T(8,128)(2,1)}, u32[]{:S(2)}, u32[]{:S(2)}) collective-permute-start(bf16[32,128,128]{2,1,0:T(8,128)(2,1)} %own_ref.3), channel_id=1, source_target_pairs={{1,2},{2,1},{5,6},{6,5},{9,10},{10,9},{13,14},{14,13},{17,18},{18,... | collective-permute-start | bytes 3145736 | tf_op jit(solution)/shard_map/ppermute | solution.py:364
  1.6 0.0 copy-start.2
  1.6 2.2 %constant_dynamic-slice_fusion = (bf16[16,128,128]{2,1,0:T(8,128)(2,1)}, bf16[16,128,128]{2,1,0:T(8,128)(2,1)S(1)}) fusion(bf16[32,128,128]{2,1,0:T(8,128)(2,1)} %own_ref.3, s32[]{:T(128)S(6)} %select_n.41, s32[]{:T(128)S(6)} %select_n.40), kind=kLoop, calls=%fused_computation.15 | loop fusion | bytes 2097160 | tf_op jit(solution)/shard_map/dynamic_slice | solution.py:362
  3.9 3.6 %collective-permute-start = (bf16[16,128,128]{2,1,0:T(8,128)(2,1)S(1)}, bf16[16,128,128]{2,1,0:T(8,128)(2,1)S(1)}, u32[]{:S(2)}, u32[]{:S(2)}) collective-permute-start(bf16[16,128,128]{2,1,0:T(8,128)(2,1)S(1)} %get-tuple-element.12), channel_id=1, source_target_pairs={{0,1},{2,3},{1,0},{3,2},{4,5},{6,7},{5,4},{7,6},{8,9},{10,11},{9,8... | collective-permute-start | bytes 1572872 | tf_op jit(solution)/shard_map/ppermute | solution.py:363
  7.4 0.0 collective-permute-start.2
  7.4 11.3 %collective-permute-done.moved_ref = bf16[16,128,128]{2,1,0:T(8,128)(2,1)S(1)} collective-permute-done((bf16[16,128,128]{2,1,0:T(8,128)(2,1)S(1)}, bf16[16,128,128]{2,1,0:T(8,128)(2,1)S(1)}, u32[]{:S(2)}, u32[]{:S(2)}) %collective-permute-start) | collective-permute-done | bytes 524320 | tf_op jit(solution)/shard_map/ppermute | solution.py:363
  18.7 0.0 copy-start
  18.7 2.3 %copy-done = bf16[8,1152,256]{2,1,0:T(8,128)(2,1)S(1)} copy-done((bf16[8,1152,256]{2,1,0:T(8,128)(2,1)S(1)}, bf16[8,1152,256]{2,1,0:T(8,128)(2,1)}, u32[]{:S(2)}) %copy-start) | copy-done | bytes 4718616
  21.1 0.0 copy-start.1
  21.1 1.2 %copy-done.1 = bf16[32,128,128]{2,1,0:T(8,128)(2,1)S(1)} copy-done((bf16[32,128,128]{2,1,0:T(8,128)(2,1)S(1)}, bf16[32,128,128]{2,1,0:T(8,128)(2,1)}, u32[]{:S(2)}) %copy-start.1) | copy-done | bytes 1048600
  22.3 0.0 copy-start.4
  22.3 3.2 %radiate.1 = bf16[2304,128]{1,0:T(8,128)(2,1)} custom-call(s32[128]{0:T(128)} %counts_ref.3, bf16[32,128,128]{2,1,0:T(8,128)(2,1)S(1)} %copy-done.1, bf16[16,128,128]{2,1,0:T(8,128)(2,1)S(1)} %collective-permute-done.moved_ref, bf16[8,1152,256]{2,1,0:T(8,128)(2,1)S(1)} %copy-done), custom_call_target="tpu_custom_call" | custom-call | tf_op jit(solution)/shard_map/radiate/pallas_call | solution.py:85
  25.5 0.0 copy-done.4
  25.5 0.0 copy-start.6
  25.6 12.3 %all-to-all-start = ((bf16[1152,2,128]{2,1,0:T(2,128)(2,1)}), bf16[1152,2,128]{2,1,0:T(2,128)(2,1)S(1)}, u32[]{:S(2)}, u32[]{:S(2)}) async-start(bf16[1152,2,128]{2,1,0:T(2,128)(2,1)} %bitcast), calls=%async_computation | async-start | bytes 1179648 | tf_op jit(solution)/shard_map/all_to_all | solution.py:345
  37.9 0.0 copy-start.3
  37.9 0.0 collective-permute-done.2.rest_ref
  37.9 0.0 collective-permute-done.1.across_ref
  37.9 0.0 copy-done.2
  37.9 0.0 copy-start.5
  37.9 1.2 %copy-done.5 = bf16[16,128,128]{2,1,0:T(8,128)(2,1)S(1)} copy-done((bf16[16,128,128]{2,1,0:T(8,128)(2,1)S(1)}, bf16[16,128,128]{2,1,0:T(8,128)(2,1)}, u32[]{:S(2)}) %copy-start.5) | copy-done | bytes 524312
  39.1 3.9 %widen.1.window_ref = bf16[96,256,128]{2,1,0:T(8,128)(2,1)S(1)} custom-call(bf16[32,128,128]{2,1,0:T(8,128)(2,1)} %collective-permute-done.1.across_ref, bf16[32,128,128]{2,1,0:T(8,128)(2,1)S(1)} %copy-done.2, bf16[16,128,128]{2,1,0:T(8,128)(2,1)S(1)} %copy-done.5, bf16[16,128,128]{2,1,0:T(8,128)(2,1)} %collective-permute-done.2.rest_ref), custom_call_target="tpu_custom_call" | custom-call | flops 49999998976 | bytes 10000000 | tf_op jit(solution)/shard_map/widen/pallas_call | solution.py:213
  43.0 0.0 copy-start.9
  43.0 2.6 %copy-done.9 = bf16[96,256,128]{2,1,0:T(8,128)(2,1)} copy-done((bf16[96,256,128]{2,1,0:T(8,128)(2,1)}, bf16[96,256,128]{2,1,0:T(8,128)(2,1)S(1)}, u32[]{:S(2)}) %copy-start.9) | copy-done | bytes 6291480
  45.6 7.1 %all-to-all-done = bf16[1152,2,128]{2,1,0:T(2,128)(2,1)S(1)} async-done(((bf16[1152,2,128]{2,1,0:T(2,128)(2,1)}), bf16[1152,2,128]{2,1,0:T(2,128)(2,1)S(1)}, u32[]{:S(2)}, u32[]{:S(2)}) %all-to-all-start) | async-done | bytes 589856 | tf_op jit(solution)/shard_map/all_to_all | solution.py:345
  52.7 0.0 copy-done.6
  52.7 0.0 copy-done.3
  52.7 0.0 copy-start.7
  52.7 0.9 copy-done.7
  53.6 0.0 copy-start.8
  53.6 0.7 copy-done.8
  54.3 3.8 %translate.1 = bf16[4608,128]{1,0:T(8,128)(2,1)} custom-call(s32[4,3]{1,0:T(4,128)S(1)} %copy-done.8, bf16[2304,128]{1,0:T(8,128)(2,1)S(1)} %bitcast.5, bf16[4,3,9,64,128]{4,3,2,1,0:T(8,128)(2,1)S(1)} %copy-done.3, bf16[144,144]{1,0:T(8,128)(2,1)S(1)} %copy-done.7, bf16[288,144]{1,0:T(8,128)(2,1)S(1)} %copy-done.6), custom_call_target="tpu_custom_call" | custom-call | tf_op jit(solution)/shard_map/translate/pallas_call | solution.py:171
  58.1 3.7 %all-to-all-start.1 = ((bf16[1152,4,128]{2,1,0:T(4,128)(2,1)}), bf16[1152,4,128]{2,1,0:T(4,128)(2,1)S(1)}, u32[]{:S(2)}, u32[]{:S(2)}) async-start(bf16[1152,4,128]{2,1,0:T(4,128)(2,1)} %bitcast.2), calls=%async_computation.1 | async-start | bytes 2359296 | tf_op jit(solution)/shard_map/all_to_all | solution.py:345
  61.8 0.7 fusion.3
  62.5 0.1 copy.11
  62.6 0.1 reshape.19.source_ref
  62.7 0.0 copy-start.10
  62.7 2.8 %copy-done.10 = bf16[96,256,128]{2,1,0:T(8,128)(2,1)S(1)} copy-done((bf16[96,256,128]{2,1,0:T(8,128)(2,1)S(1)}, bf16[96,256,128]{2,1,0:T(8,128)(2,1)}, u32[]{:S(2)}) %copy-start.10) | copy-done | bytes 6291480
  65.5 9.4 %near.1.near_ref = f32[32,128,128]{2,1,0:T(8,128)S(1)} custom-call(s32[192]{0:T(256)S(1)} %reshape.19.source_ref, bf16[96,256,128]{2,1,0:T(8,128)(2,1)S(1)} %copy-done.10, bf16[32,6,128,256]{3,2,1,0:T(8,128)(2,1)} %blocks_ref.3), custom_call_target="tpu_custom_call" | custom-call | flops 10000000000 | bytes 20000000 | tf_op jit(solution)/shard_map/near/pallas_call | solution.py:241
  74.9 8.2 %all-to-all-done.1 = bf16[1152,4,128]{2,1,0:T(4,128)(2,1)S(1)} async-done(((bf16[1152,4,128]{2,1,0:T(4,128)(2,1)}), bf16[1152,4,128]{2,1,0:T(4,128)(2,1)S(1)}, u32[]{:S(2)}, u32[]{:S(2)}) %all-to-all-start.1) | async-done | bytes 1179680 | tf_op jit(solution)/shard_map/all_to_all | solution.py:345
  83.1 6.0 %absorb.1 = bf16[32,128,128]{2,1,0:T(8,128)(2,1)} custom-call(s32[128]{0:T(128)} %counts_ref.3, bf16[4608,128]{1,0:T(8,128)(2,1)S(1)} %bitcast.4, f32[32,128,128]{2,1,0:T(8,128)S(1)} %near.1.near_ref, bf16[8,128,2304]{2,1,0:T(8,128)(2,1)} %receive_hbm.1), custom_call_target="tpu_custom_call" | custom-call | tf_op jit(solution)/shard_map/absorb/pallas_call | solution.py:320
Async XLA Ops:
  0.0 37.9 %collective-permute-start.1 = (bf16[32,128,128]{2,1,0:T(8,128)(2,1)}, bf16[32,128,128]{2,1,0:T(8,128)(2,1)}, u32[]{:S(2)}, u32[]{:S(2)}) collective-permute-start(bf16[32,128,128]{2,1,0:T(8,128)(2,1)} %own_ref.3), channel_id=1, source_target_pairs={{1,2},{2,1},{5,6},{6,5},{9,10},{10,9},{13,14},{14,13},{17,18},{18,... | collective-permute-start | bytes 3145736 | tf_op jit(solution)/shard_map/ppermute | solution.py:364
  1.6 36.3 %copy-start.2 = (bf16[32,128,128]{2,1,0:T(8,128)(2,1)S(1)}, bf16[32,128,128]{2,1,0:T(8,128)(2,1)}, u32[]{:S(2)}) copy-start(bf16[32,128,128]{2,1,0:T(8,128)(2,1)} %own_ref.3) | copy-start | bytes 3145732
  3.9 14.9 %collective-permute-start = (bf16[16,128,128]{2,1,0:T(8,128)(2,1)S(1)}, bf16[16,128,128]{2,1,0:T(8,128)(2,1)S(1)}, u32[]{:S(2)}, u32[]{:S(2)}) collective-permute-start(bf16[16,128,128]{2,1,0:T(8,128)(2,1)S(1)} %get-tuple-element.12), channel_id=1, source_target_pairs={{0,1},{2,3},{1,0},{3,2},{4,5},{6,7},{5,4},{7,6},{8,9},{10,11},{9,8... | collective-permute-start | bytes 1572872 | tf_op jit(solution)/shard_map/ppermute | solution.py:363
  7.4 30.5 %collective-permute-start.2 = (bf16[16,128,128]{2,1,0:T(8,128)(2,1)}, bf16[16,128,128]{2,1,0:T(8,128)(2,1)}, u32[]{:S(2)}, u32[]{:S(2)}) collective-permute-start(bf16[16,128,128]{2,1,0:T(8,128)(2,1)} %get-tuple-element.11), channel_id=1, source_target_pairs={{0,1},{2,3},{1,0},{3,2},{4,5},{6,7},{5,4},{7,6},{8,9},{10,11},{9,8... | collective-permute-start | bytes 1572872 | tf_op jit(solution)/shard_map/ppermute | solution.py:365
  18.7 2.3 %copy-start = (bf16[8,1152,256]{2,1,0:T(8,128)(2,1)S(1)}, bf16[8,1152,256]{2,1,0:T(8,128)(2,1)}, u32[]{:S(2)}) copy-start(bf16[8,1152,256]{2,1,0:T(8,128)(2,1)} %aggregate_ref.1) | copy-start | bytes 14155780
  21.1 1.2 %copy-start.1 = (bf16[32,128,128]{2,1,0:T(8,128)(2,1)S(1)}, bf16[32,128,128]{2,1,0:T(8,128)(2,1)}, u32[]{:S(2)}) copy-start(bf16[32,128,128]{2,1,0:T(8,128)(2,1)} %own_ref.3) | copy-start | bytes 3145732
  22.3 3.2 %copy-start.4 = (bf16[16,128,128]{2,1,0:T(8,128)(2,1)}, bf16[16,128,128]{2,1,0:T(8,128)(2,1)S(1)}, u32[]{:S(2)}) copy-start(bf16[16,128,128]{2,1,0:T(8,128)(2,1)S(1)} %collective-permute-done.moved_ref) | copy-start | bytes 1572868
  25.5 27.2 %copy-start.6 = (bf16[288,144]{1,0:T(8,128)(2,1)S(1)}, bf16[288,144]{1,0:T(8,128)(2,1)}, u32[]{:S(2)}) copy-start(bf16[288,144]{1,0:T(8,128)(2,1)} %constant.71.clone.spread_ref) | copy-start | bytes 248836
  25.6 27.2 %all-to-all-start = ((bf16[1152,2,128]{2,1,0:T(2,128)(2,1)}), bf16[1152,2,128]{2,1,0:T(2,128)(2,1)S(1)}, u32[]{:S(2)}, u32[]{:S(2)}) async-start(bf16[1152,2,128]{2,1,0:T(2,128)(2,1)} %bitcast), calls=%async_computation | async-start | bytes 1179648 | tf_op jit(solution)/shard_map/all_to_all | solution.py:345
  37.9 14.8 %copy-start.3 = (bf16[4,3,9,64,128]{4,3,2,1,0:T(8,128)(2,1)S(1)}, bf16[4,3,9,64,128]{4,3,2,1,0:T(8,128)(2,1)}, u32[]{:S(2)}) copy-start(bf16[4,3,9,64,128]{4,3,2,1,0:T(8,128)(2,1)} %translations_ref.1) | copy-start | bytes 5308420
  37.9 1.2 %copy-start.5 = (bf16[16,128,128]{2,1,0:T(8,128)(2,1)S(1)}, bf16[16,128,128]{2,1,0:T(8,128)(2,1)}, u32[]{:S(2)}) copy-start(bf16[16,128,128]{2,1,0:T(8,128)(2,1)} %copy-done.4) | copy-start | bytes 1572868
  43.0 2.7 %copy-start.9 = (bf16[96,256,128]{2,1,0:T(8,128)(2,1)}, bf16[96,256,128]{2,1,0:T(8,128)(2,1)S(1)}, u32[]{:S(2)}) copy-start(bf16[96,256,128]{2,1,0:T(8,128)(2,1)S(1)} %widen.1.window_ref) | copy-start | bytes 18874372
  52.7 0.9 copy-start.7
  53.6 0.7 copy-start.8
  58.1 25.0 %all-to-all-start.1 = ((bf16[1152,4,128]{2,1,0:T(4,128)(2,1)}), bf16[1152,4,128]{2,1,0:T(4,128)(2,1)S(1)}, u32[]{:S(2)}, u32[]{:S(2)}) async-start(bf16[1152,4,128]{2,1,0:T(4,128)(2,1)} %bitcast.2), calls=%async_computation.1 | async-start | bytes 2359296 | tf_op jit(solution)/shard_map/all_to_all | solution.py:345
  62.7 2.8 %copy-start.10 = (bf16[96,256,128]{2,1,0:T(8,128)(2,1)S(1)}, bf16[96,256,128]{2,1,0:T(8,128)(2,1)}, u32[]{:S(2)}) copy-start(bf16[96,256,128]{2,1,0:T(8,128)(2,1)} %copy-done.9) | copy-start | bytes 18874372

commit v5 on v4

v5 whole, which is shorter than its diff:
```python
import numpy as np
import jax
import jax.numpy as jnp
from jax import lax
from jax.experimental import pallas as pl
from jax.experimental.pallas import tpu as pltpu
from jax.sharding import PartitionSpec as P

AXES = ("dir", "near")
MIB = 1 << 20


def quarter(v):
    lane = lax.broadcasted_iota(jnp.int32, (1, v.shape[-1]), 1)
    sign = jnp.where(lane < v.shape[-1] // 2, -1.0, 1.0).astype(v.dtype)
    return pltpu.roll(v, v.shape[-1] // 2, 1) * sign


def own_range(counts_ref):
    device = lax.axis_index("dir") * lax.axis_size("near") + lax.axis_index("near")
    odd = device % 2
    return odd * counts_ref[device - odd], counts_ref[device]


def radiate_kernel(
    counts_ref, currents_hbm, aggregate_hbm, out_hbm, currents_ref, aggregate_ref, stacked_ref,
    rows_ref, out_ref, sems, store_sems,
):
    children, directions, width = aggregate_ref.shape
    unknowns = width // 2
    positions = stacked_ref.shape[1] // 128
    tiles = sems.shape[0] - 1
    tile = directions // tiles
    own = pltpu.make_async_copy(currents_hbm, currents_ref, sems.at[tiles])
    own.start()
    parts = []
    for i in range(tiles):
        rows = slice(i * tile, (i + 1) * tile)
        part = pltpu.make_async_copy(
            aggregate_hbm.at[:, rows, :], aggregate_ref.at[:, rows, :], sems.at[i]
        )
        part.start()
        parts.append(part)
    offset, count = own_range(counts_ref)
    own.wait()
    for p in range(positions):
        slot = p - offset
        live = jnp.logical_and(slot >= 0, slot < count)
        row = jnp.clip(slot, 0, positions - 1) * children
        lanes = slice(p * 128, (p + 1) * 128)

        @pl.when(live)
        def _():
            for c in range(children):
                v = currents_ref[row + c]
                stacked_ref[c * width : c * width + unknowns, lanes] = v
                stacked_ref[c * width + unknowns : (c + 1) * width, lanes] = quarter(v)

        @pl.when(jnp.logical_not(live))
        def _():
            stacked_ref[:, lanes] = jnp.zeros((children * width, 128), jnp.bfloat16)

    stores = []
    for i in range(tiles):
        parts[i].wait()
        rows = slice(i * tile, (i + 1) * tile)
        total = jnp.dot(
            jnp.concatenate([aggregate_ref[c, rows, :] for c in range(children)], axis=1),
            stacked_ref[...],
            preferred_element_type=jnp.float32,
        )
        for p in range(positions):
            rows_ref[pl.ds(p, tile, stride=positions), :] = total[:, p * 128 : (p + 1) * 128]
        span = slice(i * tile * positions, (i + 1) * tile * positions)
        out_ref[span, :] = rows_ref[...].astype(jnp.bfloat16)
        store = pltpu.make_async_copy(out_ref.at[span], out_hbm.at[span], store_sems.at[i])
        store.start()
        stores.append(store)
    for store in stores:
        store.wait()


def radiate(counts, currents, aggregate):
    children, directions, width = aggregate.shape
    positions = currents.shape[0] // children
    tiles = 4
    hbm = pl.BlockSpec(memory_space=pltpu.HBM)
    return pl.pallas_call(
        radiate_kernel,
        in_specs=[pl.BlockSpec(memory_space=pltpu.SMEM), hbm, hbm],
        out_specs=hbm,
        scratch_shapes=[
            pltpu.VMEM(currents.shape, currents.dtype),
            pltpu.VMEM(aggregate.shape, aggregate.dtype),
            pltpu.VMEM((children * width, positions * 128), jnp.bfloat16),
            pltpu.VMEM((directions // tiles * positions, 128), jnp.float32),
            pltpu.VMEM((directions * positions, 128), jnp.bfloat16),
            pltpu.SemaphoreType.DMA((tiles + 1,)),
            pltpu.SemaphoreType.DMA((tiles,)),
        ],
        out_shape=jax.ShapeDtypeStruct((directions * positions, 128), jnp.bfloat16),
        compiler_params=pltpu.CompilerParams(vmem_limit_bytes=40 * MIB),
        name="radiate",
    )(counts, currents, aggregate)


def pair_rows(per_group, positions):
    pairs = 4
    select = np.zeros((per_group * pairs * positions, 2 * pairs * per_group * positions))
    for r in range(per_group):
        for pair in range(pairs):
            for p in range(positions):
                row = (r * pairs + pair) * positions + p
                for side in range(2):
                    select[row, ((2 * pair + side) * per_group + r) * positions + p] = 1.0
    return select


def translate_kernel(
    blocks_ref, rows_ref, translations_ref, select_ref, spread_ref, out_hbm, values_ref, sums_ref,
    out_ref, sems,
):
    block_count, list_length, per_group = translations_ref.shape[:3]
    block = translations_ref.shape[3]
    chunk = select_ref.shape[1]
    groups = rows_ref.shape[0] // chunk
    per_block = groups // block_count
    step = block // per_block
    for g in range(groups):
        picked = jnp.dot(
            select_ref[...],
            rows_ref[g * chunk : (g + 1) * chunk, :],
            preferred_element_type=jnp.float32,
        ).astype(jnp.bfloat16)
        other = quarter(picked)
        b = g // per_block
        start = (g % per_block) * step
        for r in range(per_group):
            part = slice(r * step, (r + 1) * step)
            values_ref[b, r, start : start + step, :] = picked[part]
            values_ref[b, r, block + start : block + start + step, :] = other[part]
    stores = []
    for t in range(block_count):
        sources = [blocks_ref[t, e] for e in range(list_length)]
        for r in range(per_group):
            total = jnp.dot(
                jnp.concatenate([translations_ref[t, e, r] for e in range(list_length)], axis=1),
                jnp.concatenate([values_ref[source, r] for source in sources], axis=0),
                preferred_element_type=jnp.float32,
            )
            total = total.astype(jnp.bfloat16)
            for q in range(per_block):
                sums_ref[t * per_block + q, r * step : (r + 1) * step, :] = total[
                    q * step : (q + 1) * step
                ]
        for g in range(t * per_block, (t + 1) * per_block):
            out_ref[g * chunk : (g + 1) * chunk, :] = jnp.dot(
                spread_ref[...], sums_ref[g], preferred_element_type=jnp.float32
            ).astype(jnp.bfloat16)
        span = slice(t * per_block * chunk, (t + 1) * per_block * chunk)
        store = pltpu.make_async_copy(out_ref.at[span], out_hbm.at[span], sems.at[t])
        store.start()
        stores.append(store)
    for store in stores:
        store.wait()


def translate(source_blocks, rows, translations, positions):
    block_count, _, per_group, block, doubled = translations.shape
    select = pair_rows(per_group, positions)
    groups = rows.shape[0] // select.shape[1]
    vmem = pl.BlockSpec(memory_space=pltpu.VMEM)
    return pl.pallas_call(
        translate_kernel,
        in_specs=[pl.BlockSpec(memory_space=pltpu.SMEM), vmem, vmem, vmem, vmem],
        out_specs=pl.BlockSpec(memory_space=pltpu.HBM),
        scratch_shapes=[
            pltpu.VMEM((block_count, per_group, doubled, 128), jnp.bfloat16),
            pltpu.VMEM((groups, select.shape[0], 128), jnp.bfloat16),
            pltpu.VMEM(rows.shape, jnp.bfloat16),
            pltpu.SemaphoreType.DMA((block_count,)),
        ],
        out_shape=jax.ShapeDtypeStruct(rows.shape, jnp.bfloat16),
        compiler_params=pltpu.CompilerParams(vmem_limit_bytes=32 * MIB),
        name="translate",
    )(
        source_blocks,
        rows,
        translations,
        jnp.asarray(select, jnp.bfloat16),
        jnp.asarray(select.T, jnp.bfloat16),
    )


def near_kernel(source_ref, across_ref, own_ref, partner_ref, blocks_ref, out_ref, window_ref):
    slots = own_ref.shape[0]
    unknowns = own_ref.shape[1]
    leaves, terms = blocks_ref.shape[:2]
    first = pl.program_id(0) * leaves

    @pl.when(first == 0)
    def _():
        for part, ref in enumerate((across_ref, own_ref, partner_ref)):

            def fill(i, carry, part=part, ref=ref):
                for j in range(4):
                    v = ref[i * 4 + j]
                    row = part * slots + i * 4 + j
                    window_ref[row, 0:unknowns, :] = v
                    window_ref[row, unknowns : 2 * unknowns, :] = quarter(v)
                return carry

            lax.fori_loop(0, slots // 4, fill, 0)

    for i in range(leaves):
        sources = [source_ref[(first + i) * terms + e] for e in range(terms)]
        out_ref[i] = jnp.dot(
            jnp.concatenate([blocks_ref[i, e] for e in range(terms)], axis=1),
            jnp.concatenate([window_ref[source] for source in sources], axis=0),
            preferred_element_type=jnp.float32,
        )


def near(source, across, own, partner, blocks):
    slots, unknowns, channels = own.shape
    _, terms, _, doubled = blocks.shape
    leaves = 4
    whole = pl.BlockSpec(own.shape, lambda i, _: (0, 0, 0))
    return pl.pallas_call(
        near_kernel,
        grid_spec=pltpu.PrefetchScalarGridSpec(
            num_scalar_prefetch=1,
            grid=(slots // leaves,),
            in_specs=[
                whole,
                whole,
                whole,
                pl.BlockSpec((leaves, terms, unknowns, doubled), lambda i, _: (i, 0, 0, 0)),
            ],
            out_specs=pl.BlockSpec((leaves, unknowns, channels), lambda i, _: (i, 0, 0)),
            scratch_shapes=[pltpu.VMEM((3 * slots, doubled, channels), jnp.bfloat16)],
        ),
        out_shape=jax.ShapeDtypeStruct((slots, unknowns, channels), jnp.float32),
        compiler_params=pltpu.CompilerParams(vmem_limit_bytes=40 * MIB),
        cost_estimate=pl.CostEstimate(flops=10**10, transcendentals=0, bytes_accessed=2 * 10**7),
        name="near",
    )(source.reshape(-1), across, own, partner, blocks)


def absorb_kernel(
    counts_ref, rows_ref, near_ref, receive_hbm, out_hbm, wide_ref, doubled_ref, receive_ref,
    fields_ref, fetch_sems, store_sems,
):
    children, unknowns, doubled = receive_ref.shape
    directions = doubled // 2
    positions = doubled_ref.shape[1] // 128
    steps = fetch_sems.shape[0]
    octants = children // steps
    parts = []
    for q in range(steps):
        span = slice(q * octants, (q + 1) * octants)
        part = pltpu.make_async_copy(receive_hbm.at[span], receive_ref.at[span], fetch_sems.at[q])
        part.start()
        parts.append(part)
    offset, count = own_range(counts_ref)
    for slot in range(positions):

        @pl.when(slot >= count)
        def _():
            fields_ref[slot * children : (slot + 1) * children] = jnp.zeros(
                (children, unknowns, 128), jnp.bfloat16
            )

    wide_ref[...] = rows_ref[...].astype(jnp.float32)
    for p in range(positions):
        v = wide_ref[pl.ds(p, directions, stride=positions), :].astype(jnp.bfloat16)
        doubled_ref[0:directions, p * 128 : (p + 1) * 128] = v
        doubled_ref[directions:doubled, p * 128 : (p + 1) * 128] = quarter(v)
    stores = []
    for q in range(steps):
        parts[q].wait()
        lines = receive_ref[q * octants : (q + 1) * octants].reshape(octants * unknowns, doubled)
        far = jnp.dot(lines, doubled_ref[...], preferred_element_type=jnp.float32)
        for p in range(positions):
            slot = p - offset

            @pl.when(jnp.logical_and(slot >= 0, slot < count))
            def _():
                for c in range(octants):
                    leaf = slot * children + q * octants + c
                    part = far[c * unknowns : (c + 1) * unknowns, p * 128 : (p + 1) * 128]
                    fields_ref[leaf] = (part + near_ref[leaf]).astype(jnp.bfloat16)

        for slot in range(positions):
            span = pl.ds(slot * children + q * octants, octants)
            store = pltpu.make_async_copy(
                fields_ref.at[span], out_hbm.at[span], store_sems.at[q, slot]
            )
            store.start()
            stores.append(store)
    for store in stores:
        store.wait()


def absorb(counts, rows, receive, near_field):
    children, _, doubled = receive.shape
    positions = near_field.shape[0] // children
    steps = 4
    vmem = pl.BlockSpec(memory_space=pltpu.VMEM)
    hbm = pl.BlockSpec(memory_space=pltpu.HBM)
    return pl.pallas_call(
        absorb_kernel,
        in_specs=[pl.BlockSpec(memory_space=pltpu.SMEM), vmem, vmem, hbm],
        out_specs=hbm,
        scratch_shapes=[
            pltpu.VMEM(rows.shape, jnp.float32),
            pltpu.VMEM((doubled, positions * 128), jnp.bfloat16),
            pltpu.VMEM(receive.shape, receive.dtype),
            pltpu.VMEM(near_field.shape, jnp.bfloat16),
            pltpu.SemaphoreType.DMA((steps,)),
            pltpu.SemaphoreType.DMA((steps, positions)),
        ],
        out_shape=jax.ShapeDtypeStruct(near_field.shape, jnp.bfloat16),
        compiler_params=pltpu.CompilerParams(vmem_limit_bytes=48 * MIB),
        name="absorb",
    )(counts, rows, near_field, receive)


def in_hbm(array):
    return pltpu.with_memory_space_constraint(array, pltpu.HBM)


def swap(rows, positions):
    channels = rows.shape[-1]
    shaped = rows.reshape(-1, positions, channels)
    return lax.all_to_all(shaped, AXES, 0, 0, tiled=True).reshape(-1, channels)


def body(
    currents, counts, near_source, near_blocks, aggregate, receive, translations, source_blocks
):
    slots = currents.shape[0]
    positions = slots // aggregate.shape[0]
    device = lax.axis_index(AXES)
    local = near_source - (device - 1) * slots
    mirrored = local + 2 * slots - 2 * slots * (local // slots)
    local = jnp.where(device % 2 == 1, mirrored, local)
    count = lax.axis_size("near")
    inner = [(i, i + 1) for i in range(1, count - 1, 2)]
    outer = [(i, i + 1) for i in range(0, count, 2)]
    across = lax.ppermute(currents, "near", inner + [(j, i) for i, j in inner])
    partner = lax.ppermute(currents, "near", outer + [(j, i) for i, j in outer])

    patterns = radiate(in_hbm(counts), in_hbm(currents), in_hbm(aggregate))
    gathered = swap(patterns, positions)
    incoming = translate(source_blocks, gathered, translations, positions)
    returned = swap(incoming, positions)

    local, _ = lax.optimization_barrier((local, incoming))
    near_field = near(local, across, in_hbm(currents), partner, in_hbm(near_blocks))
    return absorb(in_hbm(counts), returned, in_hbm(receive), near_field)


def solution(mesh):
    spread = P(AXES, None, None)
    return jax.shard_map(
        body,
        mesh=mesh,
        in_specs=(
            spread,
            P(),
            P(AXES, None),
            P(AXES, None, None, None),
            P(),
            P(),
            P(None, None, AXES, None, None),
            P(),
        ),
        out_specs=spread,
        check_vma=False,
    )
```

time: 89.7 us -> 80.6 us (0.90)
  local copies, waits for them, and re-layouts: 14.1 us -> 0.22 us
  waiting for transfers between devices: 26.6 us -> 30.9 us
  Pallas kernels: 26.3 us -> 29.6 us
  starting transfers between devices: 21.2 us -> 19.4 us
    unnamed x22 -> x10, local copies, waits for them, and re-layouts: 11.7 us -> 0.03 us
    all_to_all x2, waiting for transfers between devices: 15.3 us -> 23.7 us  [swap(): return lax.all_to_all(shaped, AXES, 0, 0, tiled=True).reshape(-1, channels)]
    ppermute x3 -> x2, waiting for transfers between devices: 11.3 us -> 7.11 us  [the longest x1 7.1 us: body(): partner = lax.ppermute(currents, 'near', outer + [(j, i) for i, j in outer])]
    pallas_call x1 -> x0, Pallas kernels: 3.87 us -> none  [widen(): pl.pallas_call(widen_kernel, in_specs=[vmem] * 4, out_specs=vmem, out_sha...]
    pallas_call x1, Pallas kernels: 9.4 us -> 12.9 us  [near(): pl.pallas_call(near_kernel, grid_spec=pltpu.PrefetchScalarGridSpec(num_sc...]
    pallas_call x1, Pallas kernels: 3.22 us -> 6.56 us  [radiate(): pl.pallas_call(radiate_kernel, in_specs=[pl.BlockSpec(memory_space=pltpu....]
    dynamic_slice x1 -> x0, local copies, waits for them, and re-layouts: 2.22 us -> none  [body(): kept = lax.dynamic_slice_in_dim(currents, odd * half, half, 0)]
    all_to_all x2, starting transfers between devices: 16 us -> 14.8 us  [swap(): return lax.all_to_all(shaped, AXES, 0, 0, tiled=True).reshape(-1, channels)]
  transfers between devices with their start and end apart: 5 -> 4, of which waited for: 3 -> 3; matrix products, arithmetic and copies ran while one was open for 3% -> 0% of each run, Pallas kernels for 18% -> 21%
where the time goes in v5:
time: 80.6 us; the launch traced here: 80.3 us
  waiting for transfers between devices  30.9 us (38%)
  Pallas kernels  29.6 us (37%)
  starting transfers between devices  19.4 us (24%)
    all_to_all x2, waiting for transfers between devices, swap(): return lax.all_to_all(shaped, AXES, 0, 0, tiled=True).reshape(-1, channels)  23.7 us
    all_to_all x2, starting transfers between devices, swap(): return lax.all_to_all(shaped, AXES, 0, 0, tiled=True).reshape(-1, channels)  14.8 us
    pallas_call x1, Pallas kernels, near(): pl.pallas_call(near_kernel, grid_spec=pltpu.PrefetchScalarGridSpec(num_sc...  12.9 us
    ppermute x1, waiting for transfers between devices, body(): partner = lax.ppermute(currents, 'near', outer + [(j, i) for i, j in outer])  7.1 us
    pallas_call x1, Pallas kernels, radiate(): pl.pallas_call(radiate_kernel, in_specs=[pl.BlockSpec(memory_space=pltpu....  6.56 us
    pallas_call x1, Pallas kernels, absorb(): pl.pallas_call(absorb_kernel, in_specs=[pl.BlockSpec(memory_space=pltpu.S...  6.1 us
    pallas_call x1, Pallas kernels, translate(): pl.pallas_call(translate_kernel, in_specs=[pl.BlockSpec(memory_space=pltp...  4.1 us
    ppermute x1, starting transfers between devices, body(): partner = lax.ppermute(currents, 'near', outer + [(j, i) for i, j in outer])  2.9 us
  transfers between devices with their start and end apart: 4, of which 3 were waited for; matrix products, arithmetic and copies ran while one was open for 0% of the time, Pallas kernels for 21%

profile of v5, /device:TPU:1, one launch (start us, length us, event | category | flops | bytes accessed | tf_op | source)
XLA Modules:
  0.0 80.3 jit_solution(11361917945154702221)
XLA Ops:
  0.0 6.6 %radiate.1 = bf16[4608,128]{1,0:T(8,128)(2,1)} custom-call(s32[128]{0:T(128)} %counts_ref.3, bf16[32,128,128]{2,1,0:T(8,128)(2,1)} %own_ref.1, bf16[8,1152,256]{2,1,0:T(8,128)(2,1)} %aggregate_hbm.1), custom_call_target="tpu_custom_call" | custom-call | tf_op jit(solution)/shard_map/radiate/pallas_call | solution.py:88
  6.6 0.0 copy-start
  6.6 0.0 copy-start.1
  6.6 0.0 copy-start.2
  6.6 0.0 copy-start.3
  6.6 11.3 %all-to-all-start = ((bf16[1152,4,128]{2,1,0:T(4,128)(2,1)}), bf16[1152,4,128]{2,1,0:T(4,128)(2,1)S(1)}, u32[]{:S(2)}, u32[]{:S(2)}) async-start(bf16[1152,4,128]{2,1,0:T(4,128)(2,1)} %bitcast), calls=%async_computation | async-start | bytes 2359296 | tf_op jit(solution)/shard_map/all_to_all | solution.py:336
  17.9 1.7 %collective-permute-start = (bf16[32,128,128]{2,1,0:T(8,128)(2,1)}, bf16[32,128,128]{2,1,0:T(8,128)(2,1)}, u32[]{:S(2)}, u32[]{:S(2)}) collective-permute-start(bf16[32,128,128]{2,1,0:T(8,128)(2,1)} %own_ref.1), channel_id=1, source_target_pairs={{1,2},{2,1},{5,6},{6,5},{9,10},{10,9},{13,14},{14,13},{17,18},{18,... | collective-permute-start | bytes 3145736 | tf_op jit(solution)/shard_map/ppermute | solution.py:351
  19.6 2.9 %collective-permute-start.1 = (bf16[32,128,128]{2,1,0:T(8,128)(2,1)}, bf16[32,128,128]{2,1,0:T(8,128)(2,1)}, u32[]{:S(2)}, u32[]{:S(2)}) collective-permute-start(bf16[32,128,128]{2,1,0:T(8,128)(2,1)} %own_ref.1), channel_id=1, source_target_pairs={{0,1},{2,3},{1,0},{3,2},{4,5},{6,7},{5,4},{7,6},{8,9},{10,11},{9,8... | collective-permute-start | bytes 3145736 | tf_op jit(solution)/shard_map/ppermute | solution.py:352
  22.5 17.1 %all-to-all-done = bf16[1152,4,128]{2,1,0:T(4,128)(2,1)S(1)} async-done(((bf16[1152,4,128]{2,1,0:T(4,128)(2,1)}), bf16[1152,4,128]{2,1,0:T(4,128)(2,1)S(1)}, u32[]{:S(2)}, u32[]{:S(2)}) %all-to-all-start) | async-done | bytes 1179680 | tf_op jit(solution)/shard_map/all_to_all | solution.py:336
  39.5 0.0 copy-done
  39.5 0.0 copy-done.1
  39.5 0.0 copy-done.2
  39.5 0.0 copy-done.3
  39.5 4.1 %translate.1 = bf16[4608,128]{1,0:T(8,128)(2,1)} custom-call(s32[4,3]{1,0:T(4,128)S(1)} %copy-done.3, bf16[4608,128]{1,0:T(8,128)(2,1)S(1)} %bitcast.5, bf16[4,3,9,64,128]{4,3,2,1,0:T(8,128)(2,1)S(1)} %copy-done, bf16[144,288]{1,0:T(8,128)(2,1)S(1)} %copy-done.2, bf16[288,144]{1,0:T(8,128)(2,1)S(1)} %copy-done.1), custom_call_target="tpu_custom_call" | custom-call | tf_op jit(solution)/shard_map/translate/pallas_call | solution.py:173
  43.6 0.0 copy-start.4
  43.7 3.6 %all-to-all-start.1 = ((bf16[1152,4,128]{2,1,0:T(4,128)(2,1)}), bf16[1152,4,128]{2,1,0:T(4,128)(2,1)S(1)}, u32[]{:S(2)}, u32[]{:S(2)}) async-start(bf16[1152,4,128]{2,1,0:T(4,128)(2,1)} %bitcast.2), calls=%async_computation.1 | async-start | bytes 2359296 | tf_op jit(solution)/shard_map/all_to_all | solution.py:336
  47.3 0.0 copy-done.4
  47.3 0.1 copy.11
  47.4 0.1 reshape.19.source_ref
  47.5 0.0 collective-permute-done.across_ref
  47.5 7.1 %collective-permute-done.1.partner_ref = bf16[32,128,128]{2,1,0:T(8,128)(2,1)} collective-permute-done((bf16[32,128,128]{2,1,0:T(8,128)(2,1)}, bf16[32,128,128]{2,1,0:T(8,128)(2,1)}, u32[]{:S(2)}, u32[]{:S(2)}) %collective-permute-start.1) | collective-permute-done | bytes 1048608 | tf_op jit(solution)/shard_map/ppermute | solution.py:352
  54.6 12.9 %near.1.near_ref = f32[32,128,128]{2,1,0:T(8,128)S(1)} custom-call(s32[192]{0:T(256)S(1)} %reshape.19.source_ref, bf16[32,128,128]{2,1,0:T(8,128)(2,1)} %collective-permute-done.across_ref, bf16[32,128,128]{2,1,0:T(8,128)(2,1)} %own_ref.1, bf16[32,128,128]{2,1,0:T(8,128)(2,1)} %collective-permute-done.1.partner_ref, bf16[32,6,128,256]{3,2,1,0:T(8,128)(2,1)} %blocks_ref.3), custom_call_target="tpu_custom_call" | custom-call | flops 10000000000 | bytes 20000000 | tf_op jit(solution)/shard_map/near/pallas_call | solution.py:229
  67.5 6.7 %all-to-all-done.1 = bf16[1152,4,128]{2,1,0:T(4,128)(2,1)S(1)} async-done(((bf16[1152,4,128]{2,1,0:T(4,128)(2,1)}), bf16[1152,4,128]{2,1,0:T(4,128)(2,1)S(1)}, u32[]{:S(2)}, u32[]{:S(2)}) %all-to-all-start.1) | async-done | bytes 1179680 | tf_op jit(solution)/shard_map/all_to_all | solution.py:336
  74.2 6.1 %absorb.1 = bf16[32,128,128]{2,1,0:T(8,128)(2,1)} custom-call(s32[128]{0:T(128)} %counts_ref.3, bf16[4608,128]{1,0:T(8,128)(2,1)S(1)} %bitcast.4, f32[32,128,128]{2,1,0:T(8,128)S(1)} %near.1.near_ref, bf16[8,128,2304]{2,1,0:T(8,128)(2,1)} %receive_hbm.1), custom_call_target="tpu_custom_call" | custom-call | tf_op jit(solution)/shard_map/absorb/pallas_call | solution.py:311
  (1 shorter events, 0.0 us)
Async XLA Ops:
  6.6 32.9 %copy-start = (bf16[4,3,9,64,128]{4,3,2,1,0:T(8,128)(2,1)S(1)}, bf16[4,3,9,64,128]{4,3,2,1,0:T(8,128)(2,1)}, u32[]{:S(2)}) copy-start(bf16[4,3,9,64,128]{4,3,2,1,0:T(8,128)(2,1)} %translations_ref.1) | copy-start | bytes 5308420
  6.6 32.9 %copy-start.1 = (bf16[288,144]{1,0:T(8,128)(2,1)S(1)}, bf16[288,144]{1,0:T(8,128)(2,1)}, u32[]{:S(2)}) copy-start(bf16[288,144]{1,0:T(8,128)(2,1)} %constant.48.clone.spread_ref) | copy-start | bytes 248836
  6.6 32.9 %copy-start.2 = (bf16[144,288]{1,0:T(8,128)(2,1)S(1)}, bf16[144,288]{1,0:T(8,128)(2,1)}, u32[]{:S(2)}) copy-start(bf16[144,288]{1,0:T(8,128)(2,1)} %constant.47.clone.select_ref) | copy-start | bytes 248836
  6.6 32.9 %copy-start.3 = (s32[4,3]{1,0:T(4,128)S(1)}, s32[4,3]{1,0:T(4,128)}, u32[]{:S(2)}) copy-start(s32[4,3]{1,0:T(4,128)} %blocks_ref.2) | copy-start | bytes 148
  6.6 32.9 %all-to-all-start = ((bf16[1152,4,128]{2,1,0:T(4,128)(2,1)}), bf16[1152,4,128]{2,1,0:T(4,128)(2,1)S(1)}, u32[]{:S(2)}, u32[]{:S(2)}) async-start(bf16[1152,4,128]{2,1,0:T(4,128)(2,1)} %bitcast), calls=%async_computation | async-start | bytes 2359296 | tf_op jit(solution)/shard_map/all_to_all | solution.py:336
  17.9 29.6 %collective-permute-start = (bf16[32,128,128]{2,1,0:T(8,128)(2,1)}, bf16[32,128,128]{2,1,0:T(8,128)(2,1)}, u32[]{:S(2)}, u32[]{:S(2)}) collective-permute-start(bf16[32,128,128]{2,1,0:T(8,128)(2,1)} %own_ref.1), channel_id=1, source_target_pairs={{1,2},{2,1},{5,6},{6,5},{9,10},{10,9},{13,14},{14,13},{17,18},{18,... | collective-permute-start | bytes 3145736 | tf_op jit(solution)/shard_map/ppermute | solution.py:351
  19.6 35.0 %collective-permute-start.1 = (bf16[32,128,128]{2,1,0:T(8,128)(2,1)}, bf16[32,128,128]{2,1,0:T(8,128)(2,1)}, u32[]{:S(2)}, u32[]{:S(2)}) collective-permute-start(bf16[32,128,128]{2,1,0:T(8,128)(2,1)} %own_ref.1), channel_id=1, source_target_pairs={{0,1},{2,3},{1,0},{3,2},{4,5},{6,7},{5,4},{7,6},{8,9},{10,11},{9,8... | collective-permute-start | bytes 3145736 | tf_op jit(solution)/shard_map/ppermute | solution.py:352
  43.6 3.6 %copy-start.4 = (s32[32,6]{0,1:T(8,128)S(1)}, s32[32,6]{0,1:T(8,128)}, u32[]{:S(2)}) copy-start(s32[32,6]{0,1:T(8,128)} %param.12) | copy-start | bytes 2308
  43.7 30.5 %all-to-all-start.1 = ((bf16[1152,4,128]{2,1,0:T(4,128)(2,1)}), bf16[1152,4,128]{2,1,0:T(4,128)(2,1)S(1)}, u32[]{:S(2)}, u32[]{:S(2)}) async-start(bf16[1152,4,128]{2,1,0:T(4,128)(2,1)} %bitcast.2), calls=%async_computation.1 | async-start | bytes 2359296 | tf_op jit(solution)/shard_map/all_to_all | solution.py:336

commit v6 on v5

--- a/solution.py
+++ b/solution.py
@@ -8,6 +8,8 @@
 
 AXES = ("dir", "near")
 MIB = 1 << 20
+SPLITS = (288, 288, 288, 288)
+SHARES = (2, 2, 4)
 
 
 def quarter(v):
@@ -23,24 +25,25 @@
 
 
 def radiate_kernel(
-    counts_ref, currents_hbm, aggregate_hbm, out_hbm, currents_ref, aggregate_ref, stacked_ref,
-    rows_ref, out_ref, sems, store_sems,
+    counts_hbm, currents_hbm, aggregate_hbm, out_hbm, counts_ref, currents_ref, aggregate_ref,
+    stacked_ref, rows_ref, out_ref, sems, store_sems,
 ):
     children, directions, width = aggregate_ref.shape
     unknowns = width // 2
     positions = stacked_ref.shape[1] // 128
-    tiles = sems.shape[0] - 1
-    tile = directions // tiles
-    own = pltpu.make_async_copy(currents_hbm, currents_ref, sems.at[tiles])
+    tiles = [slice(sum(SPLITS[:i]), sum(SPLITS[: i + 1])) for i in range(len(SPLITS))]
+    table = pltpu.make_async_copy(counts_hbm, counts_ref, sems.at[len(tiles) + 1])
+    table.start()
+    own = pltpu.make_async_copy(currents_hbm, currents_ref, sems.at[len(tiles)])
     own.start()
     parts = []
-    for i in range(tiles):
-        rows = slice(i * tile, (i + 1) * tile)
+    for i, rows in enumerate(tiles):
         part = pltpu.make_async_copy(
             aggregate_hbm.at[:, rows, :], aggregate_ref.at[:, rows, :], sems.at[i]
         )
         part.start()
         parts.append(part)
+    table.wait()
     offset, count = own_range(counts_ref)
     own.wait()
     for p in range(positions):
@@ -61,9 +64,9 @@
             stacked_ref[:, lanes] = jnp.zeros((children * width, 128), jnp.bfloat16)
 
     stores = []
-    for i in range(tiles):
+    for i, rows in enumerate(tiles):
         parts[i].wait()
-        rows = slice(i * tile, (i + 1) * tile)
+        tile = SPLITS[i]
         total = jnp.dot(
             jnp.concatenate([aggregate_ref[c, rows, :] for c in range(children)], axis=1),
             stacked_ref[...],
@@ -71,8 +74,8 @@
         )
         for p in range(positions):
             rows_ref[pl.ds(p, tile, stride=positions), :] = total[:, p * 128 : (p + 1) * 128]
-        span = slice(i * tile * positions, (i + 1) * tile * positions)
-        out_ref[span, :] = rows_ref[...].astype(jnp.bfloat16)
+        span = slice(rows.start * positions, rows.stop * positions)
+        out_ref[span, :] = rows_ref[0 : tile * positions, :].astype(jnp.bfloat16)
         store = pltpu.make_async_copy(out_ref.at[span], out_hbm.at[span], store_sems.at[i])
         store.start()
         stores.append(store)
@@ -83,19 +86,20 @@
 def radiate(counts, currents, aggregate):
     children, directions, width = aggregate.shape
     positions = currents.shape[0] // children
-    tiles = 4
+    tiles = len(SPLITS)
     hbm = pl.BlockSpec(memory_space=pltpu.HBM)
     return pl.pallas_call(
         radiate_kernel,
-        in_specs=[pl.BlockSpec(memory_space=pltpu.SMEM), hbm, hbm],
+        in_specs=[hbm, hbm, hbm],
         out_specs=hbm,
         scratch_shapes=[
+            pltpu.SMEM(counts.shape, counts.dtype),
             pltpu.VMEM(currents.shape, currents.dtype),
             pltpu.VMEM(aggregate.shape, aggregate.dtype),
             pltpu.VMEM((children * width, positions * 128), jnp.bfloat16),
-            pltpu.VMEM((directions // tiles * positions, 128), jnp.float32),
+            pltpu.VMEM((max(SPLITS) * positions, 128), jnp.float32),
             pltpu.VMEM((directions * positions, 128), jnp.bfloat16),
-            pltpu.SemaphoreType.DMA((tiles + 1,)),
+            pltpu.SemaphoreType.DMA((tiles + 2,)),
             pltpu.SemaphoreType.DMA((tiles,)),
         ],
         out_shape=jax.ShapeDtypeStruct((directions * positions, 128), jnp.bfloat16),
@@ -117,28 +121,35 @@
 
 
 def translate_kernel(
-    blocks_ref, rows_ref, translations_ref, select_ref, spread_ref, out_hbm, values_ref, sums_ref,
-    out_ref, sems,
+    blocks_hbm, rows_ref, translations_ref, select_ref, spread_ref, out_hbm, blocks_ref, values_ref,
+    sums_ref, out_ref, sems,
 ):
+    table = pltpu.make_async_copy(blocks_hbm, blocks_ref, sems.at[0])
+    table.start()
     block_count, list_length, per_group = translations_ref.shape[:3]
     block = translations_ref.shape[3]
     chunk = select_ref.shape[1]
     groups = rows_ref.shape[0] // chunk
     per_block = groups // block_count
     step = block // per_block
-    for g in range(groups):
-        picked = jnp.dot(
+    for h in range(0, groups, 2):
+        both = jnp.dot(
             select_ref[...],
-            rows_ref[g * chunk : (g + 1) * chunk, :],
+            jnp.concatenate(
+                [rows_ref[g * chunk : (g + 1) * chunk, :] for g in (h, h + 1)], axis=1
+            ),
             preferred_element_type=jnp.float32,
         ).astype(jnp.bfloat16)
-        other = quarter(picked)
-        b = g // per_block
-        start = (g % per_block) * step
-        for r in range(per_group):
-            part = slice(r * step, (r + 1) * step)
-            values_ref[b, r, start : start + step, :] = picked[part]
-            values_ref[b, r, block + start : block + start + step, :] = other[part]
+        for g in (h, h + 1):
+            picked = both[:, (g - h) * 128 : (g - h + 1) * 128]
+            other = quarter(picked)
+            b = g // per_block
+            start = (g % per_block) * step
+            for r in range(per_group):
+                part = slice(r * step, (r + 1) * step)
+                values_ref[b, r, start : start + step, :] = picked[part]
+                values_ref[b, r, block + start : block + start + step, :] = other[part]
+    table.wait()
     stores = []
     for t in range(block_count):
         sources = [blocks_ref[t, e] for e in range(list_length)]
@@ -153,12 +164,16 @@
                 sums_ref[t * per_block + q, r * step : (r + 1) * step, :] = total[
                     q * step : (q + 1) * step
                 ]
-        for g in range(t * per_block, (t + 1) * per_block):
-            out_ref[g * chunk : (g + 1) * chunk, :] = jnp.dot(
-                spread_ref[...], sums_ref[g], preferred_element_type=jnp.float32
+        for h in range(t * per_block, (t + 1) * per_block, 2):
+            both = jnp.dot(
+                spread_ref[...],
+                jnp.concatenate([sums_ref[h], sums_ref[h + 1]], axis=1),
+                preferred_element_type=jnp.float32,
             ).astype(jnp.bfloat16)
+            for g in (h, h + 1):
+                out_ref[g * chunk : (g + 1) * chunk, :] = both[:, (g - h) * 128 : (g - h + 1) * 128]
         span = slice(t * per_block * chunk, (t + 1) * per_block * chunk)
-        store = pltpu.make_async_copy(out_ref.at[span], out_hbm.at[span], sems.at[t])
+        store = pltpu.make_async_copy(out_ref.at[span], out_hbm.at[span], sems.at[t + 1])
         store.start()
         stores.append(store)
     for store in stores:
@@ -172,13 +187,14 @@
     vmem = pl.BlockSpec(memory_space=pltpu.VMEM)
     return pl.pallas_call(
         translate_kernel,
-        in_specs=[pl.BlockSpec(memory_space=pltpu.SMEM), vmem, vmem, vmem, vmem],
+        in_specs=[pl.BlockSpec(memory_space=pltpu.HBM), vmem, vmem, vmem, vmem],
         out_specs=pl.BlockSpec(memory_space=pltpu.HBM),
         scratch_shapes=[
+            pltpu.SMEM(source_blocks.shape, source_blocks.dtype),
             pltpu.VMEM((block_count, per_group, doubled, 128), jnp.bfloat16),
             pltpu.VMEM((groups, select.shape[0], 128), jnp.bfloat16),
             pltpu.VMEM(rows.shape, jnp.bfloat16),
-            pltpu.SemaphoreType.DMA((block_count,)),
+            pltpu.SemaphoreType.DMA((block_count + 1,)),
         ],
         out_shape=jax.ShapeDtypeStruct(rows.shape, jnp.bfloat16),
         compiler_params=pltpu.CompilerParams(vmem_limit_bytes=32 * MIB),
@@ -248,20 +264,26 @@
 
 
 def absorb_kernel(
-    counts_ref, rows_ref, near_ref, receive_hbm, out_hbm, wide_ref, doubled_ref, receive_ref,
-    fields_ref, fetch_sems, store_sems,
+    counts_hbm, rows_ref, near_ref, receive_hbm, out_hbm, counts_ref, wide_ref, doubled_ref,
+    receive_ref, fields_ref, fetch_sems, store_sems,
 ):
     children, unknowns, doubled = receive_ref.shape
     directions = doubled // 2
     positions = doubled_ref.shape[1] // 128
-    steps = fetch_sems.shape[0]
-    octants = children // steps
+    spans = [slice(sum(SHARES[:q]), sum(SHARES[: q + 1])) for q in range(len(SHARES))]
+    table = pltpu.make_async_copy(counts_hbm, counts_ref, fetch_sems.at[len(SHARES)])
+    table.start()
     parts = []
-    for q in range(steps):
-        span = slice(q * octants, (q + 1) * octants)
+    for q, span in enumerate(spans):
         part = pltpu.make_async_copy(receive_hbm.at[span], receive_ref.at[span], fetch_sems.at[q])
         part.start()
         parts.append(part)
+    wide_ref[...] = rows_ref[...].astype(jnp.float32)
+    for p in range(positions):
+        v = wide_ref[pl.ds(p, directions, stride=positions), :].astype(jnp.bfloat16)
+        doubled_ref[0:directions, p * 128 : (p + 1) * 128] = v
+        doubled_ref[directions:doubled, p * 128 : (p + 1) * 128] = quarter(v)
+    table.wait()
     offset, count = own_range(counts_ref)
     for slot in range(positions):
 
@@ -271,15 +293,11 @@
                 (children, unknowns, 128), jnp.bfloat16
             )
 
-    wide_ref[...] = rows_ref[...].astype(jnp.float32)
-    for p in range(positions):
-        v = wide_ref[pl.ds(p, directions, stride=positions), :].astype(jnp.bfloat16)
-        doubled_ref[0:directions, p * 128 : (p + 1) * 128] = v
-        doubled_ref[directions:doubled, p * 128 : (p + 1) * 128] = quarter(v)
     stores = []
-    for q in range(steps):
+    for q, octants in enumerate(SHARES):
         parts[q].wait()
-        lines = receive_ref[q * octants : (q + 1) * octants].reshape(octants * unknowns, doubled)
+        base = spans[q].start
+        lines = receive_ref[spans[q]].reshape(octants * unknowns, doubled)
         far = jnp.dot(lines, doubled_ref[...], preferred_element_type=jnp.float32)
         for p in range(positions):
             slot = p - offset
@@ -287,12 +305,12 @@
             @pl.when(jnp.logical_and(slot >= 0, slot < count))
             def _():
                 for c in range(octants):
-                    leaf = slot * children + q * octants + c
+                    leaf = slot * children + base + c
                     part = far[c * unknowns : (c + 1) * unknowns, p * 128 : (p + 1) * 128]
                     fields_ref[leaf] = (part + near_ref[leaf]).astype(jnp.bfloat16)
 
         for slot in range(positions):
-            span = pl.ds(slot * children + q * octants, octants)
+            span = pl.ds(slot * children + base, octants)
             store = pltpu.make_async_copy(
                 fields_ref.at[span], out_hbm.at[span], store_sems.at[q, slot]
             )
@@ -305,19 +323,20 @@
 def absorb(counts, rows, receive, near_field):
     children, _, doubled = receive.shape
     positions = near_field.shape[0] // children
-    steps = 4
+    steps = len(SHARES)
     vmem = pl.BlockSpec(memory_space=pltpu.VMEM)
     hbm = pl.BlockSpec(memory_space=pltpu.HBM)
     return pl.pallas_call(
         absorb_kernel,
-        in_specs=[pl.BlockSpec(memory_space=pltpu.SMEM), vmem, vmem, hbm],
+        in_specs=[hbm, vmem, vmem, hbm],
         out_specs=hbm,
         scratch_shapes=[
+            pltpu.SMEM(counts.shape, counts.dtype),
             pltpu.VMEM(rows.shape, jnp.float32),
             pltpu.VMEM((doubled, positions * 128), jnp.bfloat16),
             pltpu.VMEM(receive.shape, receive.dtype),
             pltpu.VMEM(near_field.shape, jnp.bfloat16),
-            pltpu.SemaphoreType.DMA((steps,)),
+            pltpu.SemaphoreType.DMA((steps + 1,)),
             pltpu.SemaphoreType.DMA((steps, positions)),
         ],
         out_shape=jax.ShapeDtypeStruct(near_field.shape, jnp.bfloat16),
@@ -353,7 +372,7 @@
 
     patterns = radiate(in_hbm(counts), in_hbm(currents), in_hbm(aggregate))
     gathered = swap(patterns, positions)
-    incoming = translate(source_blocks, gathered, translations, positions)
+    incoming = translate(in_hbm(source_blocks), gathered, translations, positions)
     returned = swap(incoming, positions)
 
     local, _ = lax.optimization_barrier((local, incoming))

time: 80.6 us -> 79.4 us (0.985)
  Pallas kernels: 29.6 us -> 27.5 us
    pallas_call x2, Pallas kernels: 12.7 us -> 11.1 us  [the longest x1 5.67 us: radiate(): pl.pallas_call(radiate_kernel, in_specs=[hbm, hbm, hbm], out_specs=hbm, s...]
where the time goes in v6:
time: 79.4 us; the launch traced here: 79 us
  waiting for transfers between devices  31.5 us (40%)
  Pallas kernels  27.5 us (35%)
  starting transfers between devices  19.7 us (25%)
    all_to_all x2, waiting for transfers between devices, swap(): return lax.all_to_all(shaped, AXES, 0, 0, tiled=True).reshape(-1, channels)  23.7 us
    all_to_all x2, starting transfers between devices, swap(): return lax.all_to_all(shaped, AXES, 0, 0, tiled=True).reshape(-1, channels)  15.2 us
    pallas_call x1, Pallas kernels, near(): pl.pallas_call(near_kernel, grid_spec=pltpu.PrefetchScalarGridSpec(num_sc...  12.9 us
    ppermute x1, waiting for transfers between devices, body(): partner = lax.ppermute(currents, 'near', outer + [(j, i) for i, j in outer])  7.72 us
    pallas_call x1, Pallas kernels, radiate(): pl.pallas_call(radiate_kernel, in_specs=[hbm, hbm, hbm], out_specs=hbm, s...  5.67 us
    pallas_call x1, Pallas kernels, absorb(): pl.pallas_call(absorb_kernel, in_specs=[hbm, vmem, vmem, hbm], out_specs=...  5.46 us
    pallas_call x1, Pallas kernels, translate(): pl.pallas_call(translate_kernel, in_specs=[pl.BlockSpec(memory_space=pltp...  3.5 us
    ppermute x1, starting transfers between devices, body(): partner = lax.ppermute(currents, 'near', outer + [(j, i) for i, j in outer])  2.9 us
  transfers between devices with their start and end apart: 4, of which 3 were waited for; matrix products, arithmetic and copies ran while one was open for 0% of the time, Pallas kernels for 21%

profile of v6, /device:TPU:1, one launch (start us, length us, event | category | flops | bytes accessed | tf_op | source)
XLA Modules:
  0.0 79.0 jit_solution(13699838338447231096)
XLA Ops:
  0.0 5.7 %radiate.1 = bf16[4608,128]{1,0:T(8,128)(2,1)} custom-call(s32[128]{0:T(128)} %counts_hbm.3, bf16[32,128,128]{2,1,0:T(8,128)(2,1)} %own_ref.1, bf16[8,1152,256]{2,1,0:T(8,128)(2,1)} %aggregate_hbm.1), custom_call_target="tpu_custom_call" | custom-call | tf_op jit(solution)/shard_map/radiate/pallas_call | solution.py:91
  5.7 0.0 copy-start
  5.7 0.0 copy-start.1
  5.7 0.0 copy-start.2
  5.7 11.6 %all-to-all-start = ((bf16[1152,4,128]{2,1,0:T(4,128)(2,1)}), bf16[1152,4,128]{2,1,0:T(4,128)(2,1)S(1)}, u32[]{:S(2)}, u32[]{:S(2)}) async-start(bf16[1152,4,128]{2,1,0:T(4,128)(2,1)} %bitcast), calls=%async_computation | async-start | bytes 2359296 | tf_op jit(solution)/shard_map/all_to_all | solution.py:355
  17.3 1.7 %collective-permute-start = (bf16[32,128,128]{2,1,0:T(8,128)(2,1)}, bf16[32,128,128]{2,1,0:T(8,128)(2,1)}, u32[]{:S(2)}, u32[]{:S(2)}) collective-permute-start(bf16[32,128,128]{2,1,0:T(8,128)(2,1)} %own_ref.1), channel_id=1, source_target_pairs={{1,2},{2,1},{5,6},{6,5},{9,10},{10,9},{13,14},{14,13},{17,18},{18,... | collective-permute-start | bytes 3145736 | tf_op jit(solution)/shard_map/ppermute | solution.py:370
  19.0 2.9 %collective-permute-start.1 = (bf16[32,128,128]{2,1,0:T(8,128)(2,1)}, bf16[32,128,128]{2,1,0:T(8,128)(2,1)}, u32[]{:S(2)}, u32[]{:S(2)}) collective-permute-start(bf16[32,128,128]{2,1,0:T(8,128)(2,1)} %own_ref.1), channel_id=1, source_target_pairs={{0,1},{2,3},{1,0},{3,2},{4,5},{6,7},{5,4},{7,6},{8,9},{10,11},{9,8... | collective-permute-start | bytes 3145736 | tf_op jit(solution)/shard_map/ppermute | solution.py:371
  21.9 17.1 %all-to-all-done = bf16[1152,4,128]{2,1,0:T(4,128)(2,1)S(1)} async-done(((bf16[1152,4,128]{2,1,0:T(4,128)(2,1)}), bf16[1152,4,128]{2,1,0:T(4,128)(2,1)S(1)}, u32[]{:S(2)}, u32[]{:S(2)}) %all-to-all-start) | async-done | bytes 1179680 | tf_op jit(solution)/shard_map/all_to_all | solution.py:355
  38.9 0.0 copy-done
  39.0 0.0 copy-done.1
  39.0 0.0 copy-done.2
  39.0 3.5 %translate.1 = bf16[4608,128]{1,0:T(8,128)(2,1)} custom-call(s32[4,3]{1,0:T(4,128)} %blocks_hbm.1, bf16[4608,128]{1,0:T(8,128)(2,1)S(1)} %bitcast.5, bf16[4,3,9,64,128]{4,3,2,1,0:T(8,128)(2,1)S(1)} %copy-done, bf16[144,288]{1,0:T(8,128)(2,1)S(1)} %copy-done.2, bf16[288,144]{1,0:T(8,128)(2,1)S(1)} %copy-done.1), custom_call_target="tpu_custom_call" | custom-call | tf_op jit(solution)/shard_map/translate/pallas_call | solution.py:188
  42.5 0.0 copy-start.3
  42.5 3.6 %all-to-all-start.1 = ((bf16[1152,4,128]{2,1,0:T(4,128)(2,1)}), bf16[1152,4,128]{2,1,0:T(4,128)(2,1)S(1)}, u32[]{:S(2)}, u32[]{:S(2)}) async-start(bf16[1152,4,128]{2,1,0:T(4,128)(2,1)} %bitcast.2), calls=%async_computation.1 | async-start | bytes 2359296 | tf_op jit(solution)/shard_map/all_to_all | solution.py:355
  46.1 0.0 copy-done.3
  46.1 0.1 copy.11
  46.2 0.1 reshape.19.source_ref
  46.3 0.0 collective-permute-done.across_ref
  46.3 7.7 %collective-permute-done.1.partner_ref = bf16[32,128,128]{2,1,0:T(8,128)(2,1)} collective-permute-done((bf16[32,128,128]{2,1,0:T(8,128)(2,1)}, bf16[32,128,128]{2,1,0:T(8,128)(2,1)}, u32[]{:S(2)}, u32[]{:S(2)}) %collective-permute-start.1) | collective-permute-done | bytes 1048608 | tf_op jit(solution)/shard_map/ppermute | solution.py:371
  54.0 12.9 %near.1.near_ref = f32[32,128,128]{2,1,0:T(8,128)S(1)} custom-call(s32[192]{0:T(256)S(1)} %reshape.19.source_ref, bf16[32,128,128]{2,1,0:T(8,128)(2,1)} %collective-permute-done.across_ref, bf16[32,128,128]{2,1,0:T(8,128)(2,1)} %own_ref.1, bf16[32,128,128]{2,1,0:T(8,128)(2,1)} %collective-permute-done.1.partner_ref, bf16[32,6,128,256]{3,2,1,0:T(8,128)(2,1)} %blocks_ref.1), custom_call_target="tpu_custom_call" | custom-call | flops 10000000000 | bytes 20000000 | tf_op jit(solution)/shard_map/near/pallas_call | solution.py:245
  66.9 6.7 %all-to-all-done.1 = bf16[1152,4,128]{2,1,0:T(4,128)(2,1)S(1)} async-done(((bf16[1152,4,128]{2,1,0:T(4,128)(2,1)}), bf16[1152,4,128]{2,1,0:T(4,128)(2,1)S(1)}, u32[]{:S(2)}, u32[]{:S(2)}) %all-to-all-start.1) | async-done | bytes 1179680 | tf_op jit(solution)/shard_map/all_to_all | solution.py:355
  73.6 5.5 %absorb.1 = bf16[32,128,128]{2,1,0:T(8,128)(2,1)} custom-call(s32[128]{0:T(128)} %counts_hbm.3, bf16[4608,128]{1,0:T(8,128)(2,1)S(1)} %bitcast.4, f32[32,128,128]{2,1,0:T(8,128)S(1)} %near.1.near_ref, bf16[8,128,2304]{2,1,0:T(8,128)(2,1)} %receive_hbm.1), custom_call_target="tpu_custom_call" | custom-call | tf_op jit(solution)/shard_map/absorb/pallas_call | solution.py:329
  (1 shorter events, 0.0 us)
Async XLA Ops:
  5.7 33.3 %copy-start = (bf16[4,3,9,64,128]{4,3,2,1,0:T(8,128)(2,1)S(1)}, bf16[4,3,9,64,128]{4,3,2,1,0:T(8,128)(2,1)}, u32[]{:S(2)}) copy-start(bf16[4,3,9,64,128]{4,3,2,1,0:T(8,128)(2,1)} %translations_ref.1) | copy-start | bytes 5308420
  5.7 33.3 %copy-start.1 = (bf16[288,144]{1,0:T(8,128)(2,1)S(1)}, bf16[288,144]{1,0:T(8,128)(2,1)}, u32[]{:S(2)}) copy-start(bf16[288,144]{1,0:T(8,128)(2,1)} %constant.48.clone.spread_ref) | copy-start | bytes 248836
  5.7 33.3 %copy-start.2 = (bf16[144,288]{1,0:T(8,128)(2,1)S(1)}, bf16[144,288]{1,0:T(8,128)(2,1)}, u32[]{:S(2)}) copy-start(bf16[144,288]{1,0:T(8,128)(2,1)} %constant.47.clone.select_ref) | copy-start | bytes 248836
  5.7 33.2 %all-to-all-start = ((bf16[1152,4,128]{2,1,0:T(4,128)(2,1)}), bf16[1152,4,128]{2,1,0:T(4,128)(2,1)S(1)}, u32[]{:S(2)}, u32[]{:S(2)}) async-start(bf16[1152,4,128]{2,1,0:T(4,128)(2,1)} %bitcast), calls=%async_computation | async-start | bytes 2359296 | tf_op jit(solution)/shard_map/all_to_all | solution.py:355
  17.3 29.0 %collective-permute-start = (bf16[32,128,128]{2,1,0:T(8,128)(2,1)}, bf16[32,128,128]{2,1,0:T(8,128)(2,1)}, u32[]{:S(2)}, u32[]{:S(2)}) collective-permute-start(bf16[32,128,128]{2,1,0:T(8,128)(2,1)} %own_ref.1), channel_id=1, source_target_pairs={{1,2},{2,1},{5,6},{6,5},{9,10},{10,9},{13,14},{14,13},{17,18},{18,... | collective-permute-start | bytes 3145736 | tf_op jit(solution)/shard_map/ppermute | solution.py:370
  19.0 35.0 %collective-permute-start.1 = (bf16[32,128,128]{2,1,0:T(8,128)(2,1)}, bf16[32,128,128]{2,1,0:T(8,128)(2,1)}, u32[]{:S(2)}, u32[]{:S(2)}) collective-permute-start(bf16[32,128,128]{2,1,0:T(8,128)(2,1)} %own_ref.1), channel_id=1, source_target_pairs={{0,1},{2,3},{1,0},{3,2},{4,5},{6,7},{5,4},{7,6},{8,9},{10,11},{9,8... | collective-permute-start | bytes 3145736 | tf_op jit(solution)/shard_map/ppermute | solution.py:371
  42.5 3.6 %copy-start.3 = (s32[32,6]{0,1:T(8,128)S(1)}, s32[32,6]{0,1:T(8,128)}, u32[]{:S(2)}) copy-start(s32[32,6]{0,1:T(8,128)} %param.12) | copy-start | bytes 2308
  42.5 31.1 %all-to-all-start.1 = ((bf16[1152,4,128]{2,1,0:T(4,128)(2,1)}), bf16[1152,4,128]{2,1,0:T(4,128)(2,1)S(1)}, u32[]{:S(2)}, u32[]{:S(2)}) async-start(bf16[1152,4,128]{2,1,0:T(4,128)(2,1)} %bitcast.2), calls=%async_computation.1 | async-start | bytes 2359296 | tf_op jit(solution)/shard_map/all_to_all | solution.py:355

commit v7 on v6

--- a/solution.py
+++ b/solution.py
@@ -10,6 +10,7 @@
 MIB = 1 << 20
 SPLITS = (288, 288, 288, 288)
 SHARES = (2, 2, 4)
+HELD = 2
 
 
 def quarter(v):
@@ -103,7 +104,7 @@
             pltpu.SemaphoreType.DMA((tiles,)),
         ],
         out_shape=jax.ShapeDtypeStruct((directions * positions, 128), jnp.bfloat16),
-        compiler_params=pltpu.CompilerParams(vmem_limit_bytes=40 * MIB),
+        compiler_params=pltpu.CompilerParams(vmem_limit_bytes=28 * MIB),
         name="radiate",
     )(counts, currents, aggregate)
 
@@ -197,7 +198,7 @@
             pltpu.SemaphoreType.DMA((block_count + 1,)),
         ],
         out_shape=jax.ShapeDtypeStruct(rows.shape, jnp.bfloat16),
-        compiler_params=pltpu.CompilerParams(vmem_limit_bytes=32 * MIB),
+        compiler_params=pltpu.CompilerParams(vmem_limit_bytes=16 * MIB),
         name="translate",
     )(
         source_blocks,
@@ -208,14 +209,19 @@
     )
 
 
-def near_kernel(source_ref, across_ref, own_ref, partner_ref, blocks_ref, out_ref, window_ref):
+def near_kernel(
+    source_ref, across_ref, own_ref, partner_ref, blocks_ref, receive_hbm, out_ref, held_ref,
+    window_ref, sem,
+):
     slots = own_ref.shape[0]
     unknowns = own_ref.shape[1]
     leaves, terms = blocks_ref.shape[:2]
     first = pl.program_id(0) * leaves
+    hold = pltpu.make_async_copy(receive_hbm.at[0:HELD], held_ref, sem)
 
     @pl.when(first == 0)
     def _():
+        hold.start()
         for part, ref in enumerate((across_ref, own_ref, partner_ref)):
 
             def fill(i, carry, part=part, ref=ref):
@@ -234,10 +240,14 @@
             jnp.concatenate([blocks_ref[i, e] for e in range(terms)], axis=1),
             jnp.concatenate([window_ref[source] for source in sources], axis=0),
             preferred_element_type=jnp.float32,
-        )
-
-
-def near(source, across, own, partner, blocks):
+        ).astype(jnp.bfloat16)
+
+    @pl.when(first == slots - leaves)
+    def _():
+        hold.wait()
+
+
+def near(source, across, own, partner, blocks, receive):
     slots, unknowns, channels = own.shape
     _, terms, _, doubled = blocks.shape
     leaves = 4
@@ -252,30 +262,43 @@
                 whole,
                 whole,
                 pl.BlockSpec((leaves, terms, unknowns, doubled), lambda i, _: (i, 0, 0, 0)),
+                pl.BlockSpec(memory_space=pltpu.HBM),
             ],
-            out_specs=pl.BlockSpec((leaves, unknowns, channels), lambda i, _: (i, 0, 0)),
-            scratch_shapes=[pltpu.VMEM((3 * slots, doubled, channels), jnp.bfloat16)],
+            out_specs=[
+                pl.BlockSpec((leaves, unknowns, channels), lambda i, _: (i, 0, 0)),
+                pl.BlockSpec(memory_space=pl.ANY),
+            ],
+            scratch_shapes=[
+                pltpu.VMEM((3 * slots, doubled, channels), jnp.bfloat16),
+                pltpu.SemaphoreType.DMA,
+            ],
         ),
-        out_shape=jax.ShapeDtypeStruct((slots, unknowns, channels), jnp.float32),
-        compiler_params=pltpu.CompilerParams(vmem_limit_bytes=40 * MIB),
+        out_shape=[
+            jax.ShapeDtypeStruct((slots, unknowns, channels), jnp.bfloat16),
+            jax.ShapeDtypeStruct((HELD,) + receive.shape[1:], receive.dtype),
+        ],
+        compiler_params=pltpu.CompilerParams(vmem_limit_bytes=28 * MIB),
         cost_estimate=pl.CostEstimate(flops=10**10, transcendentals=0, bytes_accessed=2 * 10**7),
         name="near",
-    )(source.reshape(-1), across, own, partner, blocks)
+    )(source.reshape(-1), across, own, partner, blocks, receive)
 
 
 def absorb_kernel(
-    counts_hbm, rows_ref, near_ref, receive_hbm, out_hbm, counts_ref, wide_ref, doubled_ref,
-    receive_ref, fields_ref, fetch_sems, store_sems,
+    counts_hbm, rows_ref, near_ref, held_ref, receive_hbm, out_hbm, counts_ref, wide_ref,
+    doubled_ref, receive_ref, fields_ref, fetch_sems, store_sems,
 ):
-    children, unknowns, doubled = receive_ref.shape
+    children, unknowns, doubled = receive_hbm.shape
     directions = doubled // 2
     positions = doubled_ref.shape[1] // 128
     spans = [slice(sum(SHARES[:q]), sum(SHARES[: q + 1])) for q in range(len(SHARES))]
-    table = pltpu.make_async_copy(counts_hbm, counts_ref, fetch_sems.at[len(SHARES)])
+    table = pltpu.make_async_copy(counts_hbm, counts_ref, fetch_sems.at[0])
     table.start()
-    parts = []
-    for q, span in enumerate(spans):
-        part = pltpu.make_async_copy(receive_hbm.at[span], receive_ref.at[span], fetch_sems.at[q])
+    parts = [None]
+    for q in range(1, len(SHARES)):
+        span = slice(spans[q].start - HELD, spans[q].stop - HELD)
+        part = pltpu.make_async_copy(
+            receive_hbm.at[spans[q]], receive_ref.at[span], fetch_sems.at[q]
+        )
         part.start()
         parts.append(part)
     wide_ref[...] = rows_ref[...].astype(jnp.float32)
@@ -295,9 +318,11 @@
 
     stores = []
     for q, octants in enumerate(SHARES):
-        parts[q].wait()
         base = spans[q].start
-        lines = receive_ref[spans[q]].reshape(octants * unknowns, doubled)
+        if q:
+            parts[q].wait()
+        held = receive_ref[base - HELD : base - HELD + octants] if q else held_ref[...]
+        lines = held.reshape(octants * unknowns, doubled)
         far = jnp.dot(lines, doubled_ref[...], preferred_element_type=jnp.float32)
         for p in range(positions):
             slot = p - offset
@@ -320,7 +345,7 @@
         store.wait()
 
 
-def absorb(counts, rows, receive, near_field):
+def absorb(counts, rows, held, receive, near_field):
     children, _, doubled = receive.shape
     positions = near_field.shape[0] // children
     steps = len(SHARES)
@@ -328,21 +353,21 @@
     hbm = pl.BlockSpec(memory_space=pltpu.HBM)
     return pl.pallas_call(
         absorb_kernel,
-        in_specs=[hbm, vmem, vmem, hbm],
+        in_specs=[hbm, vmem, vmem, vmem, hbm],
         out_specs=hbm,
         scratch_shapes=[
             pltpu.SMEM(counts.shape, counts.dtype),
             pltpu.VMEM(rows.shape, jnp.float32),
             pltpu.VMEM((doubled, positions * 128), jnp.bfloat16),
-            pltpu.VMEM(receive.shape, receive.dtype),
+            pltpu.VMEM((children - HELD,) + receive.shape[1:], receive.dtype),
             pltpu.VMEM(near_field.shape, jnp.bfloat16),
-            pltpu.SemaphoreType.DMA((steps + 1,)),
+            pltpu.SemaphoreType.DMA((steps,)),
             pltpu.SemaphoreType.DMA((steps, positions)),
         ],
         out_shape=jax.ShapeDtypeStruct(near_field.shape, jnp.bfloat16),
-        compiler_params=pltpu.CompilerParams(vmem_limit_bytes=48 * MIB),
+        compiler_params=pltpu.CompilerParams(vmem_limit_bytes=24 * MIB),
         name="absorb",
-    )(counts, rows, near_field, receive)
+    )(counts, rows, near_field, held, receive)
 
 
 def in_hbm(array):
@@ -376,8 +401,10 @@
     returned = swap(incoming, positions)
 
     local, _ = lax.optimization_barrier((local, incoming))
-    near_field = near(local, across, in_hbm(currents), partner, in_hbm(near_blocks))
-    return absorb(in_hbm(counts), returned, in_hbm(receive), near_field)
+    near_field, held = near(
+        local, across, in_hbm(currents), partner, in_hbm(near_blocks), in_hbm(receive)
+    )
+    return absorb(in_hbm(counts), returned, held, in_hbm(receive), near_field)
 
 
 def solution(mesh):

time: 79.4 us -> 78.6 us (0.990)
  no operation moved by 1% of the time
where the time goes in v7:
time: 78.6 us; the launch traced here: 78.4 us
  waiting for transfers between devices  31.5 us (40%)
  Pallas kernels  26.8 us (34%)
  starting transfers between devices  19.7 us (25%)
    all_to_all x2, waiting for transfers between devices, swap(): return lax.all_to_all(shaped, AXES, 0, 0, tiled=True).reshape(-1, channels)  23.7 us
    all_to_all x2, starting transfers between devices, swap(): return lax.all_to_all(shaped, AXES, 0, 0, tiled=True).reshape(-1, channels)  15.2 us
    pallas_call x1, Pallas kernels, near(): pl.pallas_call(near_kernel, grid_spec=pltpu.PrefetchScalarGridSpec(num_sc...  12.9 us
    ppermute x1, waiting for transfers between devices, body(): partner = lax.ppermute(currents, 'near', outer + [(j, i) for i, j in outer])  7.74 us
    pallas_call x1, Pallas kernels, radiate(): pl.pallas_call(radiate_kernel, in_specs=[hbm, hbm, hbm], out_specs=hbm, s...  5.74 us
    pallas_call x1, Pallas kernels, absorb(): pl.pallas_call(absorb_kernel, in_specs=[hbm, vmem, vmem, vmem, hbm], out_...  4.73 us
    pallas_call x1, Pallas kernels, translate(): pl.pallas_call(translate_kernel, in_specs=[pl.BlockSpec(memory_space=pltp...  3.47 us
    ppermute x1, starting transfers between devices, body(): partner = lax.ppermute(currents, 'near', outer + [(j, i) for i, j in outer])  2.9 us
  transfers between devices with their start and end apart: 4, of which 3 were waited for; matrix products, arithmetic and copies ran while one was open for 0% of the time, Pallas kernels for 21%

profile of v7, /device:TPU:1, one launch (start us, length us, event | category | flops | bytes accessed | tf_op | source)
XLA Modules:
  0.0 78.4 jit_solution(8435472292083173844)
XLA Ops:
  0.0 5.7 %radiate.1 = bf16[4608,128]{1,0:T(8,128)(2,1)} custom-call(s32[128]{0:T(128)} %counts_hbm.3, bf16[32,128,128]{2,1,0:T(8,128)(2,1)} %own_ref.1, bf16[8,1152,256]{2,1,0:T(8,128)(2,1)} %aggregate_hbm.1), custom_call_target="tpu_custom_call" | custom-call | tf_op jit(solution)/shard_map/radiate/pallas_call | solution.py:92
  5.7 0.0 copy-start
  5.8 0.0 copy-start.1
  5.8 0.0 copy-start.2
  5.8 11.6 %all-to-all-start = ((bf16[1152,4,128]{2,1,0:T(4,128)(2,1)}), bf16[1152,4,128]{2,1,0:T(4,128)(2,1)S(1)}, u32[]{:S(2)}, u32[]{:S(2)}) async-start(bf16[1152,4,128]{2,1,0:T(4,128)(2,1)} %bitcast), calls=%async_computation | async-start | bytes 2359296 | tf_op jit(solution)/shard_map/all_to_all | solution.py:380
  17.4 1.7 %collective-permute-start = (bf16[32,128,128]{2,1,0:T(8,128)(2,1)}, bf16[32,128,128]{2,1,0:T(8,128)(2,1)}, u32[]{:S(2)}, u32[]{:S(2)}) collective-permute-start(bf16[32,128,128]{2,1,0:T(8,128)(2,1)} %own_ref.1), channel_id=1, source_target_pairs={{1,2},{2,1},{5,6},{6,5},{9,10},{10,9},{13,14},{14,13},{17,18},{18,... | collective-permute-start | bytes 3145736 | tf_op jit(solution)/shard_map/ppermute | solution.py:395
  19.0 2.9 %collective-permute-start.1 = (bf16[32,128,128]{2,1,0:T(8,128)(2,1)}, bf16[32,128,128]{2,1,0:T(8,128)(2,1)}, u32[]{:S(2)}, u32[]{:S(2)}) collective-permute-start(bf16[32,128,128]{2,1,0:T(8,128)(2,1)} %own_ref.1), channel_id=1, source_target_pairs={{0,1},{2,3},{1,0},{3,2},{4,5},{6,7},{5,4},{7,6},{8,9},{10,11},{9,8... | collective-permute-start | bytes 3145736 | tf_op jit(solution)/shard_map/ppermute | solution.py:396
  21.9 17.1 %all-to-all-done = bf16[1152,4,128]{2,1,0:T(4,128)(2,1)S(1)} async-done(((bf16[1152,4,128]{2,1,0:T(4,128)(2,1)}), bf16[1152,4,128]{2,1,0:T(4,128)(2,1)S(1)}, u32[]{:S(2)}, u32[]{:S(2)}) %all-to-all-start) | async-done | bytes 1179680 | tf_op jit(solution)/shard_map/all_to_all | solution.py:380
  39.0 0.0 copy-done
  39.0 0.0 copy-done.1
  39.0 0.0 copy-done.2
  39.0 3.5 %translate.1 = bf16[4608,128]{1,0:T(8,128)(2,1)} custom-call(s32[4,3]{1,0:T(4,128)} %blocks_hbm.1, bf16[4608,128]{1,0:T(8,128)(2,1)S(1)} %bitcast.5, bf16[4,3,9,64,128]{4,3,2,1,0:T(8,128)(2,1)S(1)} %copy-done, bf16[144,288]{1,0:T(8,128)(2,1)S(1)} %copy-done.2, bf16[288,144]{1,0:T(8,128)(2,1)S(1)} %copy-done.1), custom_call_target="tpu_custom_call" | custom-call | tf_op jit(solution)/shard_map/translate/pallas_call | solution.py:189
  42.5 0.0 copy-start.3
  42.5 3.6 %all-to-all-start.1 = ((bf16[1152,4,128]{2,1,0:T(4,128)(2,1)}), bf16[1152,4,128]{2,1,0:T(4,128)(2,1)S(1)}, u32[]{:S(2)}, u32[]{:S(2)}) async-start(bf16[1152,4,128]{2,1,0:T(4,128)(2,1)} %bitcast.2), calls=%async_computation.1 | async-start | bytes 2359296 | tf_op jit(solution)/shard_map/all_to_all | solution.py:380
  46.1 0.0 copy-done.3
  46.1 0.1 copy.11
  46.2 0.1 reshape.19.source_ref
  46.3 0.0 collective-permute-done.across_ref
  46.3 7.7 %collective-permute-done.1.partner_ref = bf16[32,128,128]{2,1,0:T(8,128)(2,1)} collective-permute-done((bf16[32,128,128]{2,1,0:T(8,128)(2,1)}, bf16[32,128,128]{2,1,0:T(8,128)(2,1)}, u32[]{:S(2)}, u32[]{:S(2)}) %collective-permute-start.1) | collective-permute-done | bytes 1048608 | tf_op jit(solution)/shard_map/ppermute | solution.py:396
  54.1 12.9 %near.1 = (bf16[32,128,128]{2,1,0:T(8,128)(2,1)S(1)}, bf16[2,128,2304]{2,1,0:T(8,128)(2,1)S(1)}) custom-call(s32[192]{0:T(256)S(1)} %reshape.19.source_ref, bf16[32,128,128]{2,1,0:T(8,128)(2,1)} %collective-permute-done.across_ref, bf16[32,128,128]{2,1,0:T(8,128)(2,1)} %own_ref.1, bf16[32,128,128]{2,1,0:T(8,128)(2,1)} %collective-permute-done.1.partner_ref, ...), custom_call_target="tpu_custom_call" | custom-call | flops 10000000000 | bytes 20000000 | tf_op jit(solution)/shard_map/near/pallas_call | solution.py:255
  67.0 6.7 %all-to-all-done.1 = bf16[1152,4,128]{2,1,0:T(4,128)(2,1)S(1)} async-done(((bf16[1152,4,128]{2,1,0:T(4,128)(2,1)}), bf16[1152,4,128]{2,1,0:T(4,128)(2,1)S(1)}, u32[]{:S(2)}, u32[]{:S(2)}) %all-to-all-start.1) | async-done | bytes 1179680 | tf_op jit(solution)/shard_map/all_to_all | solution.py:380
  73.6 4.7 %absorb.1 = bf16[32,128,128]{2,1,0:T(8,128)(2,1)} custom-call(s32[128]{0:T(128)} %counts_hbm.3, bf16[4608,128]{1,0:T(8,128)(2,1)S(1)} %bitcast.4, bf16[32,128,128]{2,1,0:T(8,128)(2,1)S(1)} %get-tuple-element.9.near_ref, bf16[2,128,2304]{2,1,0:T(8,128)(2,1)S(1)} %get-tuple-element.10.held_ref, bf16[8,128,2304]{2,1,0:T(8,128)(2,1)} %receive_hbm.3), custom_call_target="tpu_custom_call" | custom-call | tf_op jit(solution)/shard_map/absorb/pallas_call | solution.py:354
  (1 shorter events, 0.0 us)
Async XLA Ops:
  5.7 33.3 %copy-start = (bf16[4,3,9,64,128]{4,3,2,1,0:T(8,128)(2,1)S(1)}, bf16[4,3,9,64,128]{4,3,2,1,0:T(8,128)(2,1)}, u32[]{:S(2)}) copy-start(bf16[4,3,9,64,128]{4,3,2,1,0:T(8,128)(2,1)} %translations_ref.1) | copy-start | bytes 5308420
  5.8 33.3 %copy-start.1 = (bf16[288,144]{1,0:T(8,128)(2,1)S(1)}, bf16[288,144]{1,0:T(8,128)(2,1)}, u32[]{:S(2)}) copy-start(bf16[288,144]{1,0:T(8,128)(2,1)} %constant.48.clone.spread_ref) | copy-start | bytes 248836
  5.8 33.2 %copy-start.2 = (bf16[144,288]{1,0:T(8,128)(2,1)S(1)}, bf16[144,288]{1,0:T(8,128)(2,1)}, u32[]{:S(2)}) copy-start(bf16[144,288]{1,0:T(8,128)(2,1)} %constant.47.clone.select_ref) | copy-start | bytes 248836
  5.8 33.2 %all-to-all-start = ((bf16[1152,4,128]{2,1,0:T(4,128)(2,1)}), bf16[1152,4,128]{2,1,0:T(4,128)(2,1)S(1)}, u32[]{:S(2)}, u32[]{:S(2)}) async-start(bf16[1152,4,128]{2,1,0:T(4,128)(2,1)} %bitcast), calls=%async_computation | async-start | bytes 2359296 | tf_op jit(solution)/shard_map/all_to_all | solution.py:380
  17.4 29.0 %collective-permute-start = (bf16[32,128,128]{2,1,0:T(8,128)(2,1)}, bf16[32,128,128]{2,1,0:T(8,128)(2,1)}, u32[]{:S(2)}, u32[]{:S(2)}) collective-permute-start(bf16[32,128,128]{2,1,0:T(8,128)(2,1)} %own_ref.1), channel_id=1, source_target_pairs={{1,2},{2,1},{5,6},{6,5},{9,10},{10,9},{13,14},{14,13},{17,18},{18,... | collective-permute-start | bytes 3145736 | tf_op jit(solution)/shard_map/ppermute | solution.py:395
  19.0 35.0 %collective-permute-start.1 = (bf16[32,128,128]{2,1,0:T(8,128)(2,1)}, bf16[32,128,128]{2,1,0:T(8,128)(2,1)}, u32[]{:S(2)}, u32[]{:S(2)}) collective-permute-start(bf16[32,128,128]{2,1,0:T(8,128)(2,1)} %own_ref.1), channel_id=1, source_target_pairs={{0,1},{2,3},{1,0},{3,2},{4,5},{6,7},{5,4},{7,6},{8,9},{10,11},{9,8... | collective-permute-start | bytes 3145736 | tf_op jit(solution)/shard_map/ppermute | solution.py:396
  42.5 3.6 %copy-start.3 = (s32[32,6]{0,1:T(8,128)S(1)}, s32[32,6]{0,1:T(8,128)}, u32[]{:S(2)}) copy-start(s32[32,6]{0,1:T(8,128)} %param.12) | copy-start | bytes 2308
  42.5 31.1 %all-to-all-start.1 = ((bf16[1152,4,128]{2,1,0:T(4,128)(2,1)}), bf16[1152,4,128]{2,1,0:T(4,128)(2,1)S(1)}, u32[]{:S(2)}, u32[]{:S(2)}) async-start(bf16[1152,4,128]{2,1,0:T(4,128)(2,1)} %bitcast.2), calls=%async_computation.1 | async-start | bytes 2359296 | tf_op jit(solution)/shard_map/all_to_all | solution.py:380

commit v8 on v7

--- a/solution.py
+++ b/solution.py
@@ -8,7 +8,8 @@
 
 AXES = ("dir", "near")
 MIB = 1 << 20
-SPLITS = (288, 288, 288, 288)
+SPLITS = (4, 4)
+TILE = 288
 SHARES = (2, 2, 4)
 HELD = 2
 
@@ -27,20 +28,20 @@
 
 def radiate_kernel(
     counts_hbm, currents_hbm, aggregate_hbm, out_hbm, counts_ref, currents_ref, aggregate_ref,
-    stacked_ref, rows_ref, out_ref, sems, store_sems,
+    stacked_ref, sums_ref, rows_ref, out_ref, sems, store_sems,
 ):
     children, directions, width = aggregate_ref.shape
     unknowns = width // 2
     positions = stacked_ref.shape[1] // 128
-    tiles = [slice(sum(SPLITS[:i]), sum(SPLITS[: i + 1])) for i in range(len(SPLITS))]
-    table = pltpu.make_async_copy(counts_hbm, counts_ref, sems.at[len(tiles) + 1])
+    shares = [slice(sum(SPLITS[:i]), sum(SPLITS[: i + 1])) for i in range(len(SPLITS))]
+    table = pltpu.make_async_copy(counts_hbm, counts_ref, sems.at[len(shares) + 1])
     table.start()
-    own = pltpu.make_async_copy(currents_hbm, currents_ref, sems.at[len(tiles)])
+    own = pltpu.make_async_copy(currents_hbm, currents_ref, sems.at[len(shares)])
     own.start()
     parts = []
-    for i, rows in enumerate(tiles):
+    for i, share in enumerate(shares):
         part = pltpu.make_async_copy(
-            aggregate_hbm.at[:, rows, :], aggregate_ref.at[:, rows, :], sems.at[i]
+            aggregate_hbm.at[share], aggregate_ref.at[share], sems.at[i]
         )
         part.start()
         parts.append(part)
@@ -65,21 +66,29 @@
             stacked_ref[:, lanes] = jnp.zeros((children * width, 128), jnp.bfloat16)
 
     stores = []
-    for i, rows in enumerate(tiles):
+    for i, share in enumerate(shares):
         parts[i].wait()
-        tile = SPLITS[i]
-        total = jnp.dot(
-            jnp.concatenate([aggregate_ref[c, rows, :] for c in range(children)], axis=1),
-            stacked_ref[...],
-            preferred_element_type=jnp.float32,
-        )
-        for p in range(positions):
-            rows_ref[pl.ds(p, tile, stride=positions), :] = total[:, p * 128 : (p + 1) * 128]
-        span = slice(rows.start * positions, rows.stop * positions)
-        out_ref[span, :] = rows_ref[0 : tile * positions, :].astype(jnp.bfloat16)
-        store = pltpu.make_async_copy(out_ref.at[span], out_hbm.at[span], store_sems.at[i])
-        store.start()
-        stores.append(store)
+        for t in range(directions // TILE):
+            rows = slice(t * TILE, (t + 1) * TILE)
+            total = jnp.dot(
+                jnp.concatenate(
+                    [aggregate_ref[c, rows, :] for c in range(share.start, share.stop)], axis=1
+                ),
+                stacked_ref[share.start * width : share.stop * width, :],
+                preferred_element_type=jnp.float32,
+            )
+            if i:
+                total += sums_ref[rows, :]
+            if i + 1 < len(shares):
+                sums_ref[rows, :] = total
+                continue
+            for p in range(positions):
+                rows_ref[pl.ds(p, TILE, stride=positions), :] = total[:, p * 128 : (p + 1) * 128]
+            span = slice(t * TILE * positions, (t + 1) * TILE * positions)
+            out_ref[span, :] = rows_ref[...].astype(jnp.bfloat16)
+            store = pltpu.make_async_copy(out_ref.at[span], out_hbm.at[span], store_sems.at[t])
+            store.start()
+            stores.append(store)
     for store in stores:
         store.wait()
 
@@ -87,7 +96,7 @@
 def radiate(counts, currents, aggregate):
     children, directions, width = aggregate.shape
     positions = currents.shape[0] // children
-    tiles = len(SPLITS)
+    tiles = directions // TILE
     hbm = pl.BlockSpec(memory_space=pltpu.HBM)
     return pl.pallas_call(
         radiate_kernel,
@@ -98,9 +107,10 @@
             pltpu.VMEM(currents.shape, currents.dtype),
             pltpu.VMEM(aggregate.shape, aggregate.dtype),
             pltpu.VMEM((children * width, positions * 128), jnp.bfloat16),
-            pltpu.VMEM((max(SPLITS) * positions, 128), jnp.float32),
+            pltpu.VMEM((directions, positions * 128), jnp.float32),
+            pltpu.VMEM((TILE * positions, 128), jnp.float32),
             pltpu.VMEM((directions * positions, 128), jnp.bfloat16),
-            pltpu.SemaphoreType.DMA((tiles + 2,)),
+            pltpu.SemaphoreType.DMA((len(SPLITS) + 2,)),
             pltpu.SemaphoreType.DMA((tiles,)),
         ],
         out_shape=jax.ShapeDtypeStruct((directions * positions, 128), jnp.bfloat16),

time: 78.6 us -> 78.5 us (level)
  no operation moved by 1% of the time
where the time goes in v8:
time: 78.5 us; the launch traced here: 78.1 us
  waiting for transfers between devices  31.5 us (40%)
  Pallas kernels  26.7 us (34%)
  starting transfers between devices  19.6 us (25%)
    all_to_all x2, waiting for transfers between devices, swap(): return lax.all_to_all(shaped, AXES, 0, 0, tiled=True).reshape(-1, channels)  23.7 us
    all_to_all x2, starting transfers between devices, swap(): return lax.all_to_all(shaped, AXES, 0, 0, tiled=True).reshape(-1, channels)  15.1 us
    pallas_call x1, Pallas kernels, near(): pl.pallas_call(near_kernel, grid_spec=pltpu.PrefetchScalarGridSpec(num_sc...  12.9 us
    ppermute x1, waiting for transfers between devices, body(): partner = lax.ppermute(currents, 'near', outer + [(j, i) for i, j in outer])  7.73 us
    pallas_call x1, Pallas kernels, radiate(): pl.pallas_call(radiate_kernel, in_specs=[hbm, hbm, hbm], out_specs=hbm, s...  5.57 us
    pallas_call x1, Pallas kernels, absorb(): pl.pallas_call(absorb_kernel, in_specs=[hbm, vmem, vmem, vmem, hbm], out_...  4.71 us
    pallas_call x1, Pallas kernels, translate(): pl.pallas_call(translate_kernel, in_specs=[pl.BlockSpec(memory_space=pltp...  3.48 us
    ppermute x1, starting transfers between devices, body(): partner = lax.ppermute(currents, 'near', outer + [(j, i) for i, j in outer])  2.9 us
  transfers between devices with their start and end apart: 4, of which 3 were waited for; matrix products, arithmetic and copies ran while one was open for 0% of the time, Pallas kernels for 21%

profile of v8, /device:TPU:1, one launch (start us, length us, event | category | flops | bytes accessed | tf_op | source)
XLA Modules:
  0.0 78.1 jit_solution(16948201208334004836)
XLA Ops:
  0.0 5.6 %radiate.1 = bf16[4608,128]{1,0:T(8,128)(2,1)} custom-call(s32[128]{0:T(128)} %counts_hbm.3, bf16[32,128,128]{2,1,0:T(8,128)(2,1)} %own_ref.1, bf16[8,1152,256]{2,1,0:T(8,128)(2,1)} %aggregate_hbm.1), custom_call_target="tpu_custom_call" | custom-call | tf_op jit(solution)/shard_map/radiate/pallas_call | solution.py:101
  5.6 0.0 copy-start
  5.6 0.0 copy-start.1
  5.6 0.0 copy-start.2
  5.6 11.5 %all-to-all-start = ((bf16[1152,4,128]{2,1,0:T(4,128)(2,1)}), bf16[1152,4,128]{2,1,0:T(4,128)(2,1)S(1)}, u32[]{:S(2)}, u32[]{:S(2)}) async-start(bf16[1152,4,128]{2,1,0:T(4,128)(2,1)} %bitcast), calls=%async_computation | async-start | bytes 2359296 | tf_op jit(solution)/shard_map/all_to_all | solution.py:390
  17.1 1.7 %collective-permute-start = (bf16[32,128,128]{2,1,0:T(8,128)(2,1)}, bf16[32,128,128]{2,1,0:T(8,128)(2,1)}, u32[]{:S(2)}, u32[]{:S(2)}) collective-permute-start(bf16[32,128,128]{2,1,0:T(8,128)(2,1)} %own_ref.1), channel_id=1, source_target_pairs={{1,2},{2,1},{5,6},{6,5},{9,10},{10,9},{13,14},{14,13},{17,18},{18,... | collective-permute-start | bytes 3145736 | tf_op jit(solution)/shard_map/ppermute | solution.py:405
  18.8 2.9 %collective-permute-start.1 = (bf16[32,128,128]{2,1,0:T(8,128)(2,1)}, bf16[32,128,128]{2,1,0:T(8,128)(2,1)}, u32[]{:S(2)}, u32[]{:S(2)}) collective-permute-start(bf16[32,128,128]{2,1,0:T(8,128)(2,1)} %own_ref.1), channel_id=1, source_target_pairs={{0,1},{2,3},{1,0},{3,2},{4,5},{6,7},{5,4},{7,6},{8,9},{10,11},{9,8... | collective-permute-start | bytes 3145736 | tf_op jit(solution)/shard_map/ppermute | solution.py:406
  21.7 17.1 %all-to-all-done = bf16[1152,4,128]{2,1,0:T(4,128)(2,1)S(1)} async-done(((bf16[1152,4,128]{2,1,0:T(4,128)(2,1)}), bf16[1152,4,128]{2,1,0:T(4,128)(2,1)S(1)}, u32[]{:S(2)}, u32[]{:S(2)}) %all-to-all-start) | async-done | bytes 1179680 | tf_op jit(solution)/shard_map/all_to_all | solution.py:390
  38.8 0.0 copy-done
  38.8 0.0 copy-done.1
  38.8 0.0 copy-done.2
  38.8 3.5 %translate.1 = bf16[4608,128]{1,0:T(8,128)(2,1)} custom-call(s32[4,3]{1,0:T(4,128)} %blocks_hbm.1, bf16[4608,128]{1,0:T(8,128)(2,1)S(1)} %bitcast.5, bf16[4,3,9,64,128]{4,3,2,1,0:T(8,128)(2,1)S(1)} %copy-done, bf16[144,288]{1,0:T(8,128)(2,1)S(1)} %copy-done.2, bf16[288,144]{1,0:T(8,128)(2,1)S(1)} %copy-done.1), custom_call_target="tpu_custom_call" | custom-call | tf_op jit(solution)/shard_map/translate/pallas_call | solution.py:199
  42.3 0.0 copy-start.3
  42.3 3.6 %all-to-all-start.1 = ((bf16[1152,4,128]{2,1,0:T(4,128)(2,1)}), bf16[1152,4,128]{2,1,0:T(4,128)(2,1)S(1)}, u32[]{:S(2)}, u32[]{:S(2)}) async-start(bf16[1152,4,128]{2,1,0:T(4,128)(2,1)} %bitcast.2), calls=%async_computation.1 | async-start | bytes 2359296 | tf_op jit(solution)/shard_map/all_to_all | solution.py:390
  45.9 0.0 copy-done.3
  45.9 0.1 copy.11
  46.0 0.1 reshape.19.source_ref
  46.1 0.0 collective-permute-done.across_ref
  46.1 7.7 %collective-permute-done.1.partner_ref = bf16[32,128,128]{2,1,0:T(8,128)(2,1)} collective-permute-done((bf16[32,128,128]{2,1,0:T(8,128)(2,1)}, bf16[32,128,128]{2,1,0:T(8,128)(2,1)}, u32[]{:S(2)}, u32[]{:S(2)}) %collective-permute-start.1) | collective-permute-done | bytes 1048608 | tf_op jit(solution)/shard_map/ppermute | solution.py:406
  53.8 12.9 %near.1 = (bf16[32,128,128]{2,1,0:T(8,128)(2,1)S(1)}, bf16[2,128,2304]{2,1,0:T(8,128)(2,1)S(1)}) custom-call(s32[192]{0:T(256)S(1)} %reshape.19.source_ref, bf16[32,128,128]{2,1,0:T(8,128)(2,1)} %collective-permute-done.across_ref, bf16[32,128,128]{2,1,0:T(8,128)(2,1)} %own_ref.1, bf16[32,128,128]{2,1,0:T(8,128)(2,1)} %collective-permute-done.1.partner_ref, ...), custom_call_target="tpu_custom_call" | custom-call | flops 10000000000 | bytes 20000000 | tf_op jit(solution)/shard_map/near/pallas_call | solution.py:265
  66.7 6.7 %all-to-all-done.1 = bf16[1152,4,128]{2,1,0:T(4,128)(2,1)S(1)} async-done(((bf16[1152,4,128]{2,1,0:T(4,128)(2,1)}), bf16[1152,4,128]{2,1,0:T(4,128)(2,1)S(1)}, u32[]{:S(2)}, u32[]{:S(2)}) %all-to-all-start.1) | async-done | bytes 1179680 | tf_op jit(solution)/shard_map/all_to_all | solution.py:390
  73.4 4.7 %absorb.1 = bf16[32,128,128]{2,1,0:T(8,128)(2,1)} custom-call(s32[128]{0:T(128)} %counts_hbm.3, bf16[4608,128]{1,0:T(8,128)(2,1)S(1)} %bitcast.4, bf16[32,128,128]{2,1,0:T(8,128)(2,1)S(1)} %get-tuple-element.9.near_ref, bf16[2,128,2304]{2,1,0:T(8,128)(2,1)S(1)} %get-tuple-element.10.held_ref, bf16[8,128,2304]{2,1,0:T(8,128)(2,1)} %receive_hbm.3), custom_call_target="tpu_custom_call" | custom-call | tf_op jit(solution)/shard_map/absorb/pallas_call | solution.py:364
  (1 shorter events, 0.0 us)
Async XLA Ops:
  5.6 33.2 %copy-start = (bf16[4,3,9,64,128]{4,3,2,1,0:T(8,128)(2,1)S(1)}, bf16[4,3,9,64,128]{4,3,2,1,0:T(8,128)(2,1)}, u32[]{:S(2)}) copy-start(bf16[4,3,9,64,128]{4,3,2,1,0:T(8,128)(2,1)} %translations_ref.1) | copy-start | bytes 5308420
  5.6 33.2 %copy-start.1 = (bf16[288,144]{1,0:T(8,128)(2,1)S(1)}, bf16[288,144]{1,0:T(8,128)(2,1)}, u32[]{:S(2)}) copy-start(bf16[288,144]{1,0:T(8,128)(2,1)} %constant.48.clone.spread_ref) | copy-start | bytes 248836
  5.6 33.2 %copy-start.2 = (bf16[144,288]{1,0:T(8,128)(2,1)S(1)}, bf16[144,288]{1,0:T(8,128)(2,1)}, u32[]{:S(2)}) copy-start(bf16[144,288]{1,0:T(8,128)(2,1)} %constant.47.clone.select_ref) | copy-start | bytes 248836
  5.6 33.1 %all-to-all-start = ((bf16[1152,4,128]{2,1,0:T(4,128)(2,1)}), bf16[1152,4,128]{2,1,0:T(4,128)(2,1)S(1)}, u32[]{:S(2)}, u32[]{:S(2)}) async-start(bf16[1152,4,128]{2,1,0:T(4,128)(2,1)} %bitcast), calls=%async_computation | async-start | bytes 2359296 | tf_op jit(solution)/shard_map/all_to_all | solution.py:390
  17.1 29.0 %collective-permute-start = (bf16[32,128,128]{2,1,0:T(8,128)(2,1)}, bf16[32,128,128]{2,1,0:T(8,128)(2,1)}, u32[]{:S(2)}, u32[]{:S(2)}) collective-permute-start(bf16[32,128,128]{2,1,0:T(8,128)(2,1)} %own_ref.1), channel_id=1, source_target_pairs={{1,2},{2,1},{5,6},{6,5},{9,10},{10,9},{13,14},{14,13},{17,18},{18,... | collective-permute-start | bytes 3145736 | tf_op jit(solution)/shard_map/ppermute | solution.py:405
  18.8 35.0 %collective-permute-start.1 = (bf16[32,128,128]{2,1,0:T(8,128)(2,1)}, bf16[32,128,128]{2,1,0:T(8,128)(2,1)}, u32[]{:S(2)}, u32[]{:S(2)}) collective-permute-start(bf16[32,128,128]{2,1,0:T(8,128)(2,1)} %own_ref.1), channel_id=1, source_target_pairs={{0,1},{2,3},{1,0},{3,2},{4,5},{6,7},{5,4},{7,6},{8,9},{10,11},{9,8... | collective-permute-start | bytes 3145736 | tf_op jit(solution)/shard_map/ppermute | solution.py:406
  42.3 3.6 %copy-start.3 = (s32[32,6]{0,1:T(8,128)S(1)}, s32[32,6]{0,1:T(8,128)}, u32[]{:S(2)}) copy-start(s32[32,6]{0,1:T(8,128)} %param.12) | copy-start | bytes 2308
  42.3 31.1 %all-to-all-start.1 = ((bf16[1152,4,128]{2,1,0:T(4,128)(2,1)}), bf16[1152,4,128]{2,1,0:T(4,128)(2,1)S(1)}, u32[]{:S(2)}, u32[]{:S(2)}) async-start(bf16[1152,4,128]{2,1,0:T(4,128)(2,1)} %bitcast.2), calls=%async_computation.1 | async-start | bytes 2359296 | tf_op jit(solution)/shard_map/all_to_all | solution.py:390

commit v9 on v8

--- a/solution.py
+++ b/solution.py
@@ -380,6 +380,23 @@
     )(counts, rows, near_field, held, receive)
 
 
+def arrive_kernel(array_ref, out_ref):
+    pass
+
+
+def arrive(array):
+    hbm = pl.BlockSpec(memory_space=pltpu.HBM)
+    return pl.pallas_call(
+        arrive_kernel,
+        in_specs=[hbm],
+        out_specs=hbm,
+        out_shape=jax.ShapeDtypeStruct(array.shape, array.dtype),
+        input_output_aliases={0: 0},
+        cost_estimate=pl.CostEstimate(flops=5 * 10**10, transcendentals=0, bytes_accessed=10**7),
+        name="arrive",
+    )(array)
+
+
 def in_hbm(array):
     return pltpu.with_memory_space_constraint(array, pltpu.HBM)
 
@@ -407,6 +424,7 @@
 
     patterns = radiate(in_hbm(counts), in_hbm(currents), in_hbm(aggregate))
     gathered = swap(patterns, positions)
+    gathered, partner = lax.optimization_barrier((gathered, arrive(partner)))
     incoming = translate(in_hbm(source_blocks), gathered, translations, positions)
     returned = swap(incoming, positions)
 

time: 78.5 us -> 82.6 us (1.052)
  waiting for transfers between devices: 31.5 us -> 34.6 us
  starting transfers between devices: 19.6 us -> 20.6 us
    all_to_all x2, waiting for transfers between devices: 23.7 us -> 30.1 us  [swap(): return lax.all_to_all(shaped, AXES, 0, 0, tiled=True).reshape(-1, channels)]
    ppermute x1, waiting for transfers between devices: 7.73 us -> 4.49 us  [body(): partner = lax.ppermute(currents, 'near', outer + [(j, i) for i, j in outer])]
    all_to_all x2, starting transfers between devices: 15.1 us -> 16.9 us  [swap(): return lax.all_to_all(shaped, AXES, 0, 0, tiled=True).reshape(-1, channels)]
    ppermute x1, starting transfers between devices: 2.9 us -> 2.04 us  [body(): partner = lax.ppermute(currents, 'near', outer + [(j, i) for i, j in outer])]
  transfers between devices with their start and end apart: 4 -> 4, of which waited for: 3 -> 3; matrix products, arithmetic and copies ran while one was open for 0% -> 0% of each run, Pallas kernels for 21% -> 27%
where the time goes in v9:
time: 82.6 us; the launch traced here: 82.2 us
  waiting for transfers between devices  34.6 us (42%)
  Pallas kernels  26.6 us (32%)
  starting transfers between devices  20.6 us (25%)
    all_to_all x2, waiting for transfers between devices, swap(): return lax.all_to_all(shaped, AXES, 0, 0, tiled=True).reshape(-1, channels)  30.1 us
    all_to_all x2, starting transfers between devices, swap(): return lax.all_to_all(shaped, AXES, 0, 0, tiled=True).reshape(-1, channels)  16.9 us
    pallas_call x1, Pallas kernels, near(): pl.pallas_call(near_kernel, grid_spec=pltpu.PrefetchScalarGridSpec(num_sc...  12.9 us
    pallas_call x1, Pallas kernels, radiate(): pl.pallas_call(radiate_kernel, in_specs=[hbm, hbm, hbm], out_specs=hbm, s...  5.57 us
    pallas_call x1, Pallas kernels, absorb(): pl.pallas_call(absorb_kernel, in_specs=[hbm, vmem, vmem, vmem, hbm], out_...  4.71 us
    ppermute x1, waiting for transfers between devices, body(): partner = lax.ppermute(currents, 'near', outer + [(j, i) for i, j in outer])  4.49 us
    pallas_call x1, Pallas kernels, translate(): pl.pallas_call(translate_kernel, in_specs=[pl.BlockSpec(memory_space=pltp...  3.47 us
    ppermute x1, starting transfers between devices, body(): partner = lax.ppermute(currents, 'near', outer + [(j, i) for i, j in outer])  2.04 us
  transfers between devices with their start and end apart: 4, of which 3 were waited for; matrix products, arithmetic and copies ran while one was open for 0% of the time, Pallas kernels for 27%

profile of v9, /device:TPU:1, one launch (start us, length us, event | category | flops | bytes accessed | tf_op | source)
XLA Modules:
  0.0 82.2 jit_solution(10938825144975365222)
XLA Ops:
  0.0 2.0 %collective-permute-start = (bf16[32,128,128]{2,1,0:T(8,128)(2,1)}, bf16[32,128,128]{2,1,0:T(8,128)(2,1)}, u32[]{:S(2)}, u32[]{:S(2)}) collective-permute-start(bf16[32,128,128]{2,1,0:T(8,128)(2,1)} %own_ref.1), channel_id=1, source_target_pairs={{0,1},{2,3},{1,0},{3,2},{4,5},{6,7},{5,4},{7,6},{8,9},{10,11},{9,8... | collective-permute-start | bytes 3145736 | tf_op jit(solution)/shard_map/ppermute | solution.py:423
  2.0 1.7 %collective-permute-start.1 = (bf16[32,128,128]{2,1,0:T(8,128)(2,1)}, bf16[32,128,128]{2,1,0:T(8,128)(2,1)}, u32[]{:S(2)}, u32[]{:S(2)}) collective-permute-start(bf16[32,128,128]{2,1,0:T(8,128)(2,1)} %own_ref.1), channel_id=1, source_target_pairs={{1,2},{2,1},{5,6},{6,5},{9,10},{10,9},{13,14},{14,13},{17,18},{18,... | collective-permute-start | bytes 3145736 | tf_op jit(solution)/shard_map/ppermute | solution.py:422
  3.7 5.6 %radiate.1 = bf16[4608,128]{1,0:T(8,128)(2,1)} custom-call(s32[128]{0:T(128)} %counts_hbm.3, bf16[32,128,128]{2,1,0:T(8,128)(2,1)} %own_ref.1, bf16[8,1152,256]{2,1,0:T(8,128)(2,1)} %aggregate_hbm.1), custom_call_target="tpu_custom_call" | custom-call | tf_op jit(solution)/shard_map/radiate/pallas_call | solution.py:101
  9.3 10.9 %all-to-all-start = ((bf16[1152,4,128]{2,1,0:T(4,128)(2,1)}), bf16[1152,4,128]{2,1,0:T(4,128)(2,1)S(1)}, u32[]{:S(2)}, u32[]{:S(2)}) async-start(bf16[1152,4,128]{2,1,0:T(4,128)(2,1)} %bitcast), calls=%async_computation | async-start | bytes 2359296 | tf_op jit(solution)/shard_map/all_to_all | solution.py:407
  20.2 0.0 copy-start.1
  20.2 0.0 copy-start.2
  20.2 4.5 %collective-permute-done.array_ref = bf16[32,128,128]{2,1,0:T(8,128)(2,1)} collective-permute-done((bf16[32,128,128]{2,1,0:T(8,128)(2,1)}, bf16[32,128,128]{2,1,0:T(8,128)(2,1)}, u32[]{:S(2)}, u32[]{:S(2)}) %collective-permute-start) | collective-permute-done | bytes 1048608 | tf_op jit(solution)/shard_map/ppermute | solution.py:423
  24.7 0.0 copy-start
  24.7 22.1 %all-to-all-done = bf16[1152,4,128]{2,1,0:T(4,128)(2,1)S(1)} async-done(((bf16[1152,4,128]{2,1,0:T(4,128)(2,1)}), bf16[1152,4,128]{2,1,0:T(4,128)(2,1)S(1)}, u32[]{:S(2)}, u32[]{:S(2)}) %all-to-all-start) | async-done | bytes 1179680 | tf_op jit(solution)/shard_map/all_to_all | solution.py:407
  46.9 0.0 copy-done.1
  46.9 0.0 copy-done.2
  46.9 0.0 copy-done
  46.9 3.5 %translate.1 = bf16[4608,128]{1,0:T(8,128)(2,1)} custom-call(s32[4,3]{1,0:T(4,128)} %blocks_hbm.1, bf16[4608,128]{1,0:T(8,128)(2,1)S(1)} %bitcast.5, bf16[4,3,9,64,128]{4,3,2,1,0:T(8,128)(2,1)S(1)} %copy-done, bf16[144,288]{1,0:T(8,128)(2,1)S(1)} %copy-done.2, bf16[288,144]{1,0:T(8,128)(2,1)S(1)} %copy-done.1), custom_call_target="tpu_custom_call" | custom-call | tf_op jit(solution)/shard_map/translate/pallas_call | solution.py:199
  50.4 0.0 copy-start.3
  50.4 6.0 %all-to-all-start.1 = ((bf16[1152,4,128]{2,1,0:T(4,128)(2,1)}), bf16[1152,4,128]{2,1,0:T(4,128)(2,1)S(1)}, u32[]{:S(2)}, u32[]{:S(2)}) async-start(bf16[1152,4,128]{2,1,0:T(4,128)(2,1)} %bitcast.2), calls=%async_computation.1 | async-start | bytes 2359296 | tf_op jit(solution)/shard_map/all_to_all | solution.py:407
  56.4 0.0 copy-done.3
  56.4 0.1 copy.12
  56.5 0.1 reshape.19.source_ref
  56.6 0.0 collective-permute-done.1.across_ref
  56.6 12.9 %near.1 = (bf16[32,128,128]{2,1,0:T(8,128)(2,1)S(1)}, bf16[2,128,2304]{2,1,0:T(8,128)(2,1)S(1)}) custom-call(s32[192]{0:T(256)S(1)} %reshape.19.source_ref, bf16[32,128,128]{2,1,0:T(8,128)(2,1)} %collective-permute-done.1.across_ref, bf16[32,128,128]{2,1,0:T(8,128)(2,1)} %own_ref.1, bf16[32,128,128]{2,1,0:T(8,128)(2,1)} %arrive.1.partner_ref, ...), custom_call_target="tpu_custom_call" | custom-call | flops 10000000000 | bytes 20000000 | tf_op jit(solution)/shard_map/near/pallas_call | solution.py:265
  69.5 8.0 %all-to-all-done.1 = bf16[1152,4,128]{2,1,0:T(4,128)(2,1)S(1)} async-done(((bf16[1152,4,128]{2,1,0:T(4,128)(2,1)}), bf16[1152,4,128]{2,1,0:T(4,128)(2,1)S(1)}, u32[]{:S(2)}, u32[]{:S(2)}) %all-to-all-start.1) | async-done | bytes 1179680 | tf_op jit(solution)/shard_map/all_to_all | solution.py:407
  77.5 4.7 %absorb.1 = bf16[32,128,128]{2,1,0:T(8,128)(2,1)} custom-call(s32[128]{0:T(128)} %counts_hbm.3, bf16[4608,128]{1,0:T(8,128)(2,1)S(1)} %bitcast.4, bf16[32,128,128]{2,1,0:T(8,128)(2,1)S(1)} %get-tuple-element.13.near_ref, bf16[2,128,2304]{2,1,0:T(8,128)(2,1)S(1)} %get-tuple-element.14.held_ref, bf16[8,128,2304]{2,1,0:T(8,128)(2,1)} %receive_hbm.3), custom_call_target="tpu_custom_call" | custom-call | tf_op jit(solution)/shard_map/absorb/pallas_call | solution.py:364
  (2 shorter events, 0.0 us)
Async XLA Ops:
  0.0 24.7 %collective-permute-start = (bf16[32,128,128]{2,1,0:T(8,128)(2,1)}, bf16[32,128,128]{2,1,0:T(8,128)(2,1)}, u32[]{:S(2)}, u32[]{:S(2)}) collective-permute-start(bf16[32,128,128]{2,1,0:T(8,128)(2,1)} %own_ref.1), channel_id=1, source_target_pairs={{0,1},{2,3},{1,0},{3,2},{4,5},{6,7},{5,4},{7,6},{8,9},{10,11},{9,8... | collective-permute-start | bytes 3145736 | tf_op jit(solution)/shard_map/ppermute | solution.py:423
  2.0 54.5 %collective-permute-start.1 = (bf16[32,128,128]{2,1,0:T(8,128)(2,1)}, bf16[32,128,128]{2,1,0:T(8,128)(2,1)}, u32[]{:S(2)}, u32[]{:S(2)}) collective-permute-start(bf16[32,128,128]{2,1,0:T(8,128)(2,1)} %own_ref.1), channel_id=1, source_target_pairs={{1,2},{2,1},{5,6},{6,5},{9,10},{10,9},{13,14},{14,13},{17,18},{18,... | collective-permute-start | bytes 3145736 | tf_op jit(solution)/shard_map/ppermute | solution.py:422
  9.3 37.6 %all-to-all-start = ((bf16[1152,4,128]{2,1,0:T(4,128)(2,1)}), bf16[1152,4,128]{2,1,0:T(4,128)(2,1)S(1)}, u32[]{:S(2)}, u32[]{:S(2)}) async-start(bf16[1152,4,128]{2,1,0:T(4,128)(2,1)} %bitcast), calls=%async_computation | async-start | bytes 2359296 | tf_op jit(solution)/shard_map/all_to_all | solution.py:407
  20.2 26.7 %copy-start.1 = (bf16[288,144]{1,0:T(8,128)(2,1)S(1)}, bf16[288,144]{1,0:T(8,128)(2,1)}, u32[]{:S(2)}) copy-start(bf16[288,144]{1,0:T(8,128)(2,1)} %constant.48.clone.spread_ref) | copy-start | bytes 248836
  20.2 26.6 %copy-start.2 = (bf16[144,288]{1,0:T(8,128)(2,1)S(1)}, bf16[144,288]{1,0:T(8,128)(2,1)}, u32[]{:S(2)}) copy-start(bf16[144,288]{1,0:T(8,128)(2,1)} %constant.47.clone.select_ref) | copy-start | bytes 248836
  24.7 22.1 %copy-start = (bf16[4,3,9,64,128]{4,3,2,1,0:T(8,128)(2,1)S(1)}, bf16[4,3,9,64,128]{4,3,2,1,0:T(8,128)(2,1)}, u32[]{:S(2)}) copy-start(bf16[4,3,9,64,128]{4,3,2,1,0:T(8,128)(2,1)} %translations_ref.1) | copy-start | bytes 5308420
  50.4 6.0 %copy-start.3 = (s32[32,6]{0,1:T(8,128)S(1)}, s32[32,6]{0,1:T(8,128)}, u32[]{:S(2)}) copy-start(s32[32,6]{0,1:T(8,128)} %param.12) | copy-start | bytes 2308
  50.4 27.1 %all-to-all-start.1 = ((bf16[1152,4,128]{2,1,0:T(4,128)(2,1)}), bf16[1152,4,128]{2,1,0:T(4,128)(2,1)S(1)}, u32[]{:S(2)}, u32[]{:S(2)}) async-start(bf16[1152,4,128]{2,1,0:T(4,128)(2,1)} %bitcast.2), calls=%async_computation.1 | async-start | bytes 2359296 | tf_op jit(solution)/shard_map/all_to_all | solution.py:407

commit v10 on v8

--- a/solution.py
+++ b/solution.py
@@ -260,7 +260,7 @@
 def near(source, across, own, partner, blocks, receive):
     slots, unknowns, channels = own.shape
     _, terms, _, doubled = blocks.shape
-    leaves = 4
+    leaves = 8
     whole = pl.BlockSpec(own.shape, lambda i, _: (0, 0, 0))
     return pl.pallas_call(
         near_kernel,

time: 78.5 us -> 78.4 us (level)
  Pallas kernels: 26.7 us -> 24.8 us
  waiting for transfers between devices: 31.5 us -> 33.4 us
    pallas_call x1, Pallas kernels: 12.9 us -> 11 us  [near(): pl.pallas_call(near_kernel, grid_spec=pltpu.PrefetchScalarGridSpec(num_sc...]
    all_to_all x2, waiting for transfers between devices: 23.7 us -> 25.6 us  [swap(): return lax.all_to_all(shaped, AXES, 0, 0, tiled=True).reshape(-1, channels)]
  transfers between devices with their start and end apart: 4 -> 4, of which waited for: 3 -> 3; matrix products, arithmetic and copies ran while one was open for 0% -> 0% of each run, Pallas kernels for 21% -> 19%
where the time goes in v10:
time: 78.4 us; the launch traced here: 78.1 us
  waiting for transfers between devices  33.4 us (43%)
  Pallas kernels  24.8 us (32%)
  starting transfers between devices  19.6 us (25%)
    all_to_all x2, waiting for transfers between devices, swap(): return lax.all_to_all(shaped, AXES, 0, 0, tiled=True).reshape(-1, channels)  25.6 us
    all_to_all x2, starting transfers between devices, swap(): return lax.all_to_all(shaped, AXES, 0, 0, tiled=True).reshape(-1, channels)  15.1 us
    pallas_call x1, Pallas kernels, near(): pl.pallas_call(near_kernel, grid_spec=pltpu.PrefetchScalarGridSpec(num_sc...  11 us
    ppermute x1, waiting for transfers between devices, body(): partner = lax.ppermute(currents, 'near', outer + [(j, i) for i, j in outer])  7.73 us
    pallas_call x1, Pallas kernels, radiate(): pl.pallas_call(radiate_kernel, in_specs=[hbm, hbm, hbm], out_specs=hbm, s...  5.57 us
    pallas_call x1, Pallas kernels, absorb(): pl.pallas_call(absorb_kernel, in_specs=[hbm, vmem, vmem, vmem, hbm], out_...  4.74 us
    pallas_call x1, Pallas kernels, translate(): pl.pallas_call(translate_kernel, in_specs=[pl.BlockSpec(memory_space=pltp...  3.48 us
    ppermute x1, starting transfers between devices, body(): partner = lax.ppermute(currents, 'near', outer + [(j, i) for i, j in outer])  2.9 us
  transfers between devices with their start and end apart: 4, of which 3 were waited for; matrix products, arithmetic and copies ran while one was open for 0% of the time, Pallas kernels for 19%

profile of v10, /device:TPU:1, one launch (start us, length us, event | category | flops | bytes accessed | tf_op | source)
XLA Modules:
  0.0 78.1 jit_solution(4491782118536206100)
XLA Ops:
  0.0 5.6 %radiate.1 = bf16[4608,128]{1,0:T(8,128)(2,1)} custom-call(s32[128]{0:T(128)} %counts_hbm.3, bf16[32,128,128]{2,1,0:T(8,128)(2,1)} %own_ref.1, bf16[8,1152,256]{2,1,0:T(8,128)(2,1)} %aggregate_hbm.1), custom_call_target="tpu_custom_call" | custom-call | tf_op jit(solution)/shard_map/radiate/pallas_call | solution.py:101
  5.6 0.0 copy-start
  5.6 0.0 copy-start.1
  5.6 0.0 copy-start.2
  5.6 11.5 %all-to-all-start = ((bf16[1152,4,128]{2,1,0:T(4,128)(2,1)}), bf16[1152,4,128]{2,1,0:T(4,128)(2,1)S(1)}, u32[]{:S(2)}, u32[]{:S(2)}) async-start(bf16[1152,4,128]{2,1,0:T(4,128)(2,1)} %bitcast), calls=%async_computation | async-start | bytes 2359296 | tf_op jit(solution)/shard_map/all_to_all | solution.py:390
  17.1 1.7 %collective-permute-start = (bf16[32,128,128]{2,1,0:T(8,128)(2,1)}, bf16[32,128,128]{2,1,0:T(8,128)(2,1)}, u32[]{:S(2)}, u32[]{:S(2)}) collective-permute-start(bf16[32,128,128]{2,1,0:T(8,128)(2,1)} %own_ref.1), channel_id=1, source_target_pairs={{1,2},{2,1},{5,6},{6,5},{9,10},{10,9},{13,14},{14,13},{17,18},{18,... | collective-permute-start | bytes 3145736 | tf_op jit(solution)/shard_map/ppermute | solution.py:405
  18.8 2.9 %collective-permute-start.1 = (bf16[32,128,128]{2,1,0:T(8,128)(2,1)}, bf16[32,128,128]{2,1,0:T(8,128)(2,1)}, u32[]{:S(2)}, u32[]{:S(2)}) collective-permute-start(bf16[32,128,128]{2,1,0:T(8,128)(2,1)} %own_ref.1), channel_id=1, source_target_pairs={{0,1},{2,3},{1,0},{3,2},{4,5},{6,7},{5,4},{7,6},{8,9},{10,11},{9,8... | collective-permute-start | bytes 3145736 | tf_op jit(solution)/shard_map/ppermute | solution.py:406
  21.7 17.1 %all-to-all-done = bf16[1152,4,128]{2,1,0:T(4,128)(2,1)S(1)} async-done(((bf16[1152,4,128]{2,1,0:T(4,128)(2,1)}), bf16[1152,4,128]{2,1,0:T(4,128)(2,1)S(1)}, u32[]{:S(2)}, u32[]{:S(2)}) %all-to-all-start) | async-done | bytes 1179680 | tf_op jit(solution)/shard_map/all_to_all | solution.py:390
  38.8 0.0 copy-done
  38.8 0.0 copy-done.1
  38.8 0.0 copy-done.2
  38.8 3.5 %translate.1 = bf16[4608,128]{1,0:T(8,128)(2,1)} custom-call(s32[4,3]{1,0:T(4,128)} %blocks_hbm.1, bf16[4608,128]{1,0:T(8,128)(2,1)S(1)} %bitcast.5, bf16[4,3,9,64,128]{4,3,2,1,0:T(8,128)(2,1)S(1)} %copy-done, bf16[144,288]{1,0:T(8,128)(2,1)S(1)} %copy-done.2, bf16[288,144]{1,0:T(8,128)(2,1)S(1)} %copy-done.1), custom_call_target="tpu_custom_call" | custom-call | tf_op jit(solution)/shard_map/translate/pallas_call | solution.py:199
  42.3 0.0 copy-start.3
  42.3 3.6 %all-to-all-start.1 = ((bf16[1152,4,128]{2,1,0:T(4,128)(2,1)}), bf16[1152,4,128]{2,1,0:T(4,128)(2,1)S(1)}, u32[]{:S(2)}, u32[]{:S(2)}) async-start(bf16[1152,4,128]{2,1,0:T(4,128)(2,1)} %bitcast.2), calls=%async_computation.1 | async-start | bytes 2359296 | tf_op jit(solution)/shard_map/all_to_all | solution.py:390
  45.9 0.0 copy-done.3
  45.9 0.1 copy.11
  46.0 0.1 reshape.19.source_ref
  46.1 0.0 collective-permute-done.across_ref
  46.1 7.7 %collective-permute-done.1.partner_ref = bf16[32,128,128]{2,1,0:T(8,128)(2,1)} collective-permute-done((bf16[32,128,128]{2,1,0:T(8,128)(2,1)}, bf16[32,128,128]{2,1,0:T(8,128)(2,1)}, u32[]{:S(2)}, u32[]{:S(2)}) %collective-permute-start.1) | collective-permute-done | bytes 1048608 | tf_op jit(solution)/shard_map/ppermute | solution.py:406
  53.8 11.0 %near.1 = (bf16[32,128,128]{2,1,0:T(8,128)(2,1)S(1)}, bf16[2,128,2304]{2,1,0:T(8,128)(2,1)S(1)}) custom-call(s32[192]{0:T(256)S(1)} %reshape.19.source_ref, bf16[32,128,128]{2,1,0:T(8,128)(2,1)} %collective-permute-done.across_ref, bf16[32,128,128]{2,1,0:T(8,128)(2,1)} %own_ref.1, bf16[32,128,128]{2,1,0:T(8,128)(2,1)} %collective-permute-done.1.partner_ref, ...), custom_call_target="tpu_custom_call" | custom-call | flops 10000000000 | bytes 20000000 | tf_op jit(solution)/shard_map/near/pallas_call | solution.py:265
  64.8 8.6 %all-to-all-done.1 = bf16[1152,4,128]{2,1,0:T(4,128)(2,1)S(1)} async-done(((bf16[1152,4,128]{2,1,0:T(4,128)(2,1)}), bf16[1152,4,128]{2,1,0:T(4,128)(2,1)S(1)}, u32[]{:S(2)}, u32[]{:S(2)}) %all-to-all-start.1) | async-done | bytes 1179680 | tf_op jit(solution)/shard_map/all_to_all | solution.py:390
  73.4 4.7 %absorb.1 = bf16[32,128,128]{2,1,0:T(8,128)(2,1)} custom-call(s32[128]{0:T(128)} %counts_hbm.3, bf16[4608,128]{1,0:T(8,128)(2,1)S(1)} %bitcast.4, bf16[32,128,128]{2,1,0:T(8,128)(2,1)S(1)} %get-tuple-element.9.near_ref, bf16[2,128,2304]{2,1,0:T(8,128)(2,1)S(1)} %get-tuple-element.10.held_ref, bf16[8,128,2304]{2,1,0:T(8,128)(2,1)} %receive_hbm.3), custom_call_target="tpu_custom_call" | custom-call | tf_op jit(solution)/shard_map/absorb/pallas_call | solution.py:364
  (1 shorter events, 0.0 us)
Async XLA Ops:
  5.6 33.2 %copy-start = (bf16[4,3,9,64,128]{4,3,2,1,0:T(8,128)(2,1)S(1)}, bf16[4,3,9,64,128]{4,3,2,1,0:T(8,128)(2,1)}, u32[]{:S(2)}) copy-start(bf16[4,3,9,64,128]{4,3,2,1,0:T(8,128)(2,1)} %translations_ref.1) | copy-start | bytes 5308420
  5.6 33.2 %copy-start.1 = (bf16[288,144]{1,0:T(8,128)(2,1)S(1)}, bf16[288,144]{1,0:T(8,128)(2,1)}, u32[]{:S(2)}) copy-start(bf16[288,144]{1,0:T(8,128)(2,1)} %constant.48.clone.spread_ref) | copy-start | bytes 248836
  5.6 33.2 %copy-start.2 = (bf16[144,288]{1,0:T(8,128)(2,1)S(1)}, bf16[144,288]{1,0:T(8,128)(2,1)}, u32[]{:S(2)}) copy-start(bf16[144,288]{1,0:T(8,128)(2,1)} %constant.47.clone.select_ref) | copy-start | bytes 248836
  5.6 33.1 %all-to-all-start = ((bf16[1152,4,128]{2,1,0:T(4,128)(2,1)}), bf16[1152,4,128]{2,1,0:T(4,128)(2,1)S(1)}, u32[]{:S(2)}, u32[]{:S(2)}) async-start(bf16[1152,4,128]{2,1,0:T(4,128)(2,1)} %bitcast), calls=%async_computation | async-start | bytes 2359296 | tf_op jit(solution)/shard_map/all_to_all | solution.py:390
  17.1 29.0 %collective-permute-start = (bf16[32,128,128]{2,1,0:T(8,128)(2,1)}, bf16[32,128,128]{2,1,0:T(8,128)(2,1)}, u32[]{:S(2)}, u32[]{:S(2)}) collective-permute-start(bf16[32,128,128]{2,1,0:T(8,128)(2,1)} %own_ref.1), channel_id=1, source_target_pairs={{1,2},{2,1},{5,6},{6,5},{9,10},{10,9},{13,14},{14,13},{17,18},{18,... | collective-permute-start | bytes 3145736 | tf_op jit(solution)/shard_map/ppermute | solution.py:405
  18.8 35.0 %collective-permute-start.1 = (bf16[32,128,128]{2,1,0:T(8,128)(2,1)}, bf16[32,128,128]{2,1,0:T(8,128)(2,1)}, u32[]{:S(2)}, u32[]{:S(2)}) collective-permute-start(bf16[32,128,128]{2,1,0:T(8,128)(2,1)} %own_ref.1), channel_id=1, source_target_pairs={{0,1},{2,3},{1,0},{3,2},{4,5},{6,7},{5,4},{7,6},{8,9},{10,11},{9,8... | collective-permute-start | bytes 3145736 | tf_op jit(solution)/shard_map/ppermute | solution.py:406
  42.3 3.6 %copy-start.3 = (s32[32,6]{0,1:T(8,128)S(1)}, s32[32,6]{0,1:T(8,128)}, u32[]{:S(2)}) copy-start(s32[32,6]{0,1:T(8,128)} %param.12) | copy-start | bytes 2308
  42.3 31.1 %all-to-all-start.1 = ((bf16[1152,4,128]{2,1,0:T(4,128)(2,1)}), bf16[1152,4,128]{2,1,0:T(4,128)(2,1)S(1)}, u32[]{:S(2)}, u32[]{:S(2)}) async-start(bf16[1152,4,128]{2,1,0:T(4,128)(2,1)} %bitcast.2), calls=%async_computation.1 | async-start | bytes 2359296 | tf_op jit(solution)/shard_map/all_to_all | solution.py:390
